TPU v7x, 32 devices: a whole 2x2x4 slice. The times are simulated.
32 devices in a mesh: tx: 8 (over z, y), ty: 4 (over x, core).
Axes of the slice: x: 2, y: 2, z: 4, core: 2. Of those that a mesh axis runs over, the one named last changes fastest.
Arguments:
- concentration: float32 [64, 64, 256], P('tx', 'ty'), may hold values from -6 to 6
- source: float32 [64, 64, 256], P('tx', 'ty'), may hold values from -4 to 4
- material: int32 [64, 64, 256], P('tx', 'ty'), may hold values from 0 to 7
Outputs:
- updated: float32 [64, 64, 256], P('tx', 'ty')
All inputs are finite; a program needn't handle non-finite values.
Results may differ from a plain program's by a relative error of at most 0.00017.
Values sent between devices are 32-bit elements; how exact they have to be, the bound alone decides.
No kernel may reach another device: no remote copies, remote signals or barrier semaphores. Data moves between devices by JAX's collectives and lax.ppermute only.
A program may use at most 128 MiB of HBM per device.

v0:
```python
import functools

import jax
import jax.numpy as jnp
from jax import lax
from jax.experimental import pallas as pl
from jax.experimental.pallas import tpu as pltpu
from jax.sharding import PartitionSpec as P


mass_rate = 0.001
relax_weight = 0.8
diffusivities = (0.15, 0.3, 0.5, 0.8, 1.2, 2.0, 3.2, 5.0)
LANES = 128
ROWS = 8
RX = 3
RY = 4
R1 = 4
RC = 2
F32 = jnp.float32
BF16 = jnp.bfloat16


def lookup(material):
    result = jnp.zeros(material.shape, F32)
    for slot_id, coeff_value in enumerate(diffusivities):
        result = jnp.where(material == slot_id, F32(coeff_value), result)
    return result


class Planes:
    def __init__(self, first, planes):
        self.first = first
        self.planes = planes

    def __getitem__(self, x):
        ref, index = self.planes[x - self.first]
        return ref[index]


def iota(shape, dim):
    return lax.broadcasted_iota(jnp.int32, shape, dim)


def div(a, b):
    return lax.div(a, jnp.full_like(a, b))


def mod(a, b):
    return lax.rem(a, jnp.full_like(a, b))


def ones_where(mask):
    return jnp.where(mask, F32(1.0), F32(0.0)).astype(BF16)


def three_terms(x):
    high = x.astype(BF16)
    rest = x - high.astype(F32)
    middle = rest.astype(BF16)
    low = (rest - middle.astype(F32)).astype(BF16)
    return high, middle, low


def times_right(x, selector):
    parts = [jnp.dot(part, selector, preferred_element_type=F32) for part in three_terms(x)]
    return parts[0] + (parts[1] + parts[2])


def times_left(selector, x):
    parts = [jnp.dot(selector, part, preferred_element_type=F32) for part in three_terms(x)]
    return parts[0] + (parts[1] + parts[2])


def back(v, axis, step=1):
    return pltpu.roll(v, step, axis)


def ahead(v, axis, step=1):
    return pltpu.roll(v, v.shape[axis] - step, axis)


def halve_lanes(fine, coarse, start=0):
    shape = (fine, coarse)
    return ones_where(div(iota(shape, 0), 2) + start == iota(shape, 1))


def plane_setup(kappa, cx, cy, cz, weight, diag, scale, first, last):
    half = 0.5 * scale
    for x in range(first - 1, last):
        cx[x] = half * (kappa[x] + kappa[x + 1])
    for x in range(first, last):
        k = kappa[x]
        y_part = half * (k + ahead(k, 0))
        z_part = half * (k + ahead(k, 1))
        cy[x] = y_part
        cz[x] = z_part
        d = mass_rate + cx[x] + cx[x - 1] + y_part + back(y_part, 0) + z_part + back(z_part, 1)
        weight[x] = relax_weight / d
        if diag is not None:
            diag[x] = d


def in_plane(here, cy, cz, x):
    y_part = cy[x]
    z_part = cz[x]
    total = y_part * ahead(here, 0) + back(y_part * here, 0)
    return total + (z_part * ahead(here, 1) + back(z_part * here, 1))


def neighbours(v, cx, cy, cz, x):
    return (cx[x] * v[x + 1] + cx[x - 1] * v[x - 1]) + in_plane(v[x], cy, cz, x)


def plane_sweep(v, out, forcing, cx, cy, cz, weight, first, last):
    for x in range(first, last):
        out[x] = (1.0 - relax_weight) * v[x] + weight[x] * (forcing[x] + neighbours(v, cx, cy, cz, x))


def edges(conc_in, source_in, material_in, conc, source, material, to_low, to_high, arrived):
    copies = [
        pltpu.make_async_copy(whence, whither, arrived.at[n])
        for n, (whence, whither) in enumerate(
            ((conc_in, conc), (source_in, source), (material_in, material))
        )
    ]
    for copy in copies:
        copy.start()
    for copy in copies:
        copy.wait()
    tile_x, tile_y, _ = conc.shape
    for to, low in ((to_low, True), (to_high, False)):
        for x in range(tile_x):
            rows = slice(0, 4) if low else slice(tile_y - 4, tile_y)
            near = slice(0, 3) if low else slice(1, 4)
            pair = slice(0, 2) if low else slice(2, 4)
            c = conc[x, rows]
            f = mass_rate * c + source[x, rows]
            k = lookup(material[x, rows])
            to[x, 0:3] = c[near]
            to[x, 3:5] = f[pair]
            to[x, 5:8] = k[near]
            to[tile_x, x : x + 1] = k[3:4] if low else k[0:1]


def sides(conc, source, material, from_low, from_high, window, to_low, to_high):
    tile_x, tile_y, size_z = conc.shape
    top = RY + tile_y
    for x in range(tile_x):
        c = conc[x]
        window[0, x, RY:top] = c
        window[1, x, RY:top] = mass_rate * c + source[x]
        window[2, x, RY:top] = lookup(material[x])
        window[0, x, 0:1] = jnp.zeros((1, size_z), F32)
        window[0, x, 1:4] = from_low[x, 0:3]
        window[0, x, top : top + 3] = from_high[x, 0:3]
        window[0, x, top + 3 :] = jnp.zeros((1, size_z), F32)
        window[1, x, 0:2] = jnp.zeros((2, size_z), F32)
        window[1, x, 2:4] = from_low[x, 3:5]
        window[1, x, top : top + 2] = from_high[x, 3:5]
        window[1, x, top + 2 :] = jnp.zeros((2, size_z), F32)
        window[2, x, 0:1] = from_low[tile_x, x : x + 1]
        window[2, x, 1:4] = from_low[x, 5:8]
        window[2, x, top : top + 3] = from_high[x, 5:8]
        window[2, x, top + 3 :] = from_high[tile_x, x : x + 1]
    for to, plane in ((to_low, lambda l: l - 1), (to_high, lambda l: tile_x - l)):
        for at, (which, layer) in enumerate(BASE_PLANES):
            to[at] = window[which, plane(layer), RY:top]
        at = 0
        for which, layer, reach in EXTRA_ROWS:
            to[len(BASE_PLANES), at : at + reach] = window[which, plane(layer), RY - reach : RY]
            at += reach
            to[len(BASE_PLANES), at : at + reach] = window[which, plane(layer), top : top + reach]
            at += reach


BASE_PLANES = (
    (0, 1), (0, 2), (0, 3), (1, 1), (1, 2), (2, 1), (2, 2), (2, 3), (2, 4),
)
EXTRA_ROWS = ((0, 1, 2), (0, 2, 1), (1, 1, 1), (2, 1, 2), (2, 2, 2))


def shrink(window, blocks, paired, paired_one):
    _, tile_x, rows, size_z = window.shape
    tile_x1, tile_y1, size_z1 = tile_x // 2, (rows - 2 * RY) // 2, size_z // 2
    k_one = None
    for chunk in range(size_z // LANES):
        lanes = slice(chunk * LANES, (chunk + 1) * LANES)
        for pair in range(tile_x1):
            paired[pair] = window[2, 2 * pair, :, lanes] + window[2, 2 * pair + 1, :, lanes]
        stack = [
            paired[pair, pl.ds(RY, tile_y1, stride=2)] + paired[pair, pl.ds(RY + 1, tile_y1, stride=2)]
            for pair in range(tile_x1)
        ]
        part = times_right(
            jnp.concatenate(stack, 0), halve_lanes(LANES, size_z1, chunk * LANES // 2)
        )
        k_one = part if k_one is None else k_one + part
    pieces = []
    for pair in range(tile_x1 // 2):
        at = 2 * pair * tile_y1
        paired_one[...] = k_one[at : at + tile_y1] + k_one[at + tile_y1 : at + 2 * tile_y1]
        pieces.append(
            paired_one[pl.ds(0, tile_y1 // 2, stride=2)] + paired_one[pl.ds(1, tile_y1 // 2, stride=2)]
        )
    shape = (size_z1, LANES)
    twice = ones_where(div(iota(shape, 0), 2) == mod(iota(shape, 1), size_z1 // 2))
    block = (0.125 * 0.125) * times_right(jnp.concatenate(pieces, 0), twice)
    for device in range(blocks.shape[0]):
        blocks[device] = block


def fine_down(
    window, from_low, from_high,
    v_out, forcing_out, cx, cy, cz, weight, level_one, blocks, to_low, to_high,
    conc_rim, forcing_rim, kappa_rim, once, diag, paired,
    k_one, f_one, u_one, v_one, cx1, cy1, cz1, w1, d1, paired_one, packed,
):
    _, tile_x, rows, size_z = window.shape
    tile_y = rows - 2 * RY
    top = RY + tile_y
    planes = tile_x + 2 * RX
    rims = (conc_rim, forcing_rim, kappa_rim)
    depths = (3, 2, 4)
    for which, rim in enumerate(rims):
        fill = jnp.full((rows, size_z), 1.0 if which == 2 else 0.0, F32)
        for x in range(2 * depths[which]):
            rim[x] = fill

    def place(which, layer, low):
        return depths[which] - layer if low else depths[which] + layer - 1

    for message, low in ((from_low, True), (from_high, False)):
        for at, (which, layer) in enumerate(BASE_PLANES):
            rims[which][place(which, layer, low), RY:top] = message[at]
        at = 0
        for which, layer, reach in EXTRA_ROWS:
            rim, x = rims[which], place(which, layer, low)
            rim[x, RY - reach : RY] = message[len(BASE_PLANES), at : at + reach]
            at += reach
            rim[x, top : top + reach] = message[len(BASE_PLANES), at : at + reach]
            at += reach

    def stacked(which):
        depth = depths[which]
        whole = [(rims[which], x) for x in range(depth)]
        whole += [(window.at[which], x) for x in range(tile_x)]
        whole += [(rims[which], depth + x) for x in range(depth)]
        return Planes(RX - depth, whole)

    conc, forcing, kappa = stacked(0), stacked(1), stacked(2)
    plane_setup(kappa, cx, cy, cz, weight, diag, 1.0, 1, planes - 1)
    plane_sweep(conc, once, forcing, cx, cy, cz, weight, 1, planes - 1)
    plane_sweep(once, v_out, forcing, cx, cy, cz, weight, 2, planes - 2)
    for x in range(RX - 1, planes - RX + 1):
        forcing_out[x] = forcing[x]
    chunks = size_z // LANES
    size_z1 = size_z // 2
    to_half = [halve_lanes(LANES, size_z1, chunk * LANES // 2) for chunk in range(chunks)]
    tile_x1, tile_y1 = tile_x // 2, tile_y // 2

    def put(pair, total):
        for chunk in range(chunks):
            paired[chunk, pair, 0:rows] = total[:, chunk * LANES : (chunk + 1) * LANES]

    def narrowed(pairs, start, count):
        result = None
        for chunk in range(chunks):
            stack = [
                paired[chunk, pair, pl.ds(start, count, stride=2)]
                + paired[chunk, pair, pl.ds(start + 1, count, stride=2)]
                for pair in range(pairs)
            ]
            part = times_right(jnp.concatenate(stack, 0), to_half[chunk])
            result = part if result is None else result + part
        return 0.125 * result

    wide = paired.shape[2] // 2
    planes1 = tile_x1 + 2 * RC
    if 2 * wide > rows:
        for chunk in range(chunks):
            for pair in range(planes1):
                paired[chunk, pair, rows:] = jnp.ones((2 * wide - rows, LANES), F32)
    for pair in range(planes1):
        x = RX - 2 * RC + 2 * pair
        put(pair, kappa[x] + kappa[x + 1])
    coarse = narrowed(planes1, 0, wide)
    for pair in range(planes1):
        k_one[pair] = coarse[pair * wide : (pair + 1) * wide]
    plane_setup(k_one, cx1, cy1, cz1, w1, d1, 0.25, 1, planes1 - 1)

    for pair in range(tile_x1):
        total = None
        for x in (RX + 2 * pair, RX + 2 * pair + 1):
            part = forcing[x] + neighbours(v_out, cx, cy, cz, x) - diag[x] * v_out[x]
            total = part if total is None else total + part
        put(pair, total)
    forcing_one = narrowed(tile_x1, RY, tile_y1)

    low, high = RC, RC + tile_y1
    nothing = jnp.zeros((wide, size_z1), F32)
    for x in range(planes1):
        f_one[x] = nothing
        if x in (0, planes1 - 1):
            v_one[x] = nothing
    for x in (0, 1, planes1 - 2, planes1 - 1):
        u_one[x] = nothing
    for x in range(tile_x1):
        f = forcing_one[x * tile_y1 : (x + 1) * tile_y1]
        f_one[x + RC, low:high] = f
        u_one[x + RC] = w1[x + RC] * f_one[x + RC]
        level_one[0, x] = f
        level_one[1, x] = u_one[x + RC, low:high]
        level_one[2, x] = k_one[x + RC, low:high]
    plane_sweep(u_one, v_one, f_one, cx1, cy1, cz1, w1, 1, planes1 - 1)
    pairs1 = planes1 // 2
    for pair in range(pairs1):
        total = None
        for x in (2 * pair, 2 * pair + 1):
            if x == 0:
                part = cx1[0] * v_one[1]
            elif x == planes1 - 1:
                part = cx1[x - 1] * v_one[x - 1]
            else:
                part = f_one[x] + neighbours(v_one, cx1, cy1, cz1, x) - d1[x] * v_one[x]
            total = part if total is None else total + part
        paired_one[pair] = total
    for pair in range(pairs1):
        packed[pair] = (
            paired_one[pair, pl.ds(0, ROWS, stride=2)] + paired_one[pair, pl.ds(1, ROWS, stride=2)]
        )
    half_pairs = pairs1 // 2
    result = times_right(
        jnp.concatenate([packed[p] for p in range(half_pairs)], 0), halve_lanes(size_z1, size_z1)
    ) + times_right(
        jnp.concatenate([packed[half_pairs + p] for p in range(half_pairs)], 0),
        halve_lanes(size_z1, size_z1, size_z1 // 2),
    )
    for p in range(half_pairs):
        block = 0.125 * result[p * ROWS : (p + 1) * ROWS]
        for device in range(blocks.shape[0]):
            blocks[device, p] = block

    for to, rows1, row0 in (
        (to_low, slice(0, R1), RY + 1),
        (to_high, slice(tile_y1 - R1, tile_y1), top - 2),
    ):
        for which in range(3):
            for x in range(tile_x1):
                flat_row = which * tile_x1 * R1 + x * R1
                to[flat_row // ROWS, flat_row % ROWS : flat_row % ROWS + R1] = level_one[
                    which, x, rows1
                ]
        start = 3 * tile_x1 * R1 // ROWS
        for x in range(tile_x):
            row = v_out[RX + x, row0 : row0 + 1]
            for chunk in range(chunks):
                to[start + chunk, x : x + 1] = row[:, chunk * LANES : (chunk + 1) * LANES]


def reach_of(layer):
    return R1 + 1 - layer


def middle(level_one, v_zero, from_low, from_high, window, to_low, to_high):
    _, tile_x1, tile_y1, _ = level_one.shape
    planes, rows, size_z = v_zero.shape
    top1 = R1 + tile_y1
    for which in range(3):
        for x in range(tile_x1):
            flat_row = which * tile_x1 * R1 + x * R1
            at, sub = flat_row // ROWS, flat_row % ROWS
            window[which, x, R1:top1] = level_one[which, x]
            window[which, x, 0:R1] = from_low[at, sub : sub + R1]
            window[which, x, top1:] = from_high[at, sub : sub + R1]
    chunks = size_z // LANES
    top = rows - RY
    for to, low in ((to_low, True), (to_high, False)):
        at = 0
        for which in (0, 2):
            for layer in range(1, R1 + 1):
                x = layer - 1 if low else tile_x1 - layer
                outer = 1 if which == 0 and layer == R1 else which
                to[at] = window[outer, x, R1:top1]
                at += 1
        loose = at * ROWS
        for which in (0, 2):
            for layer in range(1, R1 + 1):
                x = layer - 1 if low else tile_x1 - layer
                outer = 1 if which == 0 else which
                for distance in range(1, reach_of(layer) + 1):
                    source = outer if distance == reach_of(layer) else which
                    for row in (R1 - distance, top1 + distance - 1):
                        to[loose // ROWS, loose % ROWS : loose % ROWS + 1] = window[
                            source, x, row : row + 1
                        ]
                        loose += 1
        second, first = (RX + 1, RX) if low else (planes - RX - 2, planes - RX - 1)
        for row in (RY - 1, top):
            for chunk in range(chunks):
                lanes = slice(chunk * LANES, (chunk + 1) * LANES)
                to[loose // ROWS, loose % ROWS : loose % ROWS + 1] = v_zero[first, row : row + 1, lanes]
                loose += 1
        at = -(-loose // ROWS)
        for chunk in range(chunks):
            lanes = slice(chunk * LANES, (chunk + 1) * LANES)
            for half in range((top - RY) // ROWS):
                to[at] = v_zero[second, RY + half * ROWS : RY + (half + 1) * ROWS, lanes]
                at += 1


def middle_tiles(tile_y, chunks):
    loose = 2 * sum(2 * reach_of(layer) for layer in range(1, R1 + 1)) + 2 * chunks
    return 2 * R1 + -(-loose // ROWS) + chunks * tile_y // ROWS


class Grid:
    def __init__(self, sizes, strides, scales, rows, lanes):
        self.sizes = sizes
        self.strides = strides
        self.scales = scales
        self.rows = rows
        self.lanes = lanes
        self.ratios = tuple(2 if extent % 2 == 0 else 1 for extent in sizes)
        self.cells = sizes[0] * sizes[1] * sizes[2]
        self.exact = self.cells <= 64 or self.ratios == (1, 1, 1)

    def coarser(self):
        sizes = tuple(extent // ratio for extent, ratio in zip(self.sizes, self.ratios))
        scales = tuple(s / (ratio * ratio) for s, ratio in zip(self.scales, self.ratios))
        strides = tuple(s * ratio for s, ratio in zip(self.strides, self.ratios[1:]))
        return Grid(sizes, strides, scales, self.rows, self.lanes)


def next_plane(v):
    return v if v.shape[0] == 1 else jnp.concatenate([v[1:], v[:1]], 0)


def last_plane(v):
    return v if v.shape[0] == 1 else jnp.concatenate([v[-1:], v[:-1]], 0)


def restrict_whole(v, grid):
    if grid.ratios[0] == 2:
        v = jnp.concatenate(
            [v[2 * x : 2 * x + 1] + v[2 * x + 1 : 2 * x + 2] for x in range(grid.sizes[0] // 2)], 0
        )
    for axis in (1, 2):
        if grid.ratios[axis] == 2:
            step = grid.strides[axis - 1]
            even = mod(div(iota(v.shape, axis), step), 2) == 0
            v = v + jnp.where(even, ahead(v, axis, step), back(v, axis, step))
    return (1.0 / (grid.ratios[0] * grid.ratios[1] * grid.ratios[2])) * v


def prolong_whole(v, grid):
    if grid.ratios[0] == 1:
        return v
    return jnp.concatenate([v[x // 2 : x // 2 + 1] for x in range(grid.sizes[0])], 0)


def whole_operator(kappa, grid):
    half_x, half_y, half_z = (0.5 * s for s in grid.scales)
    step_y, step_z = grid.strides
    cx = half_x * (kappa + next_plane(kappa))
    cy = half_y * (kappa + ahead(kappa, 1, step_y))
    cz = half_z * (kappa + ahead(kappa, 2, step_z))
    diag = mass_rate + cx + last_plane(cx)
    diag = diag + (cy + back(cy, 1, step_y)) + (cz + back(cz, 2, step_z))
    return cx, cy, cz, diag, relax_weight / diag


def whole_neighbours(v, operator, grid):
    cx, cy, cz = operator[:3]
    step_y, step_z = grid.strides
    total = cx * next_plane(v) + last_plane(cx * v)
    total = total + (cy * ahead(v, 1, step_y) + back(cy * v, 1, step_y))
    return total + (cz * ahead(v, 2, step_z) + back(cz * v, 2, step_z))


def whole_sweep(v, forcing, operator, grid):
    return (1.0 - relax_weight) * v + operator[4] * (forcing + whole_neighbours(v, operator, grid))


class ExactSolve:
    def __init__(self, grid, kappa=None, inverse=None):
        size_x, size_y, size_z = grid.sizes
        self.grid = grid
        self.across = across = size_x * size_y
        _, step_z = grid.strides
        self.period = period = size_z * step_z
        cells = grid.cells
        padded = -(-cells // ROWS) * ROWS
        assert across <= step_z and 2 * period <= grid.lanes
        shape = (padded, grid.lanes)
        i, j = iota(shape, 0), iota(shape, 1)
        self.i, self.j = i, j
        if kappa is None:
            self.inverse = inverse
            return

        def places_of_row(n):
            sub = mod(n, across)
            return div(sub, size_y), mod(sub, size_y), div(n, across)

        def places_of_lane(n):
            n = mod(n, period)
            sub = mod(n, step_z)
            return div(sub, size_y), mod(sub, size_y), div(n, step_z)

        at_i, at_j = places_of_row(i), places_of_lane(j)
        live = (mod(j, step_z) < across) & (i < cells)
        same = (at_i[0] == at_j[0]) & (at_i[1] == at_j[1]) & (at_i[2] == at_j[2]) & live
        left = j < period
        factor = jnp.zeros(shape, F32)
        for d in range(3):
            equal = [at_i[other] == at_j[other] for other in range(3) if other != d]
            for step in (1, grid.sizes[d] - 1):
                hit = mod(at_i[d] + step, grid.sizes[d]) == at_j[d]
                factor = factor + jnp.where(
                    hit & equal[0] & equal[1], F32(0.5 * grid.scales[d]), F32(0.0)
                )
        k_row = self.as_row(kappa)
        k_column = jnp.sum(jnp.where(same & left, k_row, 0.0), axis=1, keepdims=True)
        coupled = jnp.where(live & left, factor * (k_column + k_row), 0.0)
        diag = mass_rate + jnp.sum(coupled, axis=1, keepdims=True)
        matrix = jnp.where(same & left, diag - coupled, -coupled)
        matrix = jnp.where(left, matrix, jnp.where(same, F32(1.0), F32(0.0)))
        for n in range(cells):
            lane = (n // across) * step_z + n % across
            pivot_row = matrix[n : n + 1] / matrix[n : n + 1, lane : lane + 1]
            column = matrix[:, lane : lane + 1]
            matrix = jnp.where(i == n, pivot_row, matrix - column * pivot_row)
        self.inverse = jnp.where((j >= period) & (j < 2 * period) & live, matrix, 0.0)

    def as_row(self, v):
        grid = self.grid
        size_x, size_y, _ = grid.sizes
        step_y, step_z = grid.strides
        sub = mod(iota((1, grid.lanes), 1), step_z)
        result = jnp.zeros((1, grid.lanes), F32)
        for x in range(size_x):
            for y in range(size_y):
                row = v[x, y * step_y : y * step_y + 1]
                result = jnp.where(sub == x * size_y + y, row, result)
        return result

    def solve(self, forcing):
        grid = self.grid
        size_x, size_y, _ = grid.sizes
        step_y, step_z = grid.strides
        solved = jnp.sum(self.inverse * self.as_row(forcing), axis=1, keepdims=True)
        at_z = div(mod(self.j, self.period), step_z)
        spread = jnp.where(div(self.i, self.across) == at_z, solved, 0.0)
        planes = []
        for x in range(size_x):
            rows = []
            for y in range(size_y):
                mine = mod(self.i, self.across) == x * size_y + y
                row = jnp.sum(jnp.where(mine, spread, 0.0), axis=0, keepdims=True)
                rows.append(jnp.broadcast_to(row, (step_y, grid.lanes)))
            planes.append(jnp.concatenate(rows, 0)[None])
        return jnp.concatenate(planes, 0)


def levels_of(counts, tile_sizes):
    sizes = tuple(count * extent for count, extent in zip(counts, tile_sizes)) + tile_sizes[2:]
    grid = Grid(sizes, (1, 1), (0.0625, 0.0625, 0.0625), sizes[1], LANES)
    grids = [grid]
    while not grid.exact:
        grid = grid.coarser()
        grids.append(grid)
    return grids


class Operator:
    def __init__(self, ref):
        self.ref = ref

    def __getitem__(self, part):
        if isinstance(part, slice):
            return [self.ref[p] for p in range(*part.indices(5))]
        return self.ref[part]


def prepare(counts, grids, blocks, _, *outputs):
    count_x, count_y = counts
    planes, rows, _ = grids[0].sizes
    half_x, half_y = planes // count_x, rows // count_y
    assert half_x * half_y == ROWS and ROWS % half_y == 0
    sub = iota((ROWS, LANES), 0)
    kappa = [[jnp.ones((ROWS, LANES), F32)] * (rows // ROWS) for _ in range(planes)]
    for tx in range(count_x):
        for ty in range(count_y):
            piece = blocks[tx * count_y + ty]
            for p in range(half_x):
                x, start = tx * half_x + p, ty * half_y
                group, offset = start // ROWS, start % ROWS
                shift = (offset - p * half_y) % ROWS
                moved = pltpu.roll(piece, shift, 0) if shift else piece
                mine = (sub >= offset) & (sub < offset + half_y)
                kappa[x][group] = jnp.where(mine, moved, kappa[x][group])
    kappa = jnp.concatenate([jnp.concatenate(groups, 0)[None] for groups in kappa], 0)
    kappas = [kappa]
    for grid in grids[:-1]:
        kappas.append(restrict_whole(kappas[-1], grid))
    outputs[-1][...] = ExactSolve(grids[-1], kappas[-1]).inverse
    for number, grid in enumerate(grids[:-1]):
        for part, value in enumerate(whole_operator(kappas[number], grid)):
            outputs[number][part] = value


def solve_whole(forcing, levels, exact):
    if not levels:
        return exact.solve(forcing)
    grid, operator = levels[0]
    v = operator[4] * forcing
    v = whole_sweep(v, forcing, operator, grid)
    residual = forcing + whole_neighbours(v, operator, grid) - operator[3] * v
    v = v + prolong_whole(solve_whole(restrict_whole(residual, grid), levels[1:], exact), grid)
    for _ in range(2):
        v = whole_sweep(v, forcing, operator, grid)
    return v


def assemble(blocks, count_x, count_y, half_x, half_y, size_z2):
    rows = count_y * half_y
    groups = rows // ROWS
    planes = count_x * half_x
    assert rows % ROWS == 0
    used = half_y + RC
    sub = iota((ROWS, LANES), 0)
    lane = iota((ROWS, LANES), 1)
    nothing = jnp.zeros((ROWS, LANES), F32)
    forcing = [[nothing] * groups for _ in range(planes)]
    half_pairs = blocks.shape[1]
    ring = RC // 2
    for tx in range(count_x):
        for ty in range(count_y):
            for p in range(half_pairs):
                piece = blocks[tx * count_y + ty, p]
                start = (ty * half_y - ring) % rows
                group, offset = start // ROWS, start % ROWS
                piece = pltpu.roll(piece, offset, 0) if offset else piece
                turned = pltpu.roll(piece, size_z2, 1)
                for half in range(2):
                    moved = jnp.where((lane < size_z2) == (half == 0), piece, turned)
                    x = (tx * half_x - ring + half * half_pairs + p) % planes
                    at = group
                    mine = (sub >= offset) & (sub < offset + used)
                    forcing[x][at] = forcing[x][at] + jnp.where(mine, moved, 0.0)
                    if offset + used > ROWS:
                        at = (group + 1) % groups
                        mine = sub < offset + used - ROWS
                        forcing[x][at] = forcing[x][at] + jnp.where(mine, moved, 0.0)
    return jnp.concatenate([jnp.concatenate(groups, 0)[None] for groups in forcing], 0)


def coarse_up(
    counts, grids, blocks, window_one, one_low, one_high, row_low, row_high,
    v_zero, forcing0, cx, cy, cz, weight, *rest,
):
    prepared, rest = rest[: len(grids)], rest[len(grids) :]
    (
        out, mixed_low, mixed_high, kappa_low, kappa_high, first_low, first_high,
        v_one, cx1, cy1, cz1, w1, one_a, one_b, zero_a, zero_b,
    ) = rest
    count_x, count_y = counts
    _, tile_x1, rows1, size_z1 = window_one.shape
    tile_y1 = rows1 - 2 * R1
    top1 = R1 + tile_y1
    half_x, half_y, size_z2 = tile_x1 // 2, tile_y1 // 2, size_z1 // 2
    sizes = grids[0].sizes
    forcing2 = assemble(blocks, count_x, count_y, half_x, half_y, size_z2)
    levels = [
        (grid, Operator(prepared[number])) for number, grid in enumerate(grids[:-1])
    ]
    exact = ExactSolve(grids[-1], inverse=prepared[-1][...])

    planes1 = tile_x1 + 2 * R1
    for message, mixed, kappa_rim, low in (
        (one_low, mixed_low, kappa_low, True), (one_high, mixed_high, kappa_high, False)
    ):
        at, loose = 0, 2 * R1 * ROWS
        for rim, fill in ((mixed, 0.0), (kappa_rim, 1.0)):
            for layer in range(1, R1 + 1):
                x = R1 - layer if low else layer - 1
                rim[x] = jnp.full((rows1, size_z1), fill, F32)
                rim[x, R1:top1] = message[at]
                at += 1
                for distance in range(1, reach_of(layer) + 1):
                    for row in (R1 - distance, top1 + distance - 1):
                        rim[x, row : row + 1] = message[
                            loose // ROWS, loose % ROWS : loose % ROWS + 1
                        ]
                        loose += 1

    def stacked(low, which, high):
        whole = [(low, x) for x in range(R1)]
        whole += [(window_one.at[which], x) for x in range(tile_x1)]
        whole += [(high, x) for x in range(R1)]
        return Planes(0, whole)

    forcing1 = stacked(mixed_low, 0, mixed_high)
    kappa1 = stacked(kappa_low, 2, kappa_high)
    plane_setup(kappa1, cx1, cy1, cz1, w1, None, 0.25, 1, planes1 - 1)
    row = iota((rows1, size_z1), 0)
    for mixed, rim, low in ((mixed_low, first_low, True), (mixed_high, first_high, False)):
        for layer in range(1, R1 + 1):
            x = R1 - layer if low else layer - 1
            if layer == R1:
                rim[x] = mixed[x]
            else:
                reach = reach_of(layer) - 1
                inside = (row >= R1 - reach) & (row < top1 + reach)
                at = x if low else R1 + tile_x1 + x
                rim[x] = jnp.where(inside, w1[at] * mixed[x], mixed[x])
    start1 = stacked(first_low, 1, first_high)
    plane_sweep(start1, v_one, forcing1, cx1, cy1, cz1, w1, 1, planes1 - 1)

    solved = solve_whole(forcing2, levels, exact)
    solved = solved.reshape(sizes[0] * sizes[1], LANES)

    whole_x1, whole_y1 = 2 * sizes[0], 2 * sizes[1]
    start_x = lax.axis_index("tx") * tile_x1 + (whole_x1 - R1)
    start_y = lax.axis_index("ty") * tile_y1 + (whole_y1 - R1)
    row = iota((planes1 * rows1, 1), 0)
    at_x = mod(div(row, rows1) + start_x, whole_x1)
    at_y = mod(mod(row, rows1) + start_y, whole_y1)
    target = div(at_x, 2) * sizes[1] + div(at_y, 2)
    left = ones_where(iota((planes1 * rows1, sizes[0] * sizes[1]), 1) == target)
    shape = (LANES, size_z1)
    right = ones_where(iota(shape, 0) == div(iota(shape, 1), 2))
    raised = times_right(times_left(left, solved), right)
    for x in range(1, planes1 - 1):
        one_a[x] = v_one[x] + raised[x * rows1 : (x + 1) * rows1]
    plane_sweep(one_a, one_b, forcing1, cx1, cy1, cz1, w1, 2, planes1 - 2)
    plane_sweep(one_b, one_a, forcing1, cx1, cy1, cz1, w1, 3, planes1 - 3)

    planes, rows, size_z = v_zero.shape
    first, last = R1 - 1, planes1 - R1 + 1
    stack = jnp.concatenate([one_a[x] for x in range(first, last)], 0)
    count = last - first
    shape = (count * rows, count * rows1)
    out_row, in_row = iota((count * rows, 1), 0), iota(shape, 1)
    target = div(out_row, rows) * rows1 + div(mod(out_row, rows) + (2 * R1 - RY), 2)
    left = ones_where(in_row == target)
    shape = (size_z1, size_z)
    right = ones_where(iota(shape, 0) == div(iota(shape, 1), 2))
    raised = times_right(times_left(left, stack), right)
    chunks = size_z // LANES
    top = rows - RY
    for x in range(RX - 1, planes - RX + 1):
        zero_b[x] = v_zero[x]
    for rim_x in (RX - 2, planes - RX + 1):
        zero_b[rim_x] = jnp.zeros((rows, size_z), F32)
    for x in range(planes - 2 * RX):
        at = 3 * tile_x1 * R1 // ROWS
        for chunk in range(chunks):
            lanes = slice(chunk * LANES, (chunk + 1) * LANES)
            zero_b[RX + x, RY - 2 : RY - 1, lanes] = row_low[at + chunk, x : x + 1]
            zero_b[RX + x, top + 1 : top + 2, lanes] = row_high[at + chunk, x : x + 1]
    for message, second, nearest in (
        (one_low, RX - 2, RX - 1), (one_high, planes - RX + 1, planes - RX)
    ):
        loose = 2 * R1 * ROWS + 2 * sum(2 * reach_of(layer) for layer in range(1, R1 + 1))
        for r in (RY - 1, top):
            for chunk in range(chunks):
                lanes = slice(chunk * LANES, (chunk + 1) * LANES)
                zero_b[nearest, r : r + 1, lanes] = message[
                    loose // ROWS, loose % ROWS : loose % ROWS + 1
                ]
                loose += 1
        at = -(-loose // ROWS)
        for chunk in range(chunks):
            lanes = slice(chunk * LANES, (chunk + 1) * LANES)
            for half in range((top - RY) // ROWS):
                zero_b[second, RY + half * ROWS : RY + (half + 1) * ROWS, lanes] = message[at]
                at += 1
    for x in range(RX - 2, planes - RX + 2):
        at = (x - RX + 2 * R1) // 2 - first
        zero_a[x] = zero_b[x] + raised[at * rows : (at + 1) * rows]
    plane_sweep(zero_a, zero_b, forcing0, cx, cy, cz, weight, RX - 1, planes - RX + 1)
    plane_sweep(zero_b, zero_a, forcing0, cx, cy, cz, weight, RX, planes - RX)
    for x in range(planes - 2 * RX):
        out[x] = zero_a[x + RX, RY:top]


VM = pl.BlockSpec(memory_space=pltpu.VMEM)
IN_PLACE = pl.BlockSpec(memory_space=pltpu.HBM)


def call(kernel, operands, outputs, scratch, spec=VM):
    def typed(output):
        return output if isinstance(output, jax.ShapeDtypeStruct) else jax.ShapeDtypeStruct(output, F32)

    return pl.pallas_call(
        kernel,
        in_specs=[spec] * len(operands),
        out_specs=[VM] * len(outputs),
        out_shape=[typed(output) for output in outputs],
        scratch_shapes=[pltpu.VMEM(s, F32) if isinstance(s, tuple) else s for s in scratch],
        compiler_params=pltpu.CompilerParams(vmem_limit_bytes=24 * 1024 * 1024),
    )(*operands)


def exchange(to_low, to_high, axis):
    count = lax.axis_size(axis)
    from_low = lax.ppermute(to_high, axis, [(i, (i + 1) % count) for i in range(count)])
    from_high = lax.ppermute(to_low, axis, [((i + 1) % count, i) for i in range(count)])
    return from_low, from_high


def to_everyone(blocks):
    return lax.all_to_all(blocks, ("tx", "ty"), 0, 0)


def cycle(concentration, source, material):
    tile_x, tile_y, size_z = concentration.shape
    chunks = size_z // LANES
    counts = lax.axis_size("tx"), lax.axis_size("ty")
    everyone = counts[0] * counts[1]
    rows = tile_y + 2 * RY
    message = (tile_x + 1, ROWS, size_z)
    *inputs, to_low, to_high = call(
        edges,
        (concentration, source, material),
        tuple(jax.ShapeDtypeStruct(v.shape, v.dtype) for v in (concentration, source, material))
        + (message, message),
        (pltpu.SemaphoreType.DMA((3,)),),
        IN_PLACE,
    )
    from_low, from_high = exchange(to_low, to_high, "ty")
    message = (len(BASE_PLANES) + 1, tile_y, size_z)
    window, to_low, to_high = call(
        sides, (*inputs, from_low, from_high), ((3, tile_x, rows, size_z), message, message), ()
    )
    from_low, from_high = exchange(to_low, to_high, "tx")

    zero = (tile_x + 2 * RX, rows, size_z)
    one_tile = (tile_x // 2, tile_y // 2, size_z // 2)
    two_tile = tuple(extent // 2 for extent in one_tile)
    grids = levels_of(counts, two_tile)
    (kappa_blocks,) = call(
        shrink,
        (window,),
        ((everyone, two_tile[0] * two_tile[1], LANES),),
        ((one_tile[0], rows, LANES), one_tile[1:]),
    )
    kappa_blocks = to_everyone(kappa_blocks)

    wide = -(-rows // (2 * ROWS)) * ROWS
    small = (one_tile[0] + 2 * RC, wide, one_tile[2])
    pairs1 = small[0] // 2
    message = (3 * one_tile[0] * R1 // ROWS + chunks, ROWS, LANES)
    assert one_tile[2] == LANES and tile_x <= ROWS and one_tile[1] == ROWS
    v_zero, forcing0, cx, cy, cz, weight, level_one, blocks, to_low, to_high = call(
        fine_down,
        (window, from_low, from_high),
        (zero,) * 6
        + ((3,) + one_tile, (everyone, pairs1 // 2, ROWS, LANES), message, message),
        (
            (6, rows, size_z),
            (4, rows, size_z),
            (8, rows, size_z),
            zero,
            zero,
            (chunks, max(small[0], tile_x), 2 * wide, LANES),
        )
        + (small,) * 9
        + ((pairs1, wide, one_tile[2]), (pairs1, ROWS, one_tile[2])),
    )
    row_low, row_high = exchange(to_low, to_high, "ty")
    blocks = to_everyone(blocks)
    rows1 = one_tile[1] + 2 * R1
    message = (middle_tiles(tile_y, chunks), ROWS, LANES)
    window_one, to_low, to_high = call(
        middle,
        (level_one, v_zero, row_low, row_high),
        ((3, one_tile[0], rows1, one_tile[2]), message, message),
        (),
    )
    one_low, one_high = exchange(to_low, to_high, "tx")
    lattice = grids[0].sizes[1], LANES
    prepared = call(
        functools.partial(prepare, counts, grids),
        (kappa_blocks, window_one),
        tuple((5, grid.sizes[0]) + lattice for grid in grids[:-1])
        + ((-(-grids[-1].cells // ROWS) * ROWS, LANES),),
        (),
    )
    one = (one_tile[0] + 2 * R1, rows1, one_tile[2])
    rim = (R1,) + one[1:]
    (updated,) = call(
        functools.partial(coarse_up, counts, grids),
        (blocks, window_one, one_low, one_high, row_low, row_high)
        + (v_zero, forcing0, cx, cy, cz, weight, *prepared),
        (concentration.shape,),
        (rim,) * 6 + (one,) * 7 + (zero, zero),
    )
    return updated


def solution(mesh):
    placed = (P("tx", "ty", None), P("tx", "ty", None), P("tx", "ty", None))
    return jax.shard_map(
        cycle, mesh=mesh, in_specs=placed, out_specs=P("tx", "ty", None), check_vma=False
    )
```

profile of v0, /device:TPU:0, one launch (start us, length us, event | category | flops | bytes accessed | tf_op | source)
XLA Modules:
  0.0 54.3 jit_solution(363789406607435903)
XLA Ops:
  0.0 0.0 copy-start.2
  0.0 0.9 %copy-done.2 = f32[8,16,256]{2,1,0:T(8,128)S(1)} copy-done((f32[8,16,256]{2,1,0:T(8,128)S(1)}, f32[8,16,256]{2,1,0:T(8,128)}, u32[]{:S(2)}) %copy-start.2) | copy-done | bytes 131096
  0.9 0.0 copy-start.3
  0.9 0.9 %copy-done.3 = f32[8,16,256]{2,1,0:T(8,128)S(1)} copy-done((f32[8,16,256]{2,1,0:T(8,128)S(1)}, f32[8,16,256]{2,1,0:T(8,128)}, u32[]{:S(2)}) %copy-start.3) | copy-done | bytes 131096
  1.8 0.0 copy-start.4
  1.8 0.9 %copy-done.4 = s32[8,16,256]{2,1,0:T(8,128)S(1)} copy-done((s32[8,16,256]{2,1,0:T(8,128)S(1)}, s32[8,16,256]{2,1,0:T(8,128)}, u32[]{:S(2)}) %copy-start.4) | copy-done | bytes 131096
  2.7 0.6 %shard_map.37 = (f32[8,16,256]{2,1,0:T(8,128)S(1)}, f32[8,16,256]{2,1,0:T(8,128)S(1)}, s32[8,16,256]{2,1,0:T(8,128)S(1)}, f32[9,8,256]{2,1,0:T(8,128)S(1)}, f32[9,8,256]{2,1,0:T(8,128)S(1)}) custom-call(f32[8,16,256]{2,1,0:T(8,128)S(1)} %copy-done.2, f32[8,16,256]{2,1,0:T(8,128)S(1)} %copy-done.3, s32[8,16,256]{2,1,0:T(8,128)S(1)} %copy-done.4), custom_call_target="tpu_custom_call" | custom-call | tf_op jit(solution)/shard_map/pallas_call | solution.py:797
  3.3 0.5 %collective-permute-start = (f32[9,8,256]{2,1,0:T(8,128)S(1)}, f32[9,8,256]{2,1,0:T(8,128)S(1)}, u32[]{:S(2)}, u32[]{:S(2)}) collective-permute-start(f32[9,8,256]{2,1,0:T(8,128)S(1)} %get-tuple-element.33), channel_id=1, source_target_pairs={{0,1},{1,2},{2,3},{3,0},{4,5},{5,6},{6,7},{7,4},{8,9},{9,10},{10,1... | collective-permute-start | bytes 221192 | tf_op jit(solution)/shard_map/ppermute | solution.py:809
  3.9 2.0 %collective-permute-start.1 = (f32[9,8,256]{2,1,0:T(8,128)S(1)}, f32[9,8,256]{2,1,0:T(8,128)S(1)}, u32[]{:S(2)}, u32[]{:S(2)}) collective-permute-start(f32[9,8,256]{2,1,0:T(8,128)S(1)} %get-tuple-element.34), channel_id=1, source_target_pairs={{1,0},{2,1},{3,2},{0,3},{5,4},{6,5},{7,6},{4,7},{9,8},{10,9},{11,1... | collective-permute-start | bytes 221192 | tf_op jit(solution)/shard_map/ppermute | solution.py:810
  5.9 2.0 %collective-permute-done.from_low = f32[9,8,256]{2,1,0:T(8,128)S(1)} collective-permute-done((f32[9,8,256]{2,1,0:T(8,128)S(1)}, f32[9,8,256]{2,1,0:T(8,128)S(1)}, u32[]{:S(2)}, u32[]{:S(2)}) %collective-permute-start) | collective-permute-done | bytes 73760 | tf_op jit(solution)/shard_map/ppermute | solution.py:809
  7.8 0.6 %collective-permute-done.1.from_high = f32[9,8,256]{2,1,0:T(8,128)S(1)} collective-permute-done((f32[9,8,256]{2,1,0:T(8,128)S(1)}, f32[9,8,256]{2,1,0:T(8,128)S(1)}, u32[]{:S(2)}, u32[]{:S(2)}) %collective-permute-start.1) | collective-permute-done | bytes 73760 | tf_op jit(solution)/shard_map/ppermute | solution.py:810
  8.4 0.2 shard_map.38
  8.7 1.0 %shard_map.41 = f32[32,8,128]{2,1,0:T(8,128)} custom-call(f32[3,8,24,256]{3,2,1,0:T(8,128)S(1)} %get-tuple-element.35.window), custom_call_target="tpu_custom_call" | custom-call | tf_op jit(solution)/shard_map/pallas_call | solution.py:797
  9.7 6.3 %all-to-all-start.1 = ((f32[32,8,128]{2,1,0:T(8,128)}), f32[32,8,128]{2,1,0:T(8,128)S(1)}, u32[]{:S(2)}, u32[]{:S(2)}) async-start(f32[32,8,128]{2,1,0:T(8,128)} %shard_map.41), calls=%async_computation.1 | async-start | bytes 262144 | tf_op jit(solution)/shard_map/all_to_all | solution.py:815
  16.0 1.8 %collective-permute-start.2 = (f32[10,16,256]{2,1,0:T(8,128)S(1)}, f32[10,16,256]{2,1,0:T(8,128)S(1)}, u32[]{:S(2)}, u32[]{:S(2)}) collective-permute-start(f32[10,16,256]{2,1,0:T(8,128)S(1)} %get-tuple-element.36), channel_id=1, source_target_pairs={{0,4},{4,8},{8,12},{12,16},{16,20},{20,24},{24,28},{28,0},{1,5},{5... | collective-permute-start | bytes 491528 | tf_op jit(solution)/shard_map/ppermute | solution.py:809
  17.9 3.0 %collective-permute-start.3 = (f32[10,16,256]{2,1,0:T(8,128)S(1)}, f32[10,16,256]{2,1,0:T(8,128)S(1)}, u32[]{:S(2)}, u32[]{:S(2)}) collective-permute-start(f32[10,16,256]{2,1,0:T(8,128)S(1)} %get-tuple-element.37), channel_id=1, source_target_pairs={{4,0},{8,4},{12,8},{16,12},{20,16},{24,20},{28,24},{0,28},{5,1},{9... | collective-permute-start | bytes 491528 | tf_op jit(solution)/shard_map/ppermute | solution.py:810
  20.8 6.5 %collective-permute-done.2.from_low = f32[10,16,256]{2,1,0:T(8,128)S(1)} collective-permute-done((f32[10,16,256]{2,1,0:T(8,128)S(1)}, f32[10,16,256]{2,1,0:T(8,128)S(1)}, u32[]{:S(2)}, u32[]{:S(2)}) %collective-permute-start.2) | collective-permute-done | bytes 163872 | tf_op jit(solution)/shard_map/ppermute | solution.py:809
  27.4 1.0 %collective-permute-done.3.from_high = f32[10,16,256]{2,1,0:T(8,128)S(1)} collective-permute-done((f32[10,16,256]{2,1,0:T(8,128)S(1)}, f32[10,16,256]{2,1,0:T(8,128)S(1)}, u32[]{:S(2)}, u32[]{:S(2)}) %collective-permute-start.3) | collective-permute-done | bytes 163872 | tf_op jit(solution)/shard_map/ppermute | solution.py:810
  28.4 2.4 %shard_map.39 = (f32[14,24,256]{2,1,0:T(8,128)S(1)}, f32[14,24,256]{2,1,0:T(8,128)S(1)}, f32[14,24,256]{2,1,0:T(8,128)S(1)}, f32[14,24,256]{2,1,0:T(8,128)S(1)},...) custom-call(f32[3,8,24,256]{3,2,1,0:T(8,128)S(1)} %get-tuple-element, ...), custom_call_target="tpu_custom_call" | custom-call | tf_op jit(solution)/shard_map/pallas_call | solution.py:797
  30.8 0.0 all-to-all-done.1.blocks
  30.8 3.8 %all-to-all-start = ((f32[32,2,8,128]{3,2,1,0:T(8,128)}), f32[32,2,8,128]{3,2,1,0:T(8,128)S(1)}, u32[]{:S(2)}, u32[]{:S(2)}) async-start(f32[32,2,8,128]{3,2,1,0:T(8,128)} %get-tuple-element.38), calls=%async_computation | async-start | bytes 524288 | tf_op jit(solution)/shard_map/all_to_all | solution.py:815
  34.6 0.3 collective-permute-start.4
  34.9 1.5 %collective-permute-start.5 = (f32[8,8,128]{2,1,0:T(8,128)S(1)}, f32[8,8,128]{2,1,0:T(8,128)S(1)}, u32[]{:S(2)}, u32[]{:S(2)}) collective-permute-start(f32[8,8,128]{2,1,0:T(8,128)S(1)} %get-tuple-element.42), channel_id=1, source_target_pairs={{1,0},{2,1},{3,2},{0,3},{5,4},{6,5},{7,6},{4,7},{9,8},{10,9},{11,1... | collective-permute-start | bytes 98312 | tf_op jit(solution)/shard_map/ppermute | solution.py:810
  36.4 1.9 %collective-permute-done.4.from_low.row_low = f32[8,8,128]{2,1,0:T(8,128)S(1)} collective-permute-done((f32[8,8,128]{2,1,0:T(8,128)S(1)}, f32[8,8,128]{2,1,0:T(8,128)S(1)}, u32[]{:S(2)}, u32[]{:S(2)}) %collective-permute-start.4) | collective-permute-done | bytes 32800 | tf_op jit(solution)/shard_map/ppermute | solution.py:809
  38.2 0.0 collective-permute-done.5.from_high.row_high
  38.3 1.9 %collective-permute-start.6 = (f32[18,8,128]{2,1,0:T(8,128)S(1)}, f32[18,8,128]{2,1,0:T(8,128)S(1)}, u32[]{:S(2)}, u32[]{:S(2)}) collective-permute-start(f32[18,8,128]{2,1,0:T(8,128)S(1)} %get-tuple-element.44), channel_id=1, source_target_pairs={{0,4},{4,8},{8,12},{12,16},{16,20},{20,24},{24,28},{28,0},{1,5},{5... | collective-permute-start | bytes 221192 | tf_op jit(solution)/shard_map/ppermute | solution.py:809
  40.1 4.0 %collective-permute-start.7 = (f32[18,8,128]{2,1,0:T(8,128)S(1)}, f32[18,8,128]{2,1,0:T(8,128)S(1)}, u32[]{:S(2)}, u32[]{:S(2)}) collective-permute-start(f32[18,8,128]{2,1,0:T(8,128)S(1)} %get-tuple-element.45), channel_id=1, source_target_pairs={{4,0},{8,4},{12,8},{16,12},{20,16},{24,20},{28,24},{0,28},{5,1},{9... | collective-permute-start | bytes 221192 | tf_op jit(solution)/shard_map/ppermute | solution.py:810
  44.1 3.2 %shard_map.42 = (f32[5,16,16,128]{3,2,1,0:T(8,128)S(1)}, f32[5,8,16,128]{3,2,1,0:T(8,128)S(1)}, f32[5,4,16,128]{3,2,1,0:T(8,128)S(1)}, f32[32,128]{1,0:T(8,128)S(1)}) custom-call(f32[32,8,128]{2,1,0:T(8,128)S(1)} %all-to-all-done.1.blocks, f32[3,4,16,128]{3,2,1,0:T(8,128)S(1)} %get-tuple-element.43._.window_one), custom_call_target="tpu_custom_call" | custom-call | tf_op jit(solution)/shard_map/pallas_call | solution.py:797
  47.3 0.0 copy-start
  47.3 0.7 %copy-done = f32[5,8,16,128]{3,2,1,0:T(8,128)} copy-done((f32[5,8,16,128]{3,2,1,0:T(8,128)}, f32[5,8,16,128]{3,2,1,0:T(8,128)S(1)}, u32[]{:S(2)}) %copy-start) | copy-done | bytes 327704
  48.0 0.0 collective-permute-done.6.one_low
  48.0 0.0 collective-permute-done.7.one_high
  48.0 0.0 copy-start.5
  48.0 0.6 %copy-done.5 = f32[18,8,128]{2,1,0:T(8,128)} copy-done((f32[18,8,128]{2,1,0:T(8,128)}, f32[18,8,128]{2,1,0:T(8,128)S(1)}, u32[]{:S(2)}) %copy-start.5) | copy-done | bytes 73752
  48.6 0.0 all-to-all-done.blocks
  48.6 0.0 copy-start.1
  48.6 1.0 %copy-done.1 = f32[5,8,16,128]{3,2,1,0:T(8,128)S(1)} copy-done((f32[5,8,16,128]{3,2,1,0:T(8,128)S(1)}, f32[5,8,16,128]{3,2,1,0:T(8,128)}, u32[]{:S(2)}) %copy-start.1) | copy-done | bytes 327704
  49.6 0.0 copy-start.6
  49.6 0.9 %copy-done.6 = f32[18,8,128]{2,1,0:T(8,128)S(1)} copy-done((f32[18,8,128]{2,1,0:T(8,128)S(1)}, f32[18,8,128]{2,1,0:T(8,128)}, u32[]{:S(2)}) %copy-start.6) | copy-done | bytes 73752
  50.5 3.8 %shard_map.43 = f32[8,16,256]{2,1,0:T(8,128)} custom-call(f32[32,2,8,128]{3,2,1,0:T(8,128)S(1)} %all-to-all-done.blocks, f32[3,4,16,128]{3,2,1,0:T(8,128)S(1)} %get-tuple-element.43._.window_one, f32[18,8,128]{2,1,0:T(8,128)S(1)} %collective-permute-done.6.one_low, f32[18,8,128]{2,1,0:T(8,128)S(1)} %copy-done.6, ...), custom_call_target="tpu_custom_call" | custom-call | tf_op jit(solution)/shard_map/pallas_call | solution.py:797
  (1 shorter events, 0.0 us)
Async XLA Ops:
  0.0 0.9 %copy-start.2 = (f32[8,16,256]{2,1,0:T(8,128)S(1)}, f32[8,16,256]{2,1,0:T(8,128)}, u32[]{:S(2)}) copy-start(f32[8,16,256]{2,1,0:T(8,128)} %conc_in.1) | copy-start | bytes 393220
  0.9 0.9 %copy-start.3 = (f32[8,16,256]{2,1,0:T(8,128)S(1)}, f32[8,16,256]{2,1,0:T(8,128)}, u32[]{:S(2)}) copy-start(f32[8,16,256]{2,1,0:T(8,128)} %source_in.1) | copy-start | bytes 393220
  1.8 0.9 %copy-start.4 = (s32[8,16,256]{2,1,0:T(8,128)S(1)}, s32[8,16,256]{2,1,0:T(8,128)}, u32[]{:S(2)}) copy-start(s32[8,16,256]{2,1,0:T(8,128)} %material_in.1) | copy-start | bytes 393220
  3.3 4.5 %collective-permute-start = (f32[9,8,256]{2,1,0:T(8,128)S(1)}, f32[9,8,256]{2,1,0:T(8,128)S(1)}, u32[]{:S(2)}, u32[]{:S(2)}) collective-permute-start(f32[9,8,256]{2,1,0:T(8,128)S(1)} %get-tuple-element.33), channel_id=1, source_target_pairs={{0,1},{1,2},{2,3},{3,0},{4,5},{5,6},{6,7},{7,4},{8,9},{9,10},{10,1... | collective-permute-start | bytes 221192 | tf_op jit(solution)/shard_map/ppermute | solution.py:809
  3.9 4.6 %collective-permute-start.1 = (f32[9,8,256]{2,1,0:T(8,128)S(1)}, f32[9,8,256]{2,1,0:T(8,128)S(1)}, u32[]{:S(2)}, u32[]{:S(2)}) collective-permute-start(f32[9,8,256]{2,1,0:T(8,128)S(1)} %get-tuple-element.34), channel_id=1, source_target_pairs={{1,0},{2,1},{3,2},{0,3},{5,4},{6,5},{7,6},{4,7},{9,8},{10,9},{11,1... | collective-permute-start | bytes 221192 | tf_op jit(solution)/shard_map/ppermute | solution.py:810
  9.7 21.1 %all-to-all-start.1 = ((f32[32,8,128]{2,1,0:T(8,128)}), f32[32,8,128]{2,1,0:T(8,128)S(1)}, u32[]{:S(2)}, u32[]{:S(2)}) async-start(f32[32,8,128]{2,1,0:T(8,128)} %shard_map.41), calls=%async_computation.1 | async-start | bytes 262144 | tf_op jit(solution)/shard_map/all_to_all | solution.py:815
  16.0 11.3 %collective-permute-start.2 = (f32[10,16,256]{2,1,0:T(8,128)S(1)}, f32[10,16,256]{2,1,0:T(8,128)S(1)}, u32[]{:S(2)}, u32[]{:S(2)}) collective-permute-start(f32[10,16,256]{2,1,0:T(8,128)S(1)} %get-tuple-element.36), channel_id=1, source_target_pairs={{0,4},{4,8},{8,12},{12,16},{16,20},{20,24},{24,28},{28,0},{1,5},{5... | collective-permute-start | bytes 491528 | tf_op jit(solution)/shard_map/ppermute | solution.py:809
  17.9 10.5 %collective-permute-start.3 = (f32[10,16,256]{2,1,0:T(8,128)S(1)}, f32[10,16,256]{2,1,0:T(8,128)S(1)}, u32[]{:S(2)}, u32[]{:S(2)}) collective-permute-start(f32[10,16,256]{2,1,0:T(8,128)S(1)} %get-tuple-element.37), channel_id=1, source_target_pairs={{4,0},{8,4},{12,8},{16,12},{20,16},{24,20},{28,24},{0,28},{5,1},{9... | collective-permute-start | bytes 491528 | tf_op jit(solution)/shard_map/ppermute | solution.py:810
  30.8 17.9 %all-to-all-start = ((f32[32,2,8,128]{3,2,1,0:T(8,128)}), f32[32,2,8,128]{3,2,1,0:T(8,128)S(1)}, u32[]{:S(2)}, u32[]{:S(2)}) async-start(f32[32,2,8,128]{3,2,1,0:T(8,128)} %get-tuple-element.38), calls=%async_computation | async-start | bytes 524288 | tf_op jit(solution)/shard_map/all_to_all | solution.py:815
  34.6 3.6 %collective-permute-start.4 = (f32[8,8,128]{2,1,0:T(8,128)S(1)}, f32[8,8,128]{2,1,0:T(8,128)S(1)}, u32[]{:S(2)}, u32[]{:S(2)}) collective-permute-start(f32[8,8,128]{2,1,0:T(8,128)S(1)} %get-tuple-element.41), channel_id=1, source_target_pairs={{0,1},{1,2},{2,3},{3,0},{4,5},{5,6},{6,7},{7,4},{8,9},{9,10},{10,1... | collective-permute-start | bytes 98312 | tf_op jit(solution)/shard_map/ppermute | solution.py:809
  34.9 3.4 %collective-permute-start.5 = (f32[8,8,128]{2,1,0:T(8,128)S(1)}, f32[8,8,128]{2,1,0:T(8,128)S(1)}, u32[]{:S(2)}, u32[]{:S(2)}) collective-permute-start(f32[8,8,128]{2,1,0:T(8,128)S(1)} %get-tuple-element.42), channel_id=1, source_target_pairs={{1,0},{2,1},{3,2},{0,3},{5,4},{6,5},{7,6},{4,7},{9,8},{10,9},{11,1... | collective-permute-start | bytes 98312 | tf_op jit(solution)/shard_map/ppermute | solution.py:810
  38.3 9.7 %collective-permute-start.6 = (f32[18,8,128]{2,1,0:T(8,128)S(1)}, f32[18,8,128]{2,1,0:T(8,128)S(1)}, u32[]{:S(2)}, u32[]{:S(2)}) collective-permute-start(f32[18,8,128]{2,1,0:T(8,128)S(1)} %get-tuple-element.44), channel_id=1, source_target_pairs={{0,4},{4,8},{8,12},{12,16},{16,20},{20,24},{24,28},{28,0},{1,5},{5... | collective-permute-start | bytes 221192 | tf_op jit(solution)/shard_map/ppermute | solution.py:809
  40.1 7.9 %collective-permute-start.7 = (f32[18,8,128]{2,1,0:T(8,128)S(1)}, f32[18,8,128]{2,1,0:T(8,128)S(1)}, u32[]{:S(2)}, u32[]{:S(2)}) collective-permute-start(f32[18,8,128]{2,1,0:T(8,128)S(1)} %get-tuple-element.45), channel_id=1, source_target_pairs={{4,0},{8,4},{12,8},{16,12},{20,16},{24,20},{28,24},{0,28},{5,1},{9... | collective-permute-start | bytes 221192 | tf_op jit(solution)/shard_map/ppermute | solution.py:810
  47.3 0.7 %copy-start = (f32[5,8,16,128]{3,2,1,0:T(8,128)}, f32[5,8,16,128]{3,2,1,0:T(8,128)S(1)}, u32[]{:S(2)}) copy-start(f32[5,8,16,128]{3,2,1,0:T(8,128)S(1)} %get-tuple-element.52.rest_1_) | copy-start | bytes 983044
  48.0 0.6 %copy-start.5 = (f32[18,8,128]{2,1,0:T(8,128)}, f32[18,8,128]{2,1,0:T(8,128)S(1)}, u32[]{:S(2)}) copy-start(f32[18,8,128]{2,1,0:T(8,128)S(1)} %collective-permute-done.7.one_high) | copy-start | bytes 221188
  48.6 1.0 %copy-start.1 = (f32[5,8,16,128]{3,2,1,0:T(8,128)S(1)}, f32[5,8,16,128]{3,2,1,0:T(8,128)}, u32[]{:S(2)}) copy-start(f32[5,8,16,128]{3,2,1,0:T(8,128)} %copy-done) | copy-start | bytes 983044
  49.6 0.9 %copy-start.6 = (f32[18,8,128]{2,1,0:T(8,128)S(1)}, f32[18,8,128]{2,1,0:T(8,128)}, u32[]{:S(2)}) copy-start(f32[18,8,128]{2,1,0:T(8,128)} %copy-done.5) | copy-start | bytes 221188
where the time goes:
time: 54.8 us; the launch traced here: 54.3 us
  starting transfers between devices  25.1 us (46%)
  waiting for transfers between devices  12 us (22%)
  Pallas kernels  11.3 us (21%)
  local copies, waits for them, and re-layouts  5.91 us (11%)
    pallas_call x7, Pallas kernels, call(): pl.pallas_call(kernel, in_specs=[spec] * len(operands), out_specs=[VM] *...  11.3 us
    ppermute x4, starting transfers between devices, exchange(): lax.ppermute(to_low, axis, [((i + 1) % count, i) for i in range(count)])  10.4 us
    ppermute x4, waiting for transfers between devices, exchange(): lax.ppermute(to_high, axis, [(i, (i + 1) % count) for i in range(count)])  10.4 us
    all_to_all x2, starting transfers between devices, to_everyone(): return lax.all_to_all(blocks, ('tx', 'ty'), 0, 0)  10.1 us
    unnamed x14, local copies, waits for them, and re-layouts  5.91 us
    ppermute x4, starting transfers between devices, exchange(): lax.ppermute(to_high, axis, [(i, (i + 1) % count) for i in range(count)])  4.53 us
    ppermute x4, waiting for transfers between devices, exchange(): lax.ppermute(to_low, axis, [((i + 1) % count, i) for i in range(count)])  1.63 us
  transfers between devices with their start and end apart: 10, of which 5 were waited for; matrix products, arithmetic and copies ran while one was open for 0% of the time, Pallas kernels for 10%

commit v1 on v0

--- a/solution.py
+++ b/solution.py
@@ -36,6 +36,20 @@
     def __getitem__(self, x):
         ref, index = self.planes[x - self.first]
         return ref[index]
+
+    def __setitem__(self, x, value):
+        ref, index = self.planes[x - self.first]
+        ref[index] = value
+
+
+def kept(ref, first, before=None, after=None):
+    planes = [(ref, x) for x in range(ref.shape[0])]
+    if before is not None:
+        planes = [before] + planes
+        first -= 1
+    if after is not None:
+        planes = planes + [after]
+    return Planes(first, planes)
 
 
 def iota(shape, dim):
@@ -196,24 +210,25 @@
             jnp.concatenate(stack, 0), halve_lanes(LANES, size_z1, chunk * LANES // 2)
         )
         k_one = part if k_one is None else k_one + part
-    pieces = []
+    assert tile_x1 // 2 * (size_z1 // 2) <= LANES
+    block = None
     for pair in range(tile_x1 // 2):
         at = 2 * pair * tile_y1
         paired_one[...] = k_one[at : at + tile_y1] + k_one[at + tile_y1 : at + 2 * tile_y1]
-        pieces.append(
+        piece = (
             paired_one[pl.ds(0, tile_y1 // 2, stride=2)] + paired_one[pl.ds(1, tile_y1 // 2, stride=2)]
         )
-    shape = (size_z1, LANES)
-    twice = ones_where(div(iota(shape, 0), 2) == mod(iota(shape, 1), size_z1 // 2))
-    block = (0.125 * 0.125) * times_right(jnp.concatenate(pieces, 0), twice)
+        part = times_right(piece, halve_lanes(size_z1, LANES, pair * size_z1 // 2))
+        block = part if block is None else block + part
+    block = (0.125 * 0.125) * block
     for device in range(blocks.shape[0]):
         blocks[device] = block
 
 
 def fine_down(
     window, from_low, from_high,
-    v_out, forcing_out, cx, cy, cz, weight, level_one, blocks, to_low, to_high,
-    conc_rim, forcing_rim, kappa_rim, once, diag, paired,
+    v_zero, forcing_out, cx, cy, cz, weight, level_one, blocks, to_low, to_high,
+    conc_rim, forcing_rim, kappa_rim, once, diag, paired, outer,
     k_one, f_one, u_one, v_one, cx1, cy1, cz1, w1, d1, paired_one, packed,
 ):
     _, tile_x, rows, size_z = window.shape
@@ -249,11 +264,16 @@
         return Planes(RX - depth, whole)
 
     conc, forcing, kappa = stacked(0), stacked(1), stacked(2)
+    cx = kept(cx, RX - 2, (outer, 0), (outer, 1))
+    cy = kept(cy, RX - 1, (outer, 2), (outer, 3))
+    cz = kept(cz, RX - 1, (outer, 4), (outer, 5))
+    weight = kept(weight, RX - 1, (outer, 6), (outer, 7))
+    v_out = kept(v_zero, RX - 1)
     plane_setup(kappa, cx, cy, cz, weight, diag, 1.0, 1, planes - 1)
     plane_sweep(conc, once, forcing, cx, cy, cz, weight, 1, planes - 1)
     plane_sweep(once, v_out, forcing, cx, cy, cz, weight, 2, planes - 2)
     for x in range(RX - 1, planes - RX + 1):
-        forcing_out[x] = forcing[x]
+        forcing_out[x - RX + 1] = forcing[x]
     chunks = size_z // LANES
     size_z1 = size_z // 2
     to_half = [halve_lanes(LANES, size_z1, chunk * LANES // 2) for chunk in range(chunks)]
@@ -353,7 +373,7 @@
                 ]
         start = 3 * tile_x1 * R1 // ROWS
         for x in range(tile_x):
-            row = v_out[RX + x, row0 : row0 + 1]
+            row = v_zero[x + 1, row0 : row0 + 1]
             for chunk in range(chunks):
                 to[start + chunk, x : x + 1] = row[:, chunk * LANES : (chunk + 1) * LANES]
 
@@ -395,7 +415,7 @@
                             source, x, row : row + 1
                         ]
                         loose += 1
-        second, first = (RX + 1, RX) if low else (planes - RX - 2, planes - RX - 1)
+        second, first = (2, 1) if low else (planes - 3, planes - 2)
         for row in (RY - 1, top):
             for chunk in range(chunks):
                 lanes = slice(chunk * LANES, (chunk + 1) * LANES)
@@ -587,19 +607,19 @@
     count_x, count_y = counts
     planes, rows, _ = grids[0].sizes
     half_x, half_y = planes // count_x, rows // count_y
-    assert half_x * half_y == ROWS and ROWS % half_y == 0
-    sub = iota((ROWS, LANES), 0)
-    kappa = [[jnp.ones((ROWS, LANES), F32)] * (rows // ROWS) for _ in range(planes)]
+    size_z2 = grids[0].sizes[2]
+    assert half_x * size_z2 == LANES and half_x == 2 and ROWS % half_y == 0
+    share = ROWS // half_y
+    kappa = [[None] * (rows // ROWS) for _ in range(planes)]
+    lane = iota((ROWS, LANES), 1)
     for tx in range(count_x):
-        for ty in range(count_y):
-            piece = blocks[tx * count_y + ty]
+        for group in range(rows // ROWS):
+            pieces = [blocks[tx * count_y + group * share + n] for n in range(share)]
+            piece = jnp.concatenate(pieces, 0)
+            turned = pltpu.roll(piece, size_z2, 1)
             for p in range(half_x):
-                x, start = tx * half_x + p, ty * half_y
-                group, offset = start // ROWS, start % ROWS
-                shift = (offset - p * half_y) % ROWS
-                moved = pltpu.roll(piece, shift, 0) if shift else piece
-                mine = (sub >= offset) & (sub < offset + half_y)
-                kappa[x][group] = jnp.where(mine, moved, kappa[x][group])
+                mine = (lane < size_z2) == (p == 0)
+                kappa[tx * half_x + p][group] = jnp.where(mine, piece, turned)
     kappa = jnp.concatenate([jnp.concatenate(groups, 0)[None] for groups in kappa], 0)
     kappas = [kappa]
     for grid in grids[:-1]:
@@ -737,7 +757,9 @@
     plane_sweep(one_a, one_b, forcing1, cx1, cy1, cz1, w1, 2, planes1 - 2)
     plane_sweep(one_b, one_a, forcing1, cx1, cy1, cz1, w1, 3, planes1 - 3)
 
-    planes, rows, size_z = v_zero.shape
+    planes, rows, size_z = zero_a.shape
+    v_zero, forcing0 = kept(v_zero, RX - 1), kept(forcing0, RX - 1)
+    cx, cy, cz, weight = kept(cx, RX - 2), kept(cy, RX - 1), kept(cz, RX - 1), kept(weight, RX - 1)
     first, last = R1 - 1, planes1 - R1 + 1
     stack = jnp.concatenate([one_a[x] for x in range(first, last)], 0)
     count = last - first
@@ -824,7 +846,10 @@
     message = (tile_x + 1, ROWS, size_z)
     *inputs, to_low, to_high = call(
         edges,
-        (concentration, source, material),
+        tuple(
+            pltpu.with_memory_space_constraint(v, pltpu.HBM)
+            for v in (concentration, source, material)
+        ),
         tuple(jax.ShapeDtypeStruct(v.shape, v.dtype) for v in (concentration, source, material))
         + (message, message),
         (pltpu.SemaphoreType.DMA((3,)),),
@@ -838,13 +863,14 @@
     from_low, from_high = exchange(to_low, to_high, "tx")
 
     zero = (tile_x + 2 * RX, rows, size_z)
+    inner = (tile_x + 2, rows, size_z)
     one_tile = (tile_x // 2, tile_y // 2, size_z // 2)
     two_tile = tuple(extent // 2 for extent in one_tile)
     grids = levels_of(counts, two_tile)
     (kappa_blocks,) = call(
         shrink,
         (window,),
-        ((everyone, two_tile[0] * two_tile[1], LANES),),
+        ((everyone, two_tile[1], LANES),),
         ((one_tile[0], rows, LANES), one_tile[1:]),
     )
     kappa_blocks = to_everyone(kappa_blocks)
@@ -857,7 +883,7 @@
     v_zero, forcing0, cx, cy, cz, weight, level_one, blocks, to_low, to_high = call(
         fine_down,
         (window, from_low, from_high),
-        (zero,) * 6
+        (inner, inner, (tile_x + 3, rows, size_z), inner, inner, inner)
         + ((3,) + one_tile, (everyone, pairs1 // 2, ROWS, LANES), message, message),
         (
             (6, rows, size_z),
@@ -866,6 +892,7 @@
             zero,
             zero,
             (chunks, max(small[0], tile_x), 2 * wide, LANES),
+            (8, rows, size_z),
         )
         + (small,) * 9
         + ((pairs1, wide, one_tile[2]), (pairs1, ROWS, one_tile[2])),

time: 54.8 us -> 42.9 us (0.78)
  local copies, waits for them, and re-layouts: 5.91 us -> 0 us
  starting transfers between devices: 25.1 us -> 21.1 us
  waiting for transfers between devices: 12 us -> 9.26 us
  Pallas kernels: 11.3 us -> 12.1 us
    ppermute x4, waiting for transfers between devices: 10.4 us -> 3.71 us  [exchange(): lax.ppermute(to_high, axis, [(i, (i + 1) % count) for i in range(count)])]
    unnamed x14 -> x0, local copies, waits for them, and re-layouts: 5.91 us -> none
    all_to_all x2, starting transfers between devices: 10.1 us -> 5.84 us  [to_everyone(): return lax.all_to_all(blocks, ('tx', 'ty'), 0, 0)]
    all_to_all x2, waiting for transfers between devices: 0.01 us -> 2.17 us  [to_everyone(): return lax.all_to_all(blocks, ('tx', 'ty'), 0, 0)]
    ppermute x4, waiting for transfers between devices: 1.63 us -> 3.38 us  [exchange(): lax.ppermute(to_low, axis, [((i + 1) % count, i) for i in range(count)])]
    pallas_call x7, Pallas kernels: 11.3 us -> 12.1 us  [call(): pl.pallas_call(kernel, in_specs=[spec] * len(operands), out_specs=[VM] *...]
    ppermute x4, starting transfers between devices: 10.4 us -> 10.9 us  [exchange(): lax.ppermute(to_low, axis, [((i + 1) % count, i) for i in range(count)])]
  transfers between devices with their start and end apart: 10 -> 10, of which waited for: 5 -> 5; matrix products, arithmetic and copies ran while one was open for 0% -> 0% of each run, Pallas kernels for 10% -> 16%
where the time goes in v1:
time: 42.9 us; the launch traced here: 42.6 us
  starting transfers between devices  21.1 us (49%)
  Pallas kernels  12.1 us (28%)
  waiting for transfers between devices  9.26 us (22%)
    pallas_call x7, Pallas kernels, call(): pl.pallas_call(kernel, in_specs=[spec] * len(operands), out_specs=[VM] *...  12.1 us
    ppermute x4, starting transfers between devices, exchange(): lax.ppermute(to_low, axis, [((i + 1) % count, i) for i in range(count)])  10.9 us
    all_to_all x2, starting transfers between devices, to_everyone(): return lax.all_to_all(blocks, ('tx', 'ty'), 0, 0)  5.84 us
    ppermute x4, starting transfers between devices, exchange(): lax.ppermute(to_high, axis, [(i, (i + 1) % count) for i in range(count)])  4.32 us
    ppermute x4, waiting for transfers between devices, exchange(): lax.ppermute(to_high, axis, [(i, (i + 1) % count) for i in range(count)])  3.71 us
    ppermute x4, waiting for transfers between devices, exchange(): lax.ppermute(to_low, axis, [((i + 1) % count, i) for i in range(count)])  3.38 us
    all_to_all x2, waiting for transfers between devices, to_everyone(): return lax.all_to_all(blocks, ('tx', 'ty'), 0, 0)  2.17 us
  transfers between devices with their start and end apart: 10, of which 5 were waited for; matrix products, arithmetic and copies ran while one was open for 0% of the time, Pallas kernels for 16%

profile of v1, /device:TPU:0, one launch (start us, length us, event | category | flops | bytes accessed | tf_op | source)
XLA Modules:
  0.0 42.6 jit_solution(16544227957886772356)
XLA Ops:
  0.0 1.2 %shard_map.37 = (f32[8,16,256]{2,1,0:T(8,128)S(1)}, f32[8,16,256]{2,1,0:T(8,128)S(1)}, s32[8,16,256]{2,1,0:T(8,128)S(1)}, f32[9,8,256]{2,1,0:T(8,128)S(1)}, f32[9,8,256]{2,1,0:T(8,128)S(1)}) custom-call(f32[8,16,256]{2,1,0:T(8,128)} %conc_in.1, f32[8,16,256]{2,1,0:T(8,128)} %source_in.1, s32[8,16,256]{2,1,0:T(8,128)} %material_in.1), custom_call_target="tpu_custom_call" | custom-call | tf_op jit(solution)/shard_map/pallas_call | solution.py:819
  1.2 0.5 %collective-permute-start = (f32[9,8,256]{2,1,0:T(8,128)S(1)}, f32[9,8,256]{2,1,0:T(8,128)S(1)}, u32[]{:S(2)}, u32[]{:S(2)}) collective-permute-start(f32[9,8,256]{2,1,0:T(8,128)S(1)} %get-tuple-element.33), channel_id=1, source_target_pairs={{0,1},{1,2},{2,3},{3,0},{4,5},{5,6},{6,7},{7,4},{8,9},{9,10},{10,1... | collective-permute-start | bytes 221192 | tf_op jit(solution)/shard_map/ppermute | solution.py:831
  1.7 2.0 %collective-permute-start.1 = (f32[9,8,256]{2,1,0:T(8,128)S(1)}, f32[9,8,256]{2,1,0:T(8,128)S(1)}, u32[]{:S(2)}, u32[]{:S(2)}) collective-permute-start(f32[9,8,256]{2,1,0:T(8,128)S(1)} %get-tuple-element.34), channel_id=1, source_target_pairs={{1,0},{2,1},{3,2},{0,3},{5,4},{6,5},{7,6},{4,7},{9,8},{10,9},{11,1... | collective-permute-start | bytes 221192 | tf_op jit(solution)/shard_map/ppermute | solution.py:832
  3.7 2.0 %collective-permute-done.from_low = f32[9,8,256]{2,1,0:T(8,128)S(1)} collective-permute-done((f32[9,8,256]{2,1,0:T(8,128)S(1)}, f32[9,8,256]{2,1,0:T(8,128)S(1)}, u32[]{:S(2)}, u32[]{:S(2)}) %collective-permute-start) | collective-permute-done | bytes 73760 | tf_op jit(solution)/shard_map/ppermute | solution.py:831
  5.7 0.6 %collective-permute-done.1.from_high = f32[9,8,256]{2,1,0:T(8,128)S(1)} collective-permute-done((f32[9,8,256]{2,1,0:T(8,128)S(1)}, f32[9,8,256]{2,1,0:T(8,128)S(1)}, u32[]{:S(2)}, u32[]{:S(2)}) %collective-permute-start.1) | collective-permute-done | bytes 73760 | tf_op jit(solution)/shard_map/ppermute | solution.py:832
  6.3 0.2 shard_map.38
  6.5 1.8 %collective-permute-start.2 = (f32[10,16,256]{2,1,0:T(8,128)S(1)}, f32[10,16,256]{2,1,0:T(8,128)S(1)}, u32[]{:S(2)}, u32[]{:S(2)}) collective-permute-start(f32[10,16,256]{2,1,0:T(8,128)S(1)} %get-tuple-element.36), channel_id=1, source_target_pairs={{0,4},{4,8},{8,12},{12,16},{16,20},{20,24},{24,28},{28,0},{1,5},{5... | collective-permute-start | bytes 491528 | tf_op jit(solution)/shard_map/ppermute | solution.py:831
  8.3 3.1 %collective-permute-start.3 = (f32[10,16,256]{2,1,0:T(8,128)S(1)}, f32[10,16,256]{2,1,0:T(8,128)S(1)}, u32[]{:S(2)}, u32[]{:S(2)}) collective-permute-start(f32[10,16,256]{2,1,0:T(8,128)S(1)} %get-tuple-element.37), channel_id=1, source_target_pairs={{4,0},{8,4},{12,8},{16,12},{20,16},{24,20},{28,24},{0,28},{5,1},{9... | collective-permute-start | bytes 491528 | tf_op jit(solution)/shard_map/ppermute | solution.py:832
  11.4 1.1 %shard_map.41 = f32[32,4,128]{2,1,0:T(4,128)} custom-call(f32[3,8,24,256]{3,2,1,0:T(8,128)S(1)} %get-tuple-element.35.window), custom_call_target="tpu_custom_call" | custom-call | tf_op jit(solution)/shard_map/pallas_call | solution.py:819
  12.5 3.3 %all-to-all-start.1 = ((f32[32,4,128]{2,1,0:T(4,128)}), f32[32,4,128]{2,1,0:T(4,128)S(1)}, u32[]{:S(2)}, u32[]{:S(2)}) async-start(f32[32,4,128]{2,1,0:T(4,128)} %shard_map.41), calls=%async_computation.1 | async-start | bytes 131072 | tf_op jit(solution)/shard_map/all_to_all | solution.py:837
  15.7 0.0 collective-permute-done.2.from_low
  15.7 2.8 %collective-permute-done.3.from_high = f32[10,16,256]{2,1,0:T(8,128)S(1)} collective-permute-done((f32[10,16,256]{2,1,0:T(8,128)S(1)}, f32[10,16,256]{2,1,0:T(8,128)S(1)}, u32[]{:S(2)}, u32[]{:S(2)}) %collective-permute-start.3) | collective-permute-done | bytes 163872 | tf_op jit(solution)/shard_map/ppermute | solution.py:832
  18.5 2.5 %shard_map.39 = (f32[10,24,256]{2,1,0:T(8,128)S(1)}, f32[10,24,256]{2,1,0:T(8,128)S(1)}, f32[11,24,256]{2,1,0:T(8,128)S(1)}, f32[10,24,256]{2,1,0:T(8,128)S(1)},...) custom-call(f32[3,8,24,256]{3,2,1,0:T(8,128)S(1)} %get-tuple-element, ...), custom_call_target="tpu_custom_call" | custom-call | tf_op jit(solution)/shard_map/pallas_call | solution.py:819
  21.0 2.2 %all-to-all-done.1.blocks = f32[32,4,128]{2,1,0:T(4,128)S(1)} async-done(((f32[32,4,128]{2,1,0:T(4,128)}), f32[32,4,128]{2,1,0:T(4,128)S(1)}, u32[]{:S(2)}, u32[]{:S(2)}) %all-to-all-start.1) | async-done | bytes 65568 | tf_op jit(solution)/shard_map/all_to_all | solution.py:837
  23.1 2.6 %all-to-all-start = ((f32[32,2,8,128]{3,2,1,0:T(8,128)}), f32[32,2,8,128]{3,2,1,0:T(8,128)S(1)}, u32[]{:S(2)}, u32[]{:S(2)}) async-start(f32[32,2,8,128]{3,2,1,0:T(8,128)} %get-tuple-element.38), calls=%async_computation | async-start | bytes 524288 | tf_op jit(solution)/shard_map/all_to_all | solution.py:837
  25.7 0.2 collective-permute-start.4
  25.9 1.6 %collective-permute-start.5 = (f32[8,8,128]{2,1,0:T(8,128)S(1)}, f32[8,8,128]{2,1,0:T(8,128)S(1)}, u32[]{:S(2)}, u32[]{:S(2)}) collective-permute-start(f32[8,8,128]{2,1,0:T(8,128)S(1)} %get-tuple-element.42), channel_id=1, source_target_pairs={{1,0},{2,1},{3,2},{0,3},{5,4},{6,5},{7,6},{4,7},{9,8},{10,9},{11,1... | collective-permute-start | bytes 98312 | tf_op jit(solution)/shard_map/ppermute | solution.py:832
  27.5 1.7 %collective-permute-done.4.from_low.row_low = f32[8,8,128]{2,1,0:T(8,128)S(1)} collective-permute-done((f32[8,8,128]{2,1,0:T(8,128)S(1)}, f32[8,8,128]{2,1,0:T(8,128)S(1)}, u32[]{:S(2)}, u32[]{:S(2)}) %collective-permute-start.4) | collective-permute-done | bytes 32800 | tf_op jit(solution)/shard_map/ppermute | solution.py:831
  29.3 0.0 collective-permute-done.5.from_high.row_high
  29.3 1.8 %collective-permute-start.6 = (f32[18,8,128]{2,1,0:T(8,128)S(1)}, f32[18,8,128]{2,1,0:T(8,128)S(1)}, u32[]{:S(2)}, u32[]{:S(2)}) collective-permute-start(f32[18,8,128]{2,1,0:T(8,128)S(1)} %get-tuple-element.44), channel_id=1, source_target_pairs={{0,4},{4,8},{8,12},{12,16},{16,20},{20,24},{24,28},{28,0},{1,5},{5... | collective-permute-start | bytes 221192 | tf_op jit(solution)/shard_map/ppermute | solution.py:831
  31.1 4.2 %collective-permute-start.7 = (f32[18,8,128]{2,1,0:T(8,128)S(1)}, f32[18,8,128]{2,1,0:T(8,128)S(1)}, u32[]{:S(2)}, u32[]{:S(2)}) collective-permute-start(f32[18,8,128]{2,1,0:T(8,128)S(1)} %get-tuple-element.45), channel_id=1, source_target_pairs={{4,0},{8,4},{12,8},{16,12},{20,16},{24,20},{28,24},{0,28},{5,1},{9... | collective-permute-start | bytes 221192 | tf_op jit(solution)/shard_map/ppermute | solution.py:832
  35.4 3.2 %shard_map.42 = (f32[5,16,16,128]{3,2,1,0:T(8,128)S(1)}, f32[5,8,16,128]{3,2,1,0:T(8,128)S(1)}, f32[5,4,16,128]{3,2,1,0:T(8,128)S(1)}, f32[32,128]{1,0:T(8,128)S(1)}) custom-call(f32[32,4,128]{2,1,0:T(4,128)S(1)} %all-to-all-done.1.blocks, f32[3,4,16,128]{3,2,1,0:T(8,128)S(1)} %get-tuple-element.43._.window_one), custom_call_target="tpu_custom_call" | custom-call | tf_op jit(solution)/shard_map/pallas_call | solution.py:819
  38.6 0.0 collective-permute-done.6.one_low
  38.6 0.0 collective-permute-done.7.one_high
  38.7 0.0 all-to-all-done.blocks
  38.7 3.9 %shard_map.43 = f32[8,16,256]{2,1,0:T(8,128)} custom-call(f32[32,2,8,128]{3,2,1,0:T(8,128)S(1)} %all-to-all-done.blocks, f32[3,4,16,128]{3,2,1,0:T(8,128)S(1)} %get-tuple-element.43._.window_one, f32[18,8,128]{2,1,0:T(8,128)S(1)} %collective-permute-done.6.one_low, f32[18,8,128]{2,1,0:T(8,128)S(1)} %collective-permute-done.7.one_high, ...), custom_call_target="tpu_custom_call" | custom-call | tf_op jit(solution)/shard_map/pallas_call | solution.py:819
  (1 shorter events, 0.0 us)
Async XLA Ops:
  1.2 4.5 %collective-permute-start = (f32[9,8,256]{2,1,0:T(8,128)S(1)}, f32[9,8,256]{2,1,0:T(8,128)S(1)}, u32[]{:S(2)}, u32[]{:S(2)}) collective-permute-start(f32[9,8,256]{2,1,0:T(8,128)S(1)} %get-tuple-element.33), channel_id=1, source_target_pairs={{0,1},{1,2},{2,3},{3,0},{4,5},{5,6},{6,7},{7,4},{8,9},{9,10},{10,1... | collective-permute-start | bytes 221192 | tf_op jit(solution)/shard_map/ppermute | solution.py:831
  1.7 4.6 %collective-permute-start.1 = (f32[9,8,256]{2,1,0:T(8,128)S(1)}, f32[9,8,256]{2,1,0:T(8,128)S(1)}, u32[]{:S(2)}, u32[]{:S(2)}) collective-permute-start(f32[9,8,256]{2,1,0:T(8,128)S(1)} %get-tuple-element.34), channel_id=1, source_target_pairs={{1,0},{2,1},{3,2},{0,3},{5,4},{6,5},{7,6},{4,7},{9,8},{10,9},{11,1... | collective-permute-start | bytes 221192 | tf_op jit(solution)/shard_map/ppermute | solution.py:832
  6.5 9.2 %collective-permute-start.2 = (f32[10,16,256]{2,1,0:T(8,128)S(1)}, f32[10,16,256]{2,1,0:T(8,128)S(1)}, u32[]{:S(2)}, u32[]{:S(2)}) collective-permute-start(f32[10,16,256]{2,1,0:T(8,128)S(1)} %get-tuple-element.36), channel_id=1, source_target_pairs={{0,4},{4,8},{8,12},{12,16},{16,20},{20,24},{24,28},{28,0},{1,5},{5... | collective-permute-start | bytes 491528 | tf_op jit(solution)/shard_map/ppermute | solution.py:831
  8.3 10.2 %collective-permute-start.3 = (f32[10,16,256]{2,1,0:T(8,128)S(1)}, f32[10,16,256]{2,1,0:T(8,128)S(1)}, u32[]{:S(2)}, u32[]{:S(2)}) collective-permute-start(f32[10,16,256]{2,1,0:T(8,128)S(1)} %get-tuple-element.37), channel_id=1, source_target_pairs={{4,0},{8,4},{12,8},{16,12},{20,16},{24,20},{28,24},{0,28},{5,1},{9... | collective-permute-start | bytes 491528 | tf_op jit(solution)/shard_map/ppermute | solution.py:832
  12.5 10.7 %all-to-all-start.1 = ((f32[32,4,128]{2,1,0:T(4,128)}), f32[32,4,128]{2,1,0:T(4,128)S(1)}, u32[]{:S(2)}, u32[]{:S(2)}) async-start(f32[32,4,128]{2,1,0:T(4,128)} %shard_map.41), calls=%async_computation.1 | async-start | bytes 131072 | tf_op jit(solution)/shard_map/all_to_all | solution.py:837
  23.1 15.5 %all-to-all-start = ((f32[32,2,8,128]{3,2,1,0:T(8,128)}), f32[32,2,8,128]{3,2,1,0:T(8,128)S(1)}, u32[]{:S(2)}, u32[]{:S(2)}) async-start(f32[32,2,8,128]{3,2,1,0:T(8,128)} %get-tuple-element.38), calls=%async_computation | async-start | bytes 524288 | tf_op jit(solution)/shard_map/all_to_all | solution.py:837
  25.7 3.5 %collective-permute-start.4 = (f32[8,8,128]{2,1,0:T(8,128)S(1)}, f32[8,8,128]{2,1,0:T(8,128)S(1)}, u32[]{:S(2)}, u32[]{:S(2)}) collective-permute-start(f32[8,8,128]{2,1,0:T(8,128)S(1)} %get-tuple-element.41), channel_id=1, source_target_pairs={{0,1},{1,2},{2,3},{3,0},{4,5},{5,6},{6,7},{7,4},{8,9},{9,10},{10,1... | collective-permute-start | bytes 98312 | tf_op jit(solution)/shard_map/ppermute | solution.py:831
  25.9 3.4 %collective-permute-start.5 = (f32[8,8,128]{2,1,0:T(8,128)S(1)}, f32[8,8,128]{2,1,0:T(8,128)S(1)}, u32[]{:S(2)}, u32[]{:S(2)}) collective-permute-start(f32[8,8,128]{2,1,0:T(8,128)S(1)} %get-tuple-element.42), channel_id=1, source_target_pairs={{1,0},{2,1},{3,2},{0,3},{5,4},{6,5},{7,6},{4,7},{9,8},{10,9},{11,1... | collective-permute-start | bytes 98312 | tf_op jit(solution)/shard_map/ppermute | solution.py:832
  29.3 9.3 %collective-permute-start.6 = (f32[18,8,128]{2,1,0:T(8,128)S(1)}, f32[18,8,128]{2,1,0:T(8,128)S(1)}, u32[]{:S(2)}, u32[]{:S(2)}) collective-permute-start(f32[18,8,128]{2,1,0:T(8,128)S(1)} %get-tuple-element.44), channel_id=1, source_target_pairs={{0,4},{4,8},{8,12},{12,16},{16,20},{20,24},{24,28},{28,0},{1,5},{5... | collective-permute-start | bytes 221192 | tf_op jit(solution)/shard_map/ppermute | solution.py:831
  31.1 7.5 %collective-permute-start.7 = (f32[18,8,128]{2,1,0:T(8,128)S(1)}, f32[18,8,128]{2,1,0:T(8,128)S(1)}, u32[]{:S(2)}, u32[]{:S(2)}) collective-permute-start(f32[18,8,128]{2,1,0:T(8,128)S(1)} %get-tuple-element.45), channel_id=1, source_target_pairs={{4,0},{8,4},{12,8},{16,12},{20,16},{24,20},{28,24},{0,28},{5,1},{9... | collective-permute-start | bytes 221192 | tf_op jit(solution)/shard_map/ppermute | solution.py:832

commit v2 on v1

--- a/solution.py
+++ b/solution.py
@@ -13,6 +13,7 @@
 diffusivities = (0.15, 0.3, 0.5, 0.8, 1.2, 2.0, 3.2, 5.0)
 LANES = 128
 ROWS = 8
+SHORT = 4
 RX = 3
 RY = 4
 R1 = 4
@@ -50,6 +51,37 @@
     if after is not None:
         planes = planes + [after]
     return Planes(first, planes)
+
+
+def is_even(axis):
+    return lax.rem(lax.axis_index(axis), 2) == 0
+
+
+def on_sides(axis, near, far, body):
+    @pl.when(is_even(axis))
+    def _():
+        body(far, near)
+
+    @pl.when(jnp.logical_not(is_even(axis)))
+    def _():
+        body(near, far)
+
+
+class Picked:
+    def __init__(self, flag, when_true, when_false):
+        self.flag = flag
+        self.when_true = when_true
+        self.when_false = when_false
+
+    def __getitem__(self, index):
+        first, second = self.when_true[index], self.when_false[index]
+        flag = jnp.where(self.flag, jnp.int32(1), jnp.int32(0))
+        return jnp.where(jnp.full(first.shape, flag) == 1, first, second)
+
+
+def by_side(axis, near, far):
+    even = is_even(axis)
+    return Picked(even, far, near), Picked(even, near, far)
 
 
 def iota(shape, dim):
@@ -131,7 +163,7 @@
         out[x] = (1.0 - relax_weight) * v[x] + weight[x] * (forcing[x] + neighbours(v, cx, cy, cz, x))
 
 
-def edges(conc_in, source_in, material_in, conc, source, material, to_low, to_high, arrived):
+def edges(conc_in, source_in, material_in, conc, source, material, near, far, arrived):
     copies = [
         pltpu.make_async_copy(whence, whither, arrived.at[n])
         for n, (whence, whither) in enumerate(
@@ -143,21 +175,26 @@
     for copy in copies:
         copy.wait()
     tile_x, tile_y, _ = conc.shape
-    for to, low in ((to_low, True), (to_high, False)):
-        for x in range(tile_x):
-            rows = slice(0, 4) if low else slice(tile_y - 4, tile_y)
-            near = slice(0, 3) if low else slice(1, 4)
-            pair = slice(0, 2) if low else slice(2, 4)
-            c = conc[x, rows]
-            f = mass_rate * c + source[x, rows]
-            k = lookup(material[x, rows])
-            to[x, 0:3] = c[near]
-            to[x, 3:5] = f[pair]
-            to[x, 5:8] = k[near]
-            to[tile_x, x : x + 1] = k[3:4] if low else k[0:1]
-
-
-def sides(conc, source, material, from_low, from_high, window, to_low, to_high):
+
+    def pack(to_low, to_high):
+        for to, low in ((to_low, True), (to_high, False)):
+            for x in range(tile_x):
+                rows = slice(0, 4) if low else slice(tile_y - 4, tile_y)
+                near = slice(0, 3) if low else slice(1, 4)
+                pair = slice(0, 2) if low else slice(2, 4)
+                c = conc[x, rows]
+                f = mass_rate * c + source[x, rows]
+                k = lookup(material[x, rows])
+                to[x, 0:3] = c[near]
+                to[x, 3:5] = f[pair]
+                to[x, 5:8] = k[near]
+                to[tile_x, x : x + 1] = k[3:4] if low else k[0:1]
+
+    on_sides("ty", near, far, pack)
+
+
+def sides(conc, source, material, from_near, from_far, window, near, far):
+    from_low, from_high = by_side("ty", from_near, from_far)
     tile_x, tile_y, size_z = conc.shape
     top = RY + tile_y
     for x in range(tile_x):
@@ -177,15 +214,20 @@
         window[2, x, 1:4] = from_low[x, 5:8]
         window[2, x, top : top + 3] = from_high[x, 5:8]
         window[2, x, top + 3 :] = from_high[tile_x, x : x + 1]
-    for to, plane in ((to_low, lambda l: l - 1), (to_high, lambda l: tile_x - l)):
-        for at, (which, layer) in enumerate(BASE_PLANES):
-            to[at] = window[which, plane(layer), RY:top]
-        at = 0
-        for which, layer, reach in EXTRA_ROWS:
-            to[len(BASE_PLANES), at : at + reach] = window[which, plane(layer), RY - reach : RY]
-            at += reach
-            to[len(BASE_PLANES), at : at + reach] = window[which, plane(layer), top : top + reach]
-            at += reach
+
+    def pack(to_low, to_high):
+        for to, plane in ((to_low, lambda l: l - 1), (to_high, lambda l: tile_x - l)):
+            for at, (which, layer) in enumerate(BASE_PLANES):
+                to[at] = window[which, plane(layer), RY:top]
+            at = 0
+            for which, layer, reach in EXTRA_ROWS:
+                for start in (RY - reach, top):
+                    to[len(BASE_PLANES), at : at + reach] = window[
+                        which, plane(layer), start : start + reach
+                    ]
+                    at += reach
+
+    on_sides("tx", near, far, pack)
 
 
 BASE_PLANES = (
@@ -226,11 +268,12 @@
 
 
 def fine_down(
-    window, from_low, from_high,
-    v_zero, forcing_out, cx, cy, cz, weight, level_one, blocks, to_low, to_high,
+    window, from_near, from_far,
+    v_zero, forcing_out, cx, cy, cz, weight, level_one, blocks, near, far,
     conc_rim, forcing_rim, kappa_rim, once, diag, paired, outer,
     k_one, f_one, u_one, v_one, cx1, cy1, cz1, w1, d1, paired_one, packed,
 ):
+    from_low, from_high = by_side("tx", from_near, from_far)
     _, tile_x, rows, size_z = window.shape
     tile_y = rows - 2 * RY
     top = RY + tile_y
@@ -356,33 +399,40 @@
         jnp.concatenate([packed[half_pairs + p] for p in range(half_pairs)], 0),
         halve_lanes(size_z1, size_z1, size_z1 // 2),
     )
-    for p in range(half_pairs):
-        block = 0.125 * result[p * ROWS : (p + 1) * ROWS]
+    used = tile_y1 // 2 + RC
+    block = jnp.concatenate([result[p * ROWS : p * ROWS + used] for p in range(half_pairs)], 0)
+    block = 0.125 * block
+    for part in range(blocks.shape[1]):
+        piece = block[part * SHORT : (part + 1) * SHORT]
         for device in range(blocks.shape[0]):
-            blocks[device, p] = block
-
-    for to, rows1, row0 in (
-        (to_low, slice(0, R1), RY + 1),
-        (to_high, slice(tile_y1 - R1, tile_y1), top - 2),
-    ):
-        for which in range(3):
-            for x in range(tile_x1):
-                flat_row = which * tile_x1 * R1 + x * R1
-                to[flat_row // ROWS, flat_row % ROWS : flat_row % ROWS + R1] = level_one[
-                    which, x, rows1
-                ]
-        start = 3 * tile_x1 * R1 // ROWS
-        for x in range(tile_x):
-            row = v_zero[x + 1, row0 : row0 + 1]
-            for chunk in range(chunks):
-                to[start + chunk, x : x + 1] = row[:, chunk * LANES : (chunk + 1) * LANES]
+            blocks[device, part] = piece
+
+    def pack(to_low, to_high):
+        for to, rows1, row0 in (
+            (to_low, slice(0, R1), RY + 1),
+            (to_high, slice(tile_y1 - R1, tile_y1), top - 2),
+        ):
+            for which in range(3):
+                for x in range(tile_x1):
+                    flat_row = which * tile_x1 * R1 + x * R1
+                    to[flat_row // ROWS, flat_row % ROWS : flat_row % ROWS + R1] = level_one[
+                        which, x, rows1
+                    ]
+            start = 3 * tile_x1 * R1 // ROWS
+            for x in range(tile_x):
+                row = v_zero[x + 1, row0 : row0 + 1]
+                for chunk in range(chunks):
+                    to[start + chunk, x : x + 1] = row[:, chunk * LANES : (chunk + 1) * LANES]
+
+    on_sides("ty", near, far, pack)
 
 
 def reach_of(layer):
     return R1 + 1 - layer
 
 
-def middle(level_one, v_zero, from_low, from_high, window, to_low, to_high):
+def middle(level_one, v_zero, from_near, from_far, window, near, far):
+    from_low, from_high = by_side("ty", from_near, from_far)
     _, tile_x1, tile_y1, _ = level_one.shape
     planes, rows, size_z = v_zero.shape
     top1 = R1 + tile_y1
@@ -395,38 +445,42 @@
             window[which, x, top1:] = from_high[at, sub : sub + R1]
     chunks = size_z // LANES
     top = rows - RY
-    for to, low in ((to_low, True), (to_high, False)):
-        at = 0
-        for which in (0, 2):
-            for layer in range(1, R1 + 1):
-                x = layer - 1 if low else tile_x1 - layer
-                outer = 1 if which == 0 and layer == R1 else which
-                to[at] = window[outer, x, R1:top1]
-                at += 1
-        loose = at * ROWS
-        for which in (0, 2):
-            for layer in range(1, R1 + 1):
-                x = layer - 1 if low else tile_x1 - layer
-                outer = 1 if which == 0 else which
-                for distance in range(1, reach_of(layer) + 1):
-                    source = outer if distance == reach_of(layer) else which
-                    for row in (R1 - distance, top1 + distance - 1):
-                        to[loose // ROWS, loose % ROWS : loose % ROWS + 1] = window[
-                            source, x, row : row + 1
-                        ]
-                        loose += 1
-        second, first = (2, 1) if low else (planes - 3, planes - 2)
-        for row in (RY - 1, top):
+
+    def pack(to_low, to_high):
+        for to, low in ((to_low, True), (to_high, False)):
+            at = 0
+            for which in (0, 2):
+                for layer in range(1, R1 + 1):
+                    x = layer - 1 if low else tile_x1 - layer
+                    outer = 1 if which == 0 and layer == R1 else which
+                    to[at] = window[outer, x, R1:top1]
+                    at += 1
+            loose = at * ROWS
+            for which in (0, 2):
+                for layer in range(1, R1 + 1):
+                    x = layer - 1 if low else tile_x1 - layer
+                    outer = 1 if which == 0 else which
+                    for distance in range(1, reach_of(layer) + 1):
+                        source = outer if distance == reach_of(layer) else which
+                        for row in (R1 - distance, top1 + distance - 1):
+                            to[loose // ROWS, loose % ROWS : loose % ROWS + 1] = window[
+                                source, x, row : row + 1
+                            ]
+                            loose += 1
+            second, first = (2, 1) if low else (planes - 3, planes - 2)
+            for row in (RY - 1, top):
+                for chunk in range(chunks):
+                    lanes = slice(chunk * LANES, (chunk + 1) * LANES)
+                    to[loose // ROWS, loose % ROWS : loose % ROWS + 1] = v_zero[first, row : row + 1, lanes]
+                    loose += 1
+            at = -(-loose // ROWS)
             for chunk in range(chunks):
                 lanes = slice(chunk * LANES, (chunk + 1) * LANES)
-                to[loose // ROWS, loose % ROWS : loose % ROWS + 1] = v_zero[first, row : row + 1, lanes]
-                loose += 1
-        at = -(-loose // ROWS)
-        for chunk in range(chunks):
-            lanes = slice(chunk * LANES, (chunk + 1) * LANES)
-            for half in range((top - RY) // ROWS):
-                to[at] = v_zero[second, RY + half * ROWS : RY + (half + 1) * ROWS, lanes]
-                at += 1
+                for half in range((top - RY) // ROWS):
+                    to[at] = v_zero[second, RY + half * ROWS : RY + (half + 1) * ROWS, lanes]
+                    at += 1
+
+    on_sides("tx", near, far, pack)
 
 
 def middle_tiles(tile_y, chunks):
@@ -653,15 +707,19 @@
     lane = iota((ROWS, LANES), 1)
     nothing = jnp.zeros((ROWS, LANES), F32)
     forcing = [[nothing] * groups for _ in range(planes)]
-    half_pairs = blocks.shape[1]
+    half_pairs = (half_x + RC) // 2
     ring = RC // 2
     for tx in range(count_x):
         for ty in range(count_y):
             for p in range(half_pairs):
-                piece = blocks[tx * count_y + ty, p]
+                tile, base = p * used // SHORT, p * used % SHORT
+                assert base + used <= 2 * SHORT == ROWS
+                source = tx * count_y + ty
+                piece = jnp.concatenate([blocks[source, tile], blocks[source, tile + 1]], 0)
                 start = (ty * half_y - ring) % rows
                 group, offset = start // ROWS, start % ROWS
-                piece = pltpu.roll(piece, offset, 0) if offset else piece
+                shift = (offset - base) % ROWS
+                piece = pltpu.roll(piece, shift, 0) if shift else piece
                 turned = pltpu.roll(piece, size_z2, 1)
                 for half in range(2):
                     moved = jnp.where((lane < size_z2) == (half == 0), piece, turned)
@@ -677,7 +735,7 @@
 
 
 def coarse_up(
-    counts, grids, blocks, window_one, one_low, one_high, row_low, row_high,
+    counts, grids, blocks, window_one, one_near, one_far, row_near, row_far,
     v_zero, forcing0, cx, cy, cz, weight, *rest,
 ):
     prepared, rest = rest[: len(grids)], rest[len(grids) :]
@@ -686,6 +744,8 @@
         v_one, cx1, cy1, cz1, w1, one_a, one_b, zero_a, zero_b,
     ) = rest
     count_x, count_y = counts
+    one_low, one_high = by_side("tx", one_near, one_far)
+    row_low, row_high = by_side("ty", row_near, row_far)
     _, tile_x1, rows1, size_z1 = window_one.shape
     tile_y1 = rows1 - 2 * R1
     top1 = R1 + tile_y1
@@ -826,11 +886,14 @@
     )(*operands)
 
 
-def exchange(to_low, to_high, axis):
+def exchange(near, far, axis):
     count = lax.axis_size(axis)
-    from_low = lax.ppermute(to_high, axis, [(i, (i + 1) % count) for i in range(count)])
-    from_high = lax.ppermute(to_low, axis, [((i + 1) % count, i) for i in range(count)])
-    return from_low, from_high
+    assert count % 2 == 0
+    partner = [(i, i ^ 1) for i in range(count)]
+    other = [(i, (i - 1 if i % 2 == 0 else i + 1) % count) for i in range(count)]
+    from_far = lax.ppermute(far, axis, other)
+    from_near = lax.ppermute(near, axis, partner)
+    return from_near, from_far
 
 
 def to_everyone(blocks):
@@ -844,7 +907,7 @@
     everyone = counts[0] * counts[1]
     rows = tile_y + 2 * RY
     message = (tile_x + 1, ROWS, size_z)
-    *inputs, to_low, to_high = call(
+    *inputs, near, far = call(
         edges,
         tuple(
             pltpu.with_memory_space_constraint(v, pltpu.HBM)
@@ -855,12 +918,12 @@
         (pltpu.SemaphoreType.DMA((3,)),),
         IN_PLACE,
     )
-    from_low, from_high = exchange(to_low, to_high, "ty")
+    from_near, from_far = exchange(near, far, "ty")
     message = (len(BASE_PLANES) + 1, tile_y, size_z)
-    window, to_low, to_high = call(
-        sides, (*inputs, from_low, from_high), ((3, tile_x, rows, size_z), message, message), ()
+    window, near, far = call(
+        sides, (*inputs, from_near, from_far), ((3, tile_x, rows, size_z), message, message), ()
     )
-    from_low, from_high = exchange(to_low, to_high, "tx")
+    from_near, from_far = exchange(near, far, "tx")
 
     zero = (tile_x + 2 * RX, rows, size_z)
     inner = (tile_x + 2, rows, size_z)
@@ -878,13 +941,15 @@
     wide = -(-rows // (2 * ROWS)) * ROWS
     small = (one_tile[0] + 2 * RC, wide, one_tile[2])
     pairs1 = small[0] // 2
+    short = pairs1 // 2 * (two_tile[1] + RC) // SHORT
+    assert pairs1 // 2 * (two_tile[1] + RC) % SHORT == 0
     message = (3 * one_tile[0] * R1 // ROWS + chunks, ROWS, LANES)
     assert one_tile[2] == LANES and tile_x <= ROWS and one_tile[1] == ROWS
-    v_zero, forcing0, cx, cy, cz, weight, level_one, blocks, to_low, to_high = call(
+    v_zero, forcing0, cx, cy, cz, weight, level_one, blocks, near, far = call(
         fine_down,
-        (window, from_low, from_high),
+        (window, from_near, from_far),
         (inner, inner, (tile_x + 3, rows, size_z), inner, inner, inner)
-        + ((3,) + one_tile, (everyone, pairs1 // 2, ROWS, LANES), message, message),
+        + ((3,) + one_tile, (everyone, short, SHORT, LANES), message, message),
         (
             (6, rows, size_z),
             (4, rows, size_z),
@@ -897,17 +962,17 @@
         + (small,) * 9
         + ((pairs1, wide, one_tile[2]), (pairs1, ROWS, one_tile[2])),
     )
-    row_low, row_high = exchange(to_low, to_high, "ty")
+    row_near, row_far = exchange(near, far, "ty")
     blocks = to_everyone(blocks)
     rows1 = one_tile[1] + 2 * R1
     message = (middle_tiles(tile_y, chunks), ROWS, LANES)
-    window_one, to_low, to_high = call(
+    window_one, near, far = call(
         middle,
-        (level_one, v_zero, row_low, row_high),
+        (level_one, v_zero, row_near, row_far),
         ((3, one_tile[0], rows1, one_tile[2]), message, message),
         (),
     )
-    one_low, one_high = exchange(to_low, to_high, "tx")
+    one_near, one_far = exchange(near, far, "tx")
     lattice = grids[0].sizes[1], LANES
     prepared = call(
         functools.partial(prepare, counts, grids),
@@ -920,7 +985,7 @@
     rim = (R1,) + one[1:]
     (updated,) = call(
         functools.partial(coarse_up, counts, grids),
-        (blocks, window_one, one_low, one_high, row_low, row_high)
+        (blocks, window_one, one_near, one_far, row_near, row_far)
         + (v_zero, forcing0, cx, cy, cz, weight, *prepared),
         (concentration.shape,),
         (rim,) * 6 + (one,) * 7 + (zero, zero),

time: 42.9 us -> 43.4 us (1.012)
    all_to_all x2, waiting for transfers between devices: 2.17 us -> 3.47 us  [to_everyone(): return lax.all_to_all(blocks, ('tx', 'ty'), 0, 0)]
    ppermute x8, waiting for transfers between devices: 7.1 us -> 6.02 us  [the longest x4 5.89 us: exchange(): from_far = lax.ppermute(far, axis, other)]
    ppermute x8, starting transfers between devices: 15.3 us -> 16.1 us  [the longest x4 12.2 us: exchange(): from_far = lax.ppermute(far, axis, other)]
    all_to_all x2, starting transfers between devices: 5.84 us -> 5.39 us  [to_everyone(): return lax.all_to_all(blocks, ('tx', 'ty'), 0, 0)]
where the time goes in v2:
time: 43.4 us; the launch traced here: 43.1 us
  starting transfers between devices  21.4 us (49%)
  Pallas kernels  12.1 us (28%)
  waiting for transfers between devices  9.49 us (22%)
    ppermute x4, starting transfers between devices, exchange(): from_far = lax.ppermute(far, axis, other)  12.2 us
    pallas_call x7, Pallas kernels, call(): pl.pallas_call(kernel, in_specs=[spec] * len(operands), out_specs=[VM] *...  12.1 us
    ppermute x4, waiting for transfers between devices, exchange(): from_far = lax.ppermute(far, axis, other)  5.89 us
    all_to_all x2, starting transfers between devices, to_everyone(): return lax.all_to_all(blocks, ('tx', 'ty'), 0, 0)  5.39 us
    ppermute x4, starting transfers between devices, exchange(): from_near = lax.ppermute(near, axis, partner)  3.88 us
    all_to_all x2, waiting for transfers between devices, to_everyone(): return lax.all_to_all(blocks, ('tx', 'ty'), 0, 0)  3.47 us
  transfers between devices with their start and end apart: 10, of which 5 were waited for; matrix products, arithmetic and copies ran while one was open for 0% of the time, Pallas kernels for 16%

profile of v2, /device:TPU:0, one launch (start us, length us, event | category | flops | bytes accessed | tf_op | source)
XLA Modules:
  0.0 43.1 jit_solution(16423698672730187300)
XLA Ops:
  0.0 1.2 %shard_map.37 = (f32[8,16,256]{2,1,0:T(8,128)S(1)}, f32[8,16,256]{2,1,0:T(8,128)S(1)}, s32[8,16,256]{2,1,0:T(8,128)S(1)}, f32[9,8,256]{2,1,0:T(8,128)S(1)}, f32[9,8,256]{2,1,0:T(8,128)S(1)}) custom-call(f32[8,16,256]{2,1,0:T(8,128)} %conc_in.1, f32[8,16,256]{2,1,0:T(8,128)} %source_in.1, s32[8,16,256]{2,1,0:T(8,128)} %material_in.1), custom_call_target="tpu_custom_call" | custom-call | tf_op jit(solution)/shard_map/pallas_call | solution.py:879
  1.2 0.6 %collective-permute-start = (f32[9,8,256]{2,1,0:T(8,128)S(1)}, f32[9,8,256]{2,1,0:T(8,128)S(1)}, u32[]{:S(2)}, u32[]{:S(2)}) collective-permute-start(f32[9,8,256]{2,1,0:T(8,128)S(1)} %get-tuple-element.33), channel_id=1, source_target_pairs={{0,1},{1,0},{2,3},{3,2},{4,5},{5,4},{6,7},{7,6},{8,9},{9,8},{10,11... | collective-permute-start | bytes 221192 | tf_op jit(solution)/shard_map/ppermute | solution.py:895
  1.7 2.6 %collective-permute-start.1 = (f32[9,8,256]{2,1,0:T(8,128)S(1)}, f32[9,8,256]{2,1,0:T(8,128)S(1)}, u32[]{:S(2)}, u32[]{:S(2)}) collective-permute-start(f32[9,8,256]{2,1,0:T(8,128)S(1)} %get-tuple-element.34), channel_id=1, source_target_pairs={{0,3},{1,2},{2,1},{3,0},{4,7},{5,6},{6,5},{7,4},{8,11},{9,10},{10,... | collective-permute-start | bytes 221192 | tf_op jit(solution)/shard_map/ppermute | solution.py:894
  4.3 0.0 collective-permute-done.from_near
  4.3 2.6 %collective-permute-done.1.from_far = f32[9,8,256]{2,1,0:T(8,128)S(1)} collective-permute-done((f32[9,8,256]{2,1,0:T(8,128)S(1)}, f32[9,8,256]{2,1,0:T(8,128)S(1)}, u32[]{:S(2)}, u32[]{:S(2)}) %collective-permute-start.1) | collective-permute-done | bytes 73760 | tf_op jit(solution)/shard_map/ppermute | solution.py:894
  6.9 0.2 shard_map.38
  7.1 1.4 %collective-permute-start.2 = (f32[10,16,256]{2,1,0:T(8,128)S(1)}, f32[10,16,256]{2,1,0:T(8,128)S(1)}, u32[]{:S(2)}, u32[]{:S(2)}) collective-permute-start(f32[10,16,256]{2,1,0:T(8,128)S(1)} %get-tuple-element.36), channel_id=1, source_target_pairs={{0,4},{4,0},{8,12},{12,8},{16,20},{20,16},{24,28},{28,24},{1,5},{5... | collective-permute-start | bytes 491528 | tf_op jit(solution)/shard_map/ppermute | solution.py:895
  8.6 3.5 %collective-permute-start.3 = (f32[10,16,256]{2,1,0:T(8,128)S(1)}, f32[10,16,256]{2,1,0:T(8,128)S(1)}, u32[]{:S(2)}, u32[]{:S(2)}) collective-permute-start(f32[10,16,256]{2,1,0:T(8,128)S(1)} %get-tuple-element.37), channel_id=1, source_target_pairs={{0,28},{4,8},{8,4},{12,16},{16,12},{20,24},{24,20},{28,0},{1,29},{... | collective-permute-start | bytes 491528 | tf_op jit(solution)/shard_map/ppermute | solution.py:894
  12.1 1.1 %shard_map.41 = f32[32,4,128]{2,1,0:T(4,128)} custom-call(f32[3,8,24,256]{3,2,1,0:T(8,128)S(1)} %get-tuple-element.35.window), custom_call_target="tpu_custom_call" | custom-call | tf_op jit(solution)/shard_map/pallas_call | solution.py:879
  13.2 2.8 %all-to-all-start.1 = ((f32[32,4,128]{2,1,0:T(4,128)}), f32[32,4,128]{2,1,0:T(4,128)S(1)}, u32[]{:S(2)}, u32[]{:S(2)}) async-start(f32[32,4,128]{2,1,0:T(4,128)} %shard_map.41), calls=%async_computation.1 | async-start | bytes 131072 | tf_op jit(solution)/shard_map/all_to_all | solution.py:900
  16.0 0.1 collective-permute-done.2.from_near
  16.1 1.4 %collective-permute-done.3.from_far = f32[10,16,256]{2,1,0:T(8,128)S(1)} collective-permute-done((f32[10,16,256]{2,1,0:T(8,128)S(1)}, f32[10,16,256]{2,1,0:T(8,128)S(1)}, u32[]{:S(2)}, u32[]{:S(2)}) %collective-permute-start.3) | collective-permute-done | bytes 163872 | tf_op jit(solution)/shard_map/ppermute | solution.py:894
  17.5 2.4 %shard_map.39 = (f32[10,24,256]{2,1,0:T(8,128)S(1)}, f32[10,24,256]{2,1,0:T(8,128)S(1)}, f32[11,24,256]{2,1,0:T(8,128)S(1)}, f32[10,24,256]{2,1,0:T(8,128)S(1)},...) custom-call(f32[3,8,24,256]{3,2,1,0:T(8,128)S(1)} %get-tuple-element, ...), custom_call_target="tpu_custom_call" | custom-call | tf_op jit(solution)/shard_map/pallas_call | solution.py:879
  20.0 3.5 %all-to-all-done.1.blocks = f32[32,4,128]{2,1,0:T(4,128)S(1)} async-done(((f32[32,4,128]{2,1,0:T(4,128)}), f32[32,4,128]{2,1,0:T(4,128)S(1)}, u32[]{:S(2)}, u32[]{:S(2)}) %all-to-all-start.1) | async-done | bytes 65568 | tf_op jit(solution)/shard_map/all_to_all | solution.py:900
  23.4 2.6 %all-to-all-start = ((f32[32,3,4,128]{3,2,1,0:T(4,128)}), f32[32,3,4,128]{3,2,1,0:T(4,128)S(1)}, u32[]{:S(2)}, u32[]{:S(2)}) async-start(f32[32,3,4,128]{3,2,1,0:T(4,128)} %get-tuple-element.38), calls=%async_computation | async-start | bytes 393216 | tf_op jit(solution)/shard_map/all_to_all | solution.py:900
  26.0 0.2 collective-permute-start.4
  26.2 1.6 %collective-permute-start.5 = (f32[8,8,128]{2,1,0:T(8,128)S(1)}, f32[8,8,128]{2,1,0:T(8,128)S(1)}, u32[]{:S(2)}, u32[]{:S(2)}) collective-permute-start(f32[8,8,128]{2,1,0:T(8,128)S(1)} %get-tuple-element.42), channel_id=1, source_target_pairs={{0,3},{1,2},{2,1},{3,0},{4,7},{5,6},{6,5},{7,4},{8,11},{9,10},{10,... | collective-permute-start | bytes 98312 | tf_op jit(solution)/shard_map/ppermute | solution.py:894
  27.8 0.0 collective-permute-done.4.from_near.row_near
  27.8 1.9 %collective-permute-done.5.from_far.row_far = f32[8,8,128]{2,1,0:T(8,128)S(1)} collective-permute-done((f32[8,8,128]{2,1,0:T(8,128)S(1)}, f32[8,8,128]{2,1,0:T(8,128)S(1)}, u32[]{:S(2)}, u32[]{:S(2)}) %collective-permute-start.5) | collective-permute-done | bytes 32800 | tf_op jit(solution)/shard_map/ppermute | solution.py:894
  29.8 0.1 shard_map.40
  29.8 1.7 %collective-permute-start.6 = (f32[18,8,128]{2,1,0:T(8,128)S(1)}, f32[18,8,128]{2,1,0:T(8,128)S(1)}, u32[]{:S(2)}, u32[]{:S(2)}) collective-permute-start(f32[18,8,128]{2,1,0:T(8,128)S(1)} %get-tuple-element.44), channel_id=1, source_target_pairs={{0,4},{4,0},{8,12},{12,8},{16,20},{20,16},{24,28},{28,24},{1,5},{5... | collective-permute-start | bytes 221192 | tf_op jit(solution)/shard_map/ppermute | solution.py:895
  31.5 4.4 %collective-permute-start.7 = (f32[18,8,128]{2,1,0:T(8,128)S(1)}, f32[18,8,128]{2,1,0:T(8,128)S(1)}, u32[]{:S(2)}, u32[]{:S(2)}) collective-permute-start(f32[18,8,128]{2,1,0:T(8,128)S(1)} %get-tuple-element.45), channel_id=1, source_target_pairs={{0,28},{4,8},{8,4},{12,16},{16,12},{20,24},{24,20},{28,0},{1,29},{... | collective-permute-start | bytes 221192 | tf_op jit(solution)/shard_map/ppermute | solution.py:894
  35.9 3.2 %shard_map.42 = (f32[5,16,16,128]{3,2,1,0:T(8,128)S(1)}, f32[5,8,16,128]{3,2,1,0:T(8,128)S(1)}, f32[5,4,16,128]{3,2,1,0:T(8,128)S(1)}, f32[32,128]{1,0:T(8,128)S(1)}) custom-call(f32[32,4,128]{2,1,0:T(4,128)S(1)} %all-to-all-done.1.blocks, f32[3,4,16,128]{3,2,1,0:T(8,128)S(1)} %get-tuple-element.43._.window_one), custom_call_target="tpu_custom_call" | custom-call | tf_op jit(solution)/shard_map/pallas_call | solution.py:879
  39.2 0.0 collective-permute-done.6.one_near
  39.2 0.0 collective-permute-done.7.one_far
  39.2 0.0 all-to-all-done.blocks
  39.2 3.9 %shard_map.43 = f32[8,16,256]{2,1,0:T(8,128)} custom-call(f32[32,3,4,128]{3,2,1,0:T(4,128)S(1)} %all-to-all-done.blocks, f32[3,4,16,128]{3,2,1,0:T(8,128)S(1)} %get-tuple-element.43._.window_one, f32[18,8,128]{2,1,0:T(8,128)S(1)} %collective-permute-done.6.one_near, f32[18,8,128]{2,1,0:T(8,128)S(1)} %collective-permute-done.7.one_far, ...), custom_call_target="tpu_custom_call" | custom-call | tf_op jit(solution)/shard_map/pallas_call | solution.py:879
Async XLA Ops:
  1.2 3.2 %collective-permute-start = (f32[9,8,256]{2,1,0:T(8,128)S(1)}, f32[9,8,256]{2,1,0:T(8,128)S(1)}, u32[]{:S(2)}, u32[]{:S(2)}) collective-permute-start(f32[9,8,256]{2,1,0:T(8,128)S(1)} %get-tuple-element.33), channel_id=1, source_target_pairs={{0,1},{1,0},{2,3},{3,2},{4,5},{5,4},{6,7},{7,6},{8,9},{9,8},{10,11... | collective-permute-start | bytes 221192 | tf_op jit(solution)/shard_map/ppermute | solution.py:895
  1.7 5.2 %collective-permute-start.1 = (f32[9,8,256]{2,1,0:T(8,128)S(1)}, f32[9,8,256]{2,1,0:T(8,128)S(1)}, u32[]{:S(2)}, u32[]{:S(2)}) collective-permute-start(f32[9,8,256]{2,1,0:T(8,128)S(1)} %get-tuple-element.34), channel_id=1, source_target_pairs={{0,3},{1,2},{2,1},{3,0},{4,7},{5,6},{6,5},{7,4},{8,11},{9,10},{10,... | collective-permute-start | bytes 221192 | tf_op jit(solution)/shard_map/ppermute | solution.py:894
  7.1 9.0 %collective-permute-start.2 = (f32[10,16,256]{2,1,0:T(8,128)S(1)}, f32[10,16,256]{2,1,0:T(8,128)S(1)}, u32[]{:S(2)}, u32[]{:S(2)}) collective-permute-start(f32[10,16,256]{2,1,0:T(8,128)S(1)} %get-tuple-element.36), channel_id=1, source_target_pairs={{0,4},{4,0},{8,12},{12,8},{16,20},{20,16},{24,28},{28,24},{1,5},{5... | collective-permute-start | bytes 491528 | tf_op jit(solution)/shard_map/ppermute | solution.py:895
  8.6 9.0 %collective-permute-start.3 = (f32[10,16,256]{2,1,0:T(8,128)S(1)}, f32[10,16,256]{2,1,0:T(8,128)S(1)}, u32[]{:S(2)}, u32[]{:S(2)}) collective-permute-start(f32[10,16,256]{2,1,0:T(8,128)S(1)} %get-tuple-element.37), channel_id=1, source_target_pairs={{0,28},{4,8},{8,4},{12,16},{16,12},{20,24},{24,20},{28,0},{1,29},{... | collective-permute-start | bytes 491528 | tf_op jit(solution)/shard_map/ppermute | solution.py:894
  13.2 10.2 %all-to-all-start.1 = ((f32[32,4,128]{2,1,0:T(4,128)}), f32[32,4,128]{2,1,0:T(4,128)S(1)}, u32[]{:S(2)}, u32[]{:S(2)}) async-start(f32[32,4,128]{2,1,0:T(4,128)} %shard_map.41), calls=%async_computation.1 | async-start | bytes 131072 | tf_op jit(solution)/shard_map/all_to_all | solution.py:900
  23.4 15.8 %all-to-all-start = ((f32[32,3,4,128]{3,2,1,0:T(4,128)}), f32[32,3,4,128]{3,2,1,0:T(4,128)S(1)}, u32[]{:S(2)}, u32[]{:S(2)}) async-start(f32[32,3,4,128]{3,2,1,0:T(4,128)} %get-tuple-element.38), calls=%async_computation | async-start | bytes 393216 | tf_op jit(solution)/shard_map/all_to_all | solution.py:900
  26.0 1.8 %collective-permute-start.4 = (f32[8,8,128]{2,1,0:T(8,128)S(1)}, f32[8,8,128]{2,1,0:T(8,128)S(1)}, u32[]{:S(2)}, u32[]{:S(2)}) collective-permute-start(f32[8,8,128]{2,1,0:T(8,128)S(1)} %get-tuple-element.41), channel_id=1, source_target_pairs={{0,1},{1,0},{2,3},{3,2},{4,5},{5,4},{6,7},{7,6},{8,9},{9,8},{10,11... | collective-permute-start | bytes 98312 | tf_op jit(solution)/shard_map/ppermute | solution.py:895
  26.2 3.6 %collective-permute-start.5 = (f32[8,8,128]{2,1,0:T(8,128)S(1)}, f32[8,8,128]{2,1,0:T(8,128)S(1)}, u32[]{:S(2)}, u32[]{:S(2)}) collective-permute-start(f32[8,8,128]{2,1,0:T(8,128)S(1)} %get-tuple-element.42), channel_id=1, source_target_pairs={{0,3},{1,2},{2,1},{3,0},{4,7},{5,6},{6,5},{7,4},{8,11},{9,10},{10,... | collective-permute-start | bytes 98312 | tf_op jit(solution)/shard_map/ppermute | solution.py:894
  29.8 9.4 %collective-permute-start.6 = (f32[18,8,128]{2,1,0:T(8,128)S(1)}, f32[18,8,128]{2,1,0:T(8,128)S(1)}, u32[]{:S(2)}, u32[]{:S(2)}) collective-permute-start(f32[18,8,128]{2,1,0:T(8,128)S(1)} %get-tuple-element.44), channel_id=1, source_target_pairs={{0,4},{4,0},{8,12},{12,8},{16,20},{20,16},{24,28},{28,24},{1,5},{5... | collective-permute-start | bytes 221192 | tf_op jit(solution)/shard_map/ppermute | solution.py:895
  31.5 7.7 %collective-permute-start.7 = (f32[18,8,128]{2,1,0:T(8,128)S(1)}, f32[18,8,128]{2,1,0:T(8,128)S(1)}, u32[]{:S(2)}, u32[]{:S(2)}) collective-permute-start(f32[18,8,128]{2,1,0:T(8,128)S(1)} %get-tuple-element.45), channel_id=1, source_target_pairs={{0,28},{4,8},{8,4},{12,16},{16,12},{20,24},{24,20},{28,0},{1,29},{... | collective-permute-start | bytes 221192 | tf_op jit(solution)/shard_map/ppermute | solution.py:894

commit v3 on v2

--- a/solution.py
+++ b/solution.py
@@ -14,7 +14,7 @@
 LANES = 128
 ROWS = 8
 SHORT = 4
-RX = 3
+RX = 2
 RY = 4
 R1 = 4
 RC = 2
@@ -43,14 +43,8 @@
         ref[index] = value
 
 
-def kept(ref, first, before=None, after=None):
-    planes = [(ref, x) for x in range(ref.shape[0])]
-    if before is not None:
-        planes = [before] + planes
-        first -= 1
-    if after is not None:
-        planes = planes + [after]
-    return Planes(first, planes)
+def kept(ref, first):
+    return Planes(first, [(ref, x) for x in range(ref.shape[0])])
 
 
 def is_even(axis):
@@ -163,7 +157,7 @@
         out[x] = (1.0 - relax_weight) * v[x] + weight[x] * (forcing[x] + neighbours(v, cx, cy, cz, x))
 
 
-def edges(conc_in, source_in, material_in, conc, source, material, near, far, arrived):
+def edges(conc_in, source_in, material_in, conc, source, material, to_low, to_high, arrived):
     copies = [
         pltpu.make_async_copy(whence, whither, arrived.at[n])
         for n, (whence, whither) in enumerate(
@@ -175,26 +169,21 @@
     for copy in copies:
         copy.wait()
     tile_x, tile_y, _ = conc.shape
-
-    def pack(to_low, to_high):
-        for to, low in ((to_low, True), (to_high, False)):
-            for x in range(tile_x):
-                rows = slice(0, 4) if low else slice(tile_y - 4, tile_y)
-                near = slice(0, 3) if low else slice(1, 4)
-                pair = slice(0, 2) if low else slice(2, 4)
-                c = conc[x, rows]
-                f = mass_rate * c + source[x, rows]
-                k = lookup(material[x, rows])
-                to[x, 0:3] = c[near]
-                to[x, 3:5] = f[pair]
-                to[x, 5:8] = k[near]
-                to[tile_x, x : x + 1] = k[3:4] if low else k[0:1]
-
-    on_sides("ty", near, far, pack)
-
-
-def sides(conc, source, material, from_near, from_far, window, near, far):
-    from_low, from_high = by_side("ty", from_near, from_far)
+    for to, low in ((to_low, True), (to_high, False)):
+        for x in range(tile_x):
+            rows = slice(0, 4) if low else slice(tile_y - 4, tile_y)
+            near = slice(0, 3) if low else slice(1, 4)
+            pair = slice(0, 2) if low else slice(2, 4)
+            c = conc[x, rows]
+            f = mass_rate * c + source[x, rows]
+            k = lookup(material[x, rows])
+            to[x, 0:3] = c[near]
+            to[x, 3:5] = f[pair]
+            to[x, 5:8] = k[near]
+            to[tile_x, x : x + 1] = k[3:4] if low else k[0:1]
+
+
+def sides(conc, source, material, k_tile, from_low, from_high, window, to_low, to_high, swept):
     tile_x, tile_y, size_z = conc.shape
     top = RY + tile_y
     for x in range(tile_x):
@@ -214,44 +203,80 @@
         window[2, x, 1:4] = from_low[x, 5:8]
         window[2, x, top : top + 3] = from_high[x, 5:8]
         window[2, x, top + 3 :] = from_high[tile_x, x : x + 1]
-
-    def pack(to_low, to_high):
-        for to, plane in ((to_low, lambda l: l - 1), (to_high, lambda l: tile_x - l)):
-            for at, (which, layer) in enumerate(BASE_PLANES):
-                to[at] = window[which, plane(layer), RY:top]
-            at = 0
-            for which, layer, reach in EXTRA_ROWS:
-                for start in (RY - reach, top):
-                    to[len(BASE_PLANES), at : at + reach] = window[
-                        which, plane(layer), start : start + reach
-                    ]
-                    at += reach
-
-    on_sides("tx", near, far, pack)
-
-
-BASE_PLANES = (
-    (0, 1), (0, 2), (0, 3), (1, 1), (1, 2), (2, 1), (2, 2), (2, 3), (2, 4),
-)
+    per_plane = tile_y // ROWS
+    for to, low in ((to_low, True), (to_high, False)):
+
+        def plane(layer):
+            return layer - 1 if low else tile_x - layer
+
+        def send(at, values):
+            for n in range(per_plane):
+                to[at + n] = values(n)
+
+        for n, (which, layer) in enumerate(BASE_PLANES):
+            send(
+                n * per_plane,
+                lambda n: window[which, plane(layer), RY + n * ROWS : RY + (n + 1) * ROWS],
+            )
+        first_sweep(window, plane(2), swept)
+        at = len(BASE_PLANES) * per_plane
+        send(at, lambda n: swept[RY + n * ROWS : RY + (n + 1) * ROWS])
+        loose = (at + per_plane) * ROWS
+        for which, layer, reach in EXTRA_ROWS:
+            for start in (RY - reach, top):
+                to[loose // ROWS, loose % ROWS : loose % ROWS + reach] = window[
+                    which, plane(layer), start : start + reach
+                ]
+                loose += reach
+        at = -(-loose // ROWS)
+        to[at, :, 0 : size_z // 2] = k_tile[1 if low else k_tile.shape[0] - 2]
+        to[at, :, size_z // 2 :] = jnp.zeros((ROWS, size_z - size_z // 2), F32)
+
+
+def first_sweep(window, x, out):
+    c, f, k = window[0, x], window[1, x], window[2, x]
+    next_part = 0.5 * (k + window[2, x + 1])
+    last_part = 0.5 * (k + window[2, x - 1])
+    y_part = 0.5 * (k + ahead(k, 0))
+    z_part = 0.5 * (k + ahead(k, 1))
+    d = mass_rate + next_part + last_part
+    d = d + y_part + back(y_part, 0) + z_part + back(z_part, 1)
+    total = next_part * window[0, x + 1] + last_part * window[0, x - 1]
+    total = total + (y_part * ahead(c, 0) + back(y_part * c, 0))
+    total = total + (z_part * ahead(c, 1) + back(z_part * c, 1))
+    out[...] = (1.0 - relax_weight) * c + (relax_weight / d) * (f + total)
+
+
+BASE_PLANES = ((0, 1), (0, 2), (1, 1), (2, 1), (2, 2))
 EXTRA_ROWS = ((0, 1, 2), (0, 2, 1), (1, 1, 1), (2, 1, 2), (2, 2, 2))
 
 
-def shrink(window, blocks, paired, paired_one):
-    _, tile_x, rows, size_z = window.shape
-    tile_x1, tile_y1, size_z1 = tile_x // 2, (rows - 2 * RY) // 2, size_z // 2
+def plane_tiles(tile_y):
+    loose = sum(2 * reach for _, _, reach in EXTRA_ROWS)
+    return (len(BASE_PLANES) + 1) * tile_y // ROWS + -(-loose // ROWS) + 1
+
+
+def shrink(material, k_tile, blocks, paired, paired_one):
+    tile_x, tile_y, size_z = material.shape
+    tile_x1, tile_y1, size_z1 = tile_x // 2, tile_y // 2, size_z // 2
     k_one = None
     for chunk in range(size_z // LANES):
         lanes = slice(chunk * LANES, (chunk + 1) * LANES)
         for pair in range(tile_x1):
-            paired[pair] = window[2, 2 * pair, :, lanes] + window[2, 2 * pair + 1, :, lanes]
+            paired[pair] = lookup(material[2 * pair, :, lanes]) + lookup(
+                material[2 * pair + 1, :, lanes]
+            )
         stack = [
-            paired[pair, pl.ds(RY, tile_y1, stride=2)] + paired[pair, pl.ds(RY + 1, tile_y1, stride=2)]
+            paired[pair, pl.ds(0, tile_y1, stride=2)] + paired[pair, pl.ds(1, tile_y1, stride=2)]
             for pair in range(tile_x1)
         ]
         part = times_right(
             jnp.concatenate(stack, 0), halve_lanes(LANES, size_z1, chunk * LANES // 2)
         )
         k_one = part if k_one is None else k_one + part
+    k_one = 0.125 * k_one
+    for x in range(tile_x1):
+        k_tile[x] = k_one[x * tile_y1 : (x + 1) * tile_y1]
     assert tile_x1 // 2 * (size_z1 // 2) <= LANES
     block = None
     for pair in range(tile_x1 // 2):
@@ -262,24 +287,23 @@
         )
         part = times_right(piece, halve_lanes(size_z1, LANES, pair * size_z1 // 2))
         block = part if block is None else block + part
-    block = (0.125 * 0.125) * block
+    block = 0.125 * block
     for device in range(blocks.shape[0]):
         blocks[device] = block
 
 
 def fine_down(
-    window, from_near, from_far,
-    v_zero, forcing_out, cx, cy, cz, weight, level_one, blocks, near, far,
-    conc_rim, forcing_rim, kappa_rim, once, diag, paired, outer,
+    window, from_low, from_high,
+    v_zero, forcing_out, cx, cy, cz, weight, level_one, blocks_out, to_low, to_high,
+    conc_rim, forcing_rim, kappa_rim, once, diag, paired, blocks, left,
     k_one, f_one, u_one, v_one, cx1, cy1, cz1, w1, d1, paired_one, packed,
 ):
-    from_low, from_high = by_side("tx", from_near, from_far)
     _, tile_x, rows, size_z = window.shape
     tile_y = rows - 2 * RY
     top = RY + tile_y
     planes = tile_x + 2 * RX
     rims = (conc_rim, forcing_rim, kappa_rim)
-    depths = (3, 2, 4)
+    depths = (2, 1, 2)
     for which, rim in enumerate(rims):
         fill = jnp.full((rows, size_z), 1.0 if which == 2 else 0.0, F32)
         for x in range(2 * depths[which]):
@@ -288,16 +312,28 @@
     def place(which, layer, low):
         return depths[which] - layer if low else depths[which] + layer - 1
 
+    per_plane = tile_y // ROWS
+    last_tile = plane_tiles(tile_y) - 1
     for message, low in ((from_low, True), (from_high, False)):
         for at, (which, layer) in enumerate(BASE_PLANES):
-            rims[which][place(which, layer, low), RY:top] = message[at]
-        at = 0
+            for n in range(per_plane):
+                start = RY + n * ROWS
+                rims[which][place(which, layer, low), start : start + ROWS] = message[
+                    at * per_plane + n
+                ]
+        rim_x = 0 if low else planes - 1
+        once[rim_x] = jnp.zeros((rows, size_z), F32)
+        at = len(BASE_PLANES) * per_plane
+        for n in range(per_plane):
+            start = RY + n * ROWS
+            once[rim_x, start : start + ROWS] = message[at + n]
+        loose = (at + per_plane) * ROWS
         for which, layer, reach in EXTRA_ROWS:
-            rim, x = rims[which], place(which, layer, low)
-            rim[x, RY - reach : RY] = message[len(BASE_PLANES), at : at + reach]
-            at += reach
-            rim[x, top : top + reach] = message[len(BASE_PLANES), at : at + reach]
-            at += reach
+            for start in (RY - reach, top):
+                rims[which][place(which, layer, low), start : start + reach] = message[
+                    loose // ROWS, loose % ROWS : loose % ROWS + reach
+                ]
+                loose += reach
 
     def stacked(which):
         depth = depths[which]
@@ -307,16 +343,11 @@
         return Planes(RX - depth, whole)
 
     conc, forcing, kappa = stacked(0), stacked(1), stacked(2)
-    cx = kept(cx, RX - 2, (outer, 0), (outer, 1))
-    cy = kept(cy, RX - 1, (outer, 2), (outer, 3))
-    cz = kept(cz, RX - 1, (outer, 4), (outer, 5))
-    weight = kept(weight, RX - 1, (outer, 6), (outer, 7))
+    cx, cy, cz, weight = kept(cx, RX - 2), kept(cy, RX - 1), kept(cz, RX - 1), kept(weight, RX - 1)
     v_out = kept(v_zero, RX - 1)
     plane_setup(kappa, cx, cy, cz, weight, diag, 1.0, 1, planes - 1)
     plane_sweep(conc, once, forcing, cx, cy, cz, weight, 1, planes - 1)
-    plane_sweep(once, v_out, forcing, cx, cy, cz, weight, 2, planes - 2)
-    for x in range(RX - 1, planes - RX + 1):
-        forcing_out[x - RX + 1] = forcing[x]
+    plane_sweep(once, v_out, forcing, cx, cy, cz, weight, 1, planes - 1)
     chunks = size_z // LANES
     size_z1 = size_z // 2
     to_half = [halve_lanes(LANES, size_z1, chunk * LANES // 2) for chunk in range(chunks)]
@@ -342,14 +373,16 @@
     planes1 = tile_x1 + 2 * RC
     if 2 * wide > rows:
         for chunk in range(chunks):
-            for pair in range(planes1):
+            for pair in range(planes1 - 2):
                 paired[chunk, pair, rows:] = jnp.ones((2 * wide - rows, LANES), F32)
-    for pair in range(planes1):
-        x = RX - 2 * RC + 2 * pair
-        put(pair, kappa[x] + kappa[x + 1])
-    coarse = narrowed(planes1, 0, wide)
-    for pair in range(planes1):
-        k_one[pair] = coarse[pair * wide : (pair + 1) * wide]
+    for pair in range(planes1 - 2):
+        put(pair, kappa[2 * pair] + kappa[2 * pair + 1])
+    coarse = narrowed(planes1 - 2, 0, wide)
+    for pair in range(planes1 - 2):
+        k_one[pair + 1] = coarse[pair * wide : (pair + 1) * wide]
+    for message, x in ((from_low, 0), (from_high, planes1 - 1)):
+        k_one[x] = jnp.ones((wide, size_z1), F32)
+        k_one[x, RC : RC + tile_y1] = message[last_tile, :, 0:size_z1]
     plane_setup(k_one, cx1, cy1, cz1, w1, d1, 0.25, 1, planes1 - 1)
 
     for pair in range(tile_x1):
@@ -406,33 +439,34 @@
         piece = block[part * SHORT : (part + 1) * SHORT]
         for device in range(blocks.shape[0]):
             blocks[device, part] = piece
-
-    def pack(to_low, to_high):
-        for to, rows1, row0 in (
-            (to_low, slice(0, R1), RY + 1),
-            (to_high, slice(tile_y1 - R1, tile_y1), top - 2),
-        ):
-            for which in range(3):
-                for x in range(tile_x1):
-                    flat_row = which * tile_x1 * R1 + x * R1
-                    to[flat_row // ROWS, flat_row % ROWS : flat_row % ROWS + R1] = level_one[
-                        which, x, rows1
-                    ]
-            start = 3 * tile_x1 * R1 // ROWS
-            for x in range(tile_x):
-                row = v_zero[x + 1, row0 : row0 + 1]
-                for chunk in range(chunks):
-                    to[start + chunk, x : x + 1] = row[:, chunk * LANES : (chunk + 1) * LANES]
-
-    on_sides("ty", near, far, pack)
+    copy = pltpu.make_async_copy(blocks, blocks_out, left)
+    copy.start()
+    for x in range(RX - 1, planes - RX + 1):
+        forcing_out[x - RX + 1] = forcing[x]
+
+    for to, rows1, row0 in (
+        (to_low, slice(0, R1), RY + 1),
+        (to_high, slice(tile_y1 - R1, tile_y1), top - 2),
+    ):
+        for which in range(3):
+            for x in range(tile_x1):
+                flat_row = which * tile_x1 * R1 + x * R1
+                to[flat_row // ROWS, flat_row % ROWS : flat_row % ROWS + R1] = level_one[
+                    which, x, rows1
+                ]
+        start = 3 * tile_x1 * R1 // ROWS
+        for x in range(tile_x):
+            row = v_zero[x + 1, row0 : row0 + 1]
+            for chunk in range(chunks):
+                to[start + chunk, x : x + 1] = row[:, chunk * LANES : (chunk + 1) * LANES]
+    copy.wait()
 
 
 def reach_of(layer):
     return R1 + 1 - layer
 
 
-def middle(level_one, v_zero, from_near, from_far, window, near, far):
-    from_low, from_high = by_side("ty", from_near, from_far)
+def middle(level_one, v_zero, from_low, from_high, window, near, far):
     _, tile_x1, tile_y1, _ = level_one.shape
     planes, rows, size_z = v_zero.shape
     top1 = R1 + tile_y1
@@ -735,7 +769,7 @@
 
 
 def coarse_up(
-    counts, grids, blocks, window_one, one_near, one_far, row_near, row_far,
+    counts, grids, blocks, window_one, one_near, one_far, row_low, row_high,
     v_zero, forcing0, cx, cy, cz, weight, *rest,
 ):
     prepared, rest = rest[: len(grids)], rest[len(grids) :]
@@ -745,7 +779,6 @@
     ) = rest
     count_x, count_y = counts
     one_low, one_high = by_side("tx", one_near, one_far)
-    row_low, row_high = by_side("ty", row_near, row_far)
     _, tile_x1, rows1, size_z1 = window_one.shape
     tile_y1 = rows1 - 2 * R1
     top1 = R1 + tile_y1
@@ -872,21 +905,28 @@
 IN_PLACE = pl.BlockSpec(memory_space=pltpu.HBM)
 
 
-def call(kernel, operands, outputs, scratch, spec=VM):
+def call(kernel, operands, outputs, scratch, spec=VM, in_hbm=()):
     def typed(output):
         return output if isinstance(output, jax.ShapeDtypeStruct) else jax.ShapeDtypeStruct(output, F32)
 
     return pl.pallas_call(
         kernel,
         in_specs=[spec] * len(operands),
-        out_specs=[VM] * len(outputs),
+        out_specs=[IN_PLACE if n in in_hbm else VM for n in range(len(outputs))],
         out_shape=[typed(output) for output in outputs],
         scratch_shapes=[pltpu.VMEM(s, F32) if isinstance(s, tuple) else s for s in scratch],
         compiler_params=pltpu.CompilerParams(vmem_limit_bytes=24 * 1024 * 1024),
     )(*operands)
 
 
-def exchange(near, far, axis):
+def shift_both(to_low, to_high, axis):
+    count = lax.axis_size(axis)
+    from_low = lax.ppermute(to_high, axis, [(i, (i + 1) % count) for i in range(count)])
+    from_high = lax.ppermute(to_low, axis, [((i + 1) % count, i) for i in range(count)])
+    return from_low, from_high
+
+
+def swap_both(near, far, axis):
     count = lax.axis_size(axis)
     assert count % 2 == 0
     partner = [(i, i ^ 1) for i in range(count)]
@@ -907,7 +947,7 @@
     everyone = counts[0] * counts[1]
     rows = tile_y + 2 * RY
     message = (tile_x + 1, ROWS, size_z)
-    *inputs, near, far = call(
+    *inputs, to_low, to_high = call(
         edges,
         tuple(
             pltpu.with_memory_space_constraint(v, pltpu.HBM)
@@ -918,24 +958,26 @@
         (pltpu.SemaphoreType.DMA((3,)),),
         IN_PLACE,
     )
-    from_near, from_far = exchange(near, far, "ty")
-    message = (len(BASE_PLANES) + 1, tile_y, size_z)
-    window, near, far = call(
-        sides, (*inputs, from_near, from_far), ((3, tile_x, rows, size_z), message, message), ()
-    )
-    from_near, from_far = exchange(near, far, "tx")
-
+    from_low, from_high = shift_both(to_low, to_high, "ty")
     zero = (tile_x + 2 * RX, rows, size_z)
     inner = (tile_x + 2, rows, size_z)
     one_tile = (tile_x // 2, tile_y // 2, size_z // 2)
     two_tile = tuple(extent // 2 for extent in one_tile)
     grids = levels_of(counts, two_tile)
-    (kappa_blocks,) = call(
+    k_tile, kappa_blocks = call(
         shrink,
-        (window,),
-        ((everyone, two_tile[1], LANES),),
-        ((one_tile[0], rows, LANES), one_tile[1:]),
+        inputs[2:],
+        (one_tile, (everyone, two_tile[1], LANES)),
+        ((one_tile[0], tile_y, LANES), one_tile[1:]),
     )
+    message = (plane_tiles(tile_y), ROWS, size_z)
+    window, to_low, to_high = call(
+        sides,
+        (*inputs, k_tile, from_low, from_high),
+        ((3, tile_x, rows, size_z), message, message),
+        ((rows, size_z),),
+    )
+    from_low, from_high = shift_both(to_low, to_high, "tx")
     kappa_blocks = to_everyone(kappa_blocks)
 
     wide = -(-rows // (2 * ROWS)) * ROWS
@@ -945,34 +987,36 @@
     assert pairs1 // 2 * (two_tile[1] + RC) % SHORT == 0
     message = (3 * one_tile[0] * R1 // ROWS + chunks, ROWS, LANES)
     assert one_tile[2] == LANES and tile_x <= ROWS and one_tile[1] == ROWS
-    v_zero, forcing0, cx, cy, cz, weight, level_one, blocks, near, far = call(
+    v_zero, forcing0, cx, cy, cz, weight, level_one, blocks, to_low, to_high = call(
         fine_down,
-        (window, from_near, from_far),
+        (window, from_low, from_high),
         (inner, inner, (tile_x + 3, rows, size_z), inner, inner, inner)
         + ((3,) + one_tile, (everyone, short, SHORT, LANES), message, message),
         (
-            (6, rows, size_z),
             (4, rows, size_z),
-            (8, rows, size_z),
+            (2, rows, size_z),
+            (4, rows, size_z),
             zero,
             zero,
             (chunks, max(small[0], tile_x), 2 * wide, LANES),
-            (8, rows, size_z),
+            (everyone, short, SHORT, LANES),
+            pltpu.SemaphoreType.DMA,
         )
         + (small,) * 9
         + ((pairs1, wide, one_tile[2]), (pairs1, ROWS, one_tile[2])),
+        in_hbm=(7,),
     )
-    row_near, row_far = exchange(near, far, "ty")
+    row_low, row_high = shift_both(to_low, to_high, "ty")
     blocks = to_everyone(blocks)
     rows1 = one_tile[1] + 2 * R1
     message = (middle_tiles(tile_y, chunks), ROWS, LANES)
     window_one, near, far = call(
         middle,
-        (level_one, v_zero, row_near, row_far),
+        (level_one, v_zero, row_low, row_high),
         ((3, one_tile[0], rows1, one_tile[2]), message, message),
         (),
     )
-    one_near, one_far = exchange(near, far, "tx")
+    one_near, one_far = swap_both(near, far, "tx")
     lattice = grids[0].sizes[1], LANES
     prepared = call(
         functools.partial(prepare, counts, grids),
@@ -985,7 +1029,7 @@
     rim = (R1,) + one[1:]
     (updated,) = call(
         functools.partial(coarse_up, counts, grids),
-        (blocks, window_one, one_near, one_far, row_near, row_far)
+        (blocks, window_one, one_near, one_far, row_low, row_high)
         + (v_zero, forcing0, cx, cy, cz, weight, *prepared),
         (concentration.shape,),
         (rim,) * 6 + (one,) * 7 + (zero, zero),

time: 43.4 us -> 45.5 us (1.048)
  starting transfers between devices: 21.4 us -> 26 us
  waiting for transfers between devices: 9.49 us -> 6.87 us
    all_to_all x2, starting transfers between devices: 5.39 us -> 10.8 us  [to_everyone(): return lax.all_to_all(blocks, ('tx', 'ty'), 0, 0)]
    all_to_all x2, waiting for transfers between devices: 3.47 us -> 0.01 us  [to_everyone(): return lax.all_to_all(blocks, ('tx', 'ty'), 0, 0)]
    ppermute x8, waiting for transfers between devices: 6.02 us -> 6.87 us  [the longest x3 5.91 us: shift_both(): lax.ppermute(to_high, axis, [(i, (i + 1) % count) for i in range(count)])]
    ppermute x8, starting transfers between devices: 16.1 us -> 15.3 us  [the longest x3 6.43 us: shift_both(): lax.ppermute(to_low, axis, [((i + 1) % count, i) for i in range(count)])]
  transfers between devices with their start and end apart: 10 -> 10, of which waited for: 5 -> 3; matrix products, arithmetic and copies ran while one was open for 0% -> 0% of each run, Pallas kernels for 16% -> 16%
where the time goes in v3:
time: 45.5 us; the launch traced here: 45.2 us
  starting transfers between devices  26 us (57%)
  Pallas kernels  12.2 us (27%)
  waiting for transfers between devices  6.87 us (15%)
    pallas_call x7, Pallas kernels, call(): pl.pallas_call(kernel, in_specs=[spec] * len(operands), out_specs=[IN_PLA...  12.2 us
    all_to_all x2, starting transfers between devices, to_everyone(): return lax.all_to_all(blocks, ('tx', 'ty'), 0, 0)  10.8 us
    ppermute x3, starting transfers between devices, shift_both(): lax.ppermute(to_low, axis, [((i + 1) % count, i) for i in range(count)])  6.43 us
    ppermute x3, waiting for transfers between devices, shift_both(): lax.ppermute(to_high, axis, [(i, (i + 1) % count) for i in range(count)])  5.91 us
    ppermute x1, starting transfers between devices, swap_both(): from_far = lax.ppermute(far, axis, other)  4.16 us
    ppermute x3, starting transfers between devices, shift_both(): lax.ppermute(to_high, axis, [(i, (i + 1) % count) for i in range(count)])  2.67 us
    ppermute x1, starting transfers between devices, swap_both(): from_near = lax.ppermute(near, axis, partner)  2.03 us
    ppermute x3, waiting for transfers between devices, shift_both(): lax.ppermute(to_low, axis, [((i + 1) % count, i) for i in range(count)])  0.95 us
  transfers between devices with their start and end apart: 10, of which 3 were waited for; matrix products, arithmetic and copies ran while one was open for 0% of the time, Pallas kernels for 16%

profile of v3, /device:TPU:0, one launch (start us, length us, event | category | flops | bytes accessed | tf_op | source)
XLA Modules:
  0.0 45.2 jit_solution(11822170542284850024)
XLA Ops:
  0.0 1.2 %shard_map.37 = (f32[8,16,256]{2,1,0:T(8,128)S(1)}, f32[8,16,256]{2,1,0:T(8,128)S(1)}, s32[8,16,256]{2,1,0:T(8,128)S(1)}, f32[9,8,256]{2,1,0:T(8,128)S(1)}, f32[9,8,256]{2,1,0:T(8,128)S(1)}) custom-call(f32[8,16,256]{2,1,0:T(8,128)} %conc_in.1, f32[8,16,256]{2,1,0:T(8,128)} %source_in.1, s32[8,16,256]{2,1,0:T(8,128)} %material_in.1), custom_call_target="tpu_custom_call" | custom-call | tf_op jit(solution)/shard_map/pallas_call | solution.py:912
  1.2 0.5 %collective-permute-start = (f32[9,8,256]{2,1,0:T(8,128)S(1)}, f32[9,8,256]{2,1,0:T(8,128)S(1)}, u32[]{:S(2)}, u32[]{:S(2)}) collective-permute-start(f32[9,8,256]{2,1,0:T(8,128)S(1)} %get-tuple-element.36), channel_id=1, source_target_pairs={{0,1},{1,2},{2,3},{3,0},{4,5},{5,6},{6,7},{7,4},{8,9},{9,10},{10,1... | collective-permute-start | bytes 221192 | tf_op jit(solution)/shard_map/ppermute | solution.py:924
  1.7 2.0 %collective-permute-start.1 = (f32[9,8,256]{2,1,0:T(8,128)S(1)}, f32[9,8,256]{2,1,0:T(8,128)S(1)}, u32[]{:S(2)}, u32[]{:S(2)}) collective-permute-start(f32[9,8,256]{2,1,0:T(8,128)S(1)} %get-tuple-element.37), channel_id=1, source_target_pairs={{1,0},{2,1},{3,2},{0,3},{5,4},{6,5},{7,6},{4,7},{9,8},{10,9},{11,1... | collective-permute-start | bytes 221192 | tf_op jit(solution)/shard_map/ppermute | solution.py:925
  3.7 1.1 %shard_map.38 = (f32[4,8,128]{2,1,0:T(8,128)S(1)}, f32[32,4,128]{2,1,0:T(4,128)}) custom-call(s32[8,16,256]{2,1,0:T(8,128)S(1)} %get-tuple-element.34.material), custom_call_target="tpu_custom_call" | custom-call | tf_op jit(solution)/shard_map/pallas_call | solution.py:912
  4.8 6.6 %all-to-all-start.1 = ((f32[32,4,128]{2,1,0:T(4,128)}), f32[32,4,128]{2,1,0:T(4,128)S(1)}, u32[]{:S(2)}, u32[]{:S(2)}) async-start(f32[32,4,128]{2,1,0:T(4,128)} %get-tuple-element.54), calls=%async_computation.1 | async-start | bytes 131072 | tf_op jit(solution)/shard_map/all_to_all | solution.py:940
  11.4 0.0 collective-permute-done.from_low
  11.5 0.0 collective-permute-done.1.from_high
  11.5 0.3 shard_map.39
  11.8 1.8 %collective-permute-start.2 = (f32[15,8,256]{2,1,0:T(8,128)S(1)}, f32[15,8,256]{2,1,0:T(8,128)S(1)}, u32[]{:S(2)}, u32[]{:S(2)}) collective-permute-start(f32[15,8,256]{2,1,0:T(8,128)S(1)} %get-tuple-element.39), channel_id=1, source_target_pairs={{0,4},{4,8},{8,12},{12,16},{16,20},{20,24},{24,28},{28,0},{1,5},{5... | collective-permute-start | bytes 368648 | tf_op jit(solution)/shard_map/ppermute | solution.py:924
  13.6 3.0 %collective-permute-start.3 = (f32[15,8,256]{2,1,0:T(8,128)S(1)}, f32[15,8,256]{2,1,0:T(8,128)S(1)}, u32[]{:S(2)}, u32[]{:S(2)}) collective-permute-start(f32[15,8,256]{2,1,0:T(8,128)S(1)} %get-tuple-element.40), channel_id=1, source_target_pairs={{4,0},{8,4},{12,8},{16,12},{20,16},{24,20},{28,24},{0,28},{5,1},{9... | collective-permute-start | bytes 368648 | tf_op jit(solution)/shard_map/ppermute | solution.py:925
  16.6 4.2 %collective-permute-done.2.from_low = f32[15,8,256]{2,1,0:T(8,128)S(1)} collective-permute-done((f32[15,8,256]{2,1,0:T(8,128)S(1)}, f32[15,8,256]{2,1,0:T(8,128)S(1)}, u32[]{:S(2)}, u32[]{:S(2)}) %collective-permute-start.2) | collective-permute-done | bytes 122912 | tf_op jit(solution)/shard_map/ppermute | solution.py:924
  20.8 0.9 %collective-permute-done.3.from_high = f32[15,8,256]{2,1,0:T(8,128)S(1)} collective-permute-done((f32[15,8,256]{2,1,0:T(8,128)S(1)}, f32[15,8,256]{2,1,0:T(8,128)S(1)}, u32[]{:S(2)}, u32[]{:S(2)}) %collective-permute-start.3) | collective-permute-done | bytes 122912 | tf_op jit(solution)/shard_map/ppermute | solution.py:925
  21.7 2.4 %shard_map.40 = (f32[10,24,256]{2,1,0:T(8,128)S(1)}, f32[10,24,256]{2,1,0:T(8,128)S(1)}, f32[11,24,256]{2,1,0:T(8,128)S(1)}, f32[10,24,256]{2,1,0:T(8,128)S(1)},...) custom-call(f32[3,8,24,256]{3,2,1,0:T(8,128)S(1)} %get-tuple-element, ...), custom_call_target="tpu_custom_call" | custom-call | tf_op jit(solution)/shard_map/pallas_call | solution.py:912
  24.2 0.0 all-to-all-done.1.blocks
  24.2 4.2 %all-to-all-start = ((f32[32,3,4,128]{3,2,1,0:T(4,128)}), f32[32,3,4,128]{3,2,1,0:T(4,128)S(1)}, u32[]{:S(2)}, u32[]{:S(2)}) async-start(f32[32,3,4,128]{3,2,1,0:T(4,128)} %get-tuple-element.41), calls=%async_computation | async-start | bytes 393216 | tf_op jit(solution)/shard_map/all_to_all | solution.py:940
  28.3 0.3 collective-permute-start.4
  28.6 1.5 %collective-permute-start.5 = (f32[8,8,128]{2,1,0:T(8,128)S(1)}, f32[8,8,128]{2,1,0:T(8,128)S(1)}, u32[]{:S(2)}, u32[]{:S(2)}) collective-permute-start(f32[8,8,128]{2,1,0:T(8,128)S(1)} %get-tuple-element.45), channel_id=1, source_target_pairs={{1,0},{2,1},{3,2},{0,3},{5,4},{6,5},{7,6},{4,7},{9,8},{10,9},{11,1... | collective-permute-start | bytes 98312 | tf_op jit(solution)/shard_map/ppermute | solution.py:925
  30.1 1.7 %collective-permute-done.4.from_low.row_low = f32[8,8,128]{2,1,0:T(8,128)S(1)} collective-permute-done((f32[8,8,128]{2,1,0:T(8,128)S(1)}, f32[8,8,128]{2,1,0:T(8,128)S(1)}, u32[]{:S(2)}, u32[]{:S(2)}) %collective-permute-start.4) | collective-permute-done | bytes 32800 | tf_op jit(solution)/shard_map/ppermute | solution.py:924
  31.8 0.0 collective-permute-done.5.from_high.row_high
  31.8 0.1 shard_map.41
  31.9 2.0 %collective-permute-start.6 = (f32[18,8,128]{2,1,0:T(8,128)S(1)}, f32[18,8,128]{2,1,0:T(8,128)S(1)}, u32[]{:S(2)}, u32[]{:S(2)}) collective-permute-start(f32[18,8,128]{2,1,0:T(8,128)S(1)} %get-tuple-element.47), channel_id=1, source_target_pairs={{0,4},{4,0},{8,12},{12,8},{16,20},{20,16},{24,28},{28,24},{1,5},{5... | collective-permute-start | bytes 221192 | tf_op jit(solution)/shard_map/ppermute | solution.py:935
  33.9 4.2 %collective-permute-start.7 = (f32[18,8,128]{2,1,0:T(8,128)S(1)}, f32[18,8,128]{2,1,0:T(8,128)S(1)}, u32[]{:S(2)}, u32[]{:S(2)}) collective-permute-start(f32[18,8,128]{2,1,0:T(8,128)S(1)} %get-tuple-element.48), channel_id=1, source_target_pairs={{0,28},{4,8},{8,4},{12,16},{16,12},{20,24},{24,20},{28,0},{1,29},{... | collective-permute-start | bytes 221192 | tf_op jit(solution)/shard_map/ppermute | solution.py:934
  38.1 3.2 %shard_map.42 = (f32[5,16,16,128]{3,2,1,0:T(8,128)S(1)}, f32[5,8,16,128]{3,2,1,0:T(8,128)S(1)}, f32[5,4,16,128]{3,2,1,0:T(8,128)S(1)}, f32[32,128]{1,0:T(8,128)S(1)}) custom-call(f32[32,4,128]{2,1,0:T(4,128)S(1)} %all-to-all-done.1.blocks, f32[3,4,16,128]{3,2,1,0:T(8,128)S(1)} %get-tuple-element.46._.window_one), custom_call_target="tpu_custom_call" | custom-call | tf_op jit(solution)/shard_map/pallas_call | solution.py:912
  41.3 0.0 collective-permute-done.6.one_near
  41.3 0.0 collective-permute-done.7.one_far
  41.3 0.0 all-to-all-done.blocks
  41.3 3.9 %shard_map.43 = f32[8,16,256]{2,1,0:T(8,128)} custom-call(f32[32,3,4,128]{3,2,1,0:T(4,128)S(1)} %all-to-all-done.blocks, f32[3,4,16,128]{3,2,1,0:T(8,128)S(1)} %get-tuple-element.46._.window_one, f32[18,8,128]{2,1,0:T(8,128)S(1)} %collective-permute-done.6.one_near, f32[18,8,128]{2,1,0:T(8,128)S(1)} %collective-permute-done.7.one_far, ...), custom_call_target="tpu_custom_call" | custom-call | tf_op jit(solution)/shard_map/pallas_call | solution.py:912
Async XLA Ops:
  1.2 10.3 %collective-permute-start = (f32[9,8,256]{2,1,0:T(8,128)S(1)}, f32[9,8,256]{2,1,0:T(8,128)S(1)}, u32[]{:S(2)}, u32[]{:S(2)}) collective-permute-start(f32[9,8,256]{2,1,0:T(8,128)S(1)} %get-tuple-element.36), channel_id=1, source_target_pairs={{0,1},{1,2},{2,3},{3,0},{4,5},{5,6},{6,7},{7,4},{8,9},{9,10},{10,1... | collective-permute-start | bytes 221192 | tf_op jit(solution)/shard_map/ppermute | solution.py:924
  1.7 9.7 %collective-permute-start.1 = (f32[9,8,256]{2,1,0:T(8,128)S(1)}, f32[9,8,256]{2,1,0:T(8,128)S(1)}, u32[]{:S(2)}, u32[]{:S(2)}) collective-permute-start(f32[9,8,256]{2,1,0:T(8,128)S(1)} %get-tuple-element.37), channel_id=1, source_target_pairs={{1,0},{2,1},{3,2},{0,3},{5,4},{6,5},{7,6},{4,7},{9,8},{10,9},{11,1... | collective-permute-start | bytes 221192 | tf_op jit(solution)/shard_map/ppermute | solution.py:925
  4.8 19.3 %all-to-all-start.1 = ((f32[32,4,128]{2,1,0:T(4,128)}), f32[32,4,128]{2,1,0:T(4,128)S(1)}, u32[]{:S(2)}, u32[]{:S(2)}) async-start(f32[32,4,128]{2,1,0:T(4,128)} %get-tuple-element.54), calls=%async_computation.1 | async-start | bytes 131072 | tf_op jit(solution)/shard_map/all_to_all | solution.py:940
  11.8 9.0 %collective-permute-start.2 = (f32[15,8,256]{2,1,0:T(8,128)S(1)}, f32[15,8,256]{2,1,0:T(8,128)S(1)}, u32[]{:S(2)}, u32[]{:S(2)}) collective-permute-start(f32[15,8,256]{2,1,0:T(8,128)S(1)} %get-tuple-element.39), channel_id=1, source_target_pairs={{0,4},{4,8},{8,12},{12,16},{16,20},{20,24},{24,28},{28,0},{1,5},{5... | collective-permute-start | bytes 368648 | tf_op jit(solution)/shard_map/ppermute | solution.py:924
  13.6 8.1 %collective-permute-start.3 = (f32[15,8,256]{2,1,0:T(8,128)S(1)}, f32[15,8,256]{2,1,0:T(8,128)S(1)}, u32[]{:S(2)}, u32[]{:S(2)}) collective-permute-start(f32[15,8,256]{2,1,0:T(8,128)S(1)} %get-tuple-element.40), channel_id=1, source_target_pairs={{4,0},{8,4},{12,8},{16,12},{20,16},{24,20},{28,24},{0,28},{5,1},{9... | collective-permute-start | bytes 368648 | tf_op jit(solution)/shard_map/ppermute | solution.py:925
  24.2 17.2 %all-to-all-start = ((f32[32,3,4,128]{3,2,1,0:T(4,128)}), f32[32,3,4,128]{3,2,1,0:T(4,128)S(1)}, u32[]{:S(2)}, u32[]{:S(2)}) async-start(f32[32,3,4,128]{3,2,1,0:T(4,128)} %get-tuple-element.41), calls=%async_computation | async-start | bytes 393216 | tf_op jit(solution)/shard_map/all_to_all | solution.py:940
  28.3 3.5 %collective-permute-start.4 = (f32[8,8,128]{2,1,0:T(8,128)S(1)}, f32[8,8,128]{2,1,0:T(8,128)S(1)}, u32[]{:S(2)}, u32[]{:S(2)}) collective-permute-start(f32[8,8,128]{2,1,0:T(8,128)S(1)} %get-tuple-element.44), channel_id=1, source_target_pairs={{0,1},{1,2},{2,3},{3,0},{4,5},{5,6},{6,7},{7,4},{8,9},{9,10},{10,1... | collective-permute-start | bytes 98312 | tf_op jit(solution)/shard_map/ppermute | solution.py:924
  28.6 3.2 %collective-permute-start.5 = (f32[8,8,128]{2,1,0:T(8,128)S(1)}, f32[8,8,128]{2,1,0:T(8,128)S(1)}, u32[]{:S(2)}, u32[]{:S(2)}) collective-permute-start(f32[8,8,128]{2,1,0:T(8,128)S(1)} %get-tuple-element.45), channel_id=1, source_target_pairs={{1,0},{2,1},{3,2},{0,3},{5,4},{6,5},{7,6},{4,7},{9,8},{10,9},{11,1... | collective-permute-start | bytes 98312 | tf_op jit(solution)/shard_map/ppermute | solution.py:925
  31.9 9.4 %collective-permute-start.6 = (f32[18,8,128]{2,1,0:T(8,128)S(1)}, f32[18,8,128]{2,1,0:T(8,128)S(1)}, u32[]{:S(2)}, u32[]{:S(2)}) collective-permute-start(f32[18,8,128]{2,1,0:T(8,128)S(1)} %get-tuple-element.47), channel_id=1, source_target_pairs={{0,4},{4,0},{8,12},{12,8},{16,20},{20,16},{24,28},{28,24},{1,5},{5... | collective-permute-start | bytes 221192 | tf_op jit(solution)/shard_map/ppermute | solution.py:935
  33.9 7.4 %collective-permute-start.7 = (f32[18,8,128]{2,1,0:T(8,128)S(1)}, f32[18,8,128]{2,1,0:T(8,128)S(1)}, u32[]{:S(2)}, u32[]{:S(2)}) collective-permute-start(f32[18,8,128]{2,1,0:T(8,128)S(1)} %get-tuple-element.48), channel_id=1, source_target_pairs={{0,28},{4,8},{8,4},{12,16},{16,12},{20,24},{24,20},{28,0},{1,29},{... | collective-permute-start | bytes 221192 | tf_op jit(solution)/shard_map/ppermute | solution.py:934

commit v4 on v3

--- a/solution.py
+++ b/solution.py
@@ -104,11 +104,6 @@
 
 def times_right(x, selector):
     parts = [jnp.dot(part, selector, preferred_element_type=F32) for part in three_terms(x)]
-    return parts[0] + (parts[1] + parts[2])
-
-
-def times_left(selector, x):
-    parts = [jnp.dot(selector, part, preferred_element_type=F32) for part in three_terms(x)]
     return parts[0] + (parts[1] + parts[2])
 
 
@@ -256,7 +251,7 @@
     return (len(BASE_PLANES) + 1) * tile_y // ROWS + -(-loose // ROWS) + 1
 
 
-def shrink(material, k_tile, blocks, paired, paired_one):
+def shrink(material, k_tile, k_two, halves, halves_one, paired, paired_one):
     tile_x, tile_y, size_z = material.shape
     tile_x1, tile_y1, size_z1 = tile_x // 2, tile_y // 2, size_z // 2
     k_one = None
@@ -288,12 +283,15 @@
         part = times_right(piece, halve_lanes(size_z1, LANES, pair * size_z1 // 2))
         block = part if block is None else block + part
     block = 0.125 * block
-    for device in range(blocks.shape[0]):
-        blocks[device] = block
+    k_two[...] = block
+    for chunk in range(size_z // LANES):
+        halves[chunk] = halve_lanes(LANES, size_z1, chunk * LANES // 2)
+    for half in range(2):
+        halves_one[half] = halve_lanes(size_z1, size_z1, half * size_z1 // 2)
 
 
 def fine_down(
-    window, from_low, from_high,
+    window, k_two, halves, halves_one, from_low, from_high,
     v_zero, forcing_out, cx, cy, cz, weight, level_one, blocks_out, to_low, to_high,
     conc_rim, forcing_rim, kappa_rim, once, diag, paired, blocks, left,
     k_one, f_one, u_one, v_one, cx1, cy1, cz1, w1, d1, paired_one, packed,
@@ -350,7 +348,7 @@
     plane_sweep(once, v_out, forcing, cx, cy, cz, weight, 1, planes - 1)
     chunks = size_z // LANES
     size_z1 = size_z // 2
-    to_half = [halve_lanes(LANES, size_z1, chunk * LANES // 2) for chunk in range(chunks)]
+    to_half = [halves[chunk] for chunk in range(chunks)]
     tile_x1, tile_y1 = tile_x // 2, tile_y // 2
 
     def put(pair, total):
@@ -427,15 +425,17 @@
         )
     half_pairs = pairs1 // 2
     result = times_right(
-        jnp.concatenate([packed[p] for p in range(half_pairs)], 0), halve_lanes(size_z1, size_z1)
+        jnp.concatenate([packed[p] for p in range(half_pairs)], 0), halves_one[0]
     ) + times_right(
-        jnp.concatenate([packed[half_pairs + p] for p in range(half_pairs)], 0),
-        halve_lanes(size_z1, size_z1, size_z1 // 2),
+        jnp.concatenate([packed[half_pairs + p] for p in range(half_pairs)], 0), halves_one[1]
     )
     used = tile_y1 // 2 + RC
     block = jnp.concatenate([result[p * ROWS : p * ROWS + used] for p in range(half_pairs)], 0)
     block = 0.125 * block
-    for part in range(blocks.shape[1]):
+    k_block = k_two[...]
+    for device in range(blocks.shape[0]):
+        blocks[device, blocks.shape[1] - 1] = k_block
+    for part in range(blocks.shape[1] - 1):
         piece = block[part * SHORT : (part + 1) * SHORT]
         for device in range(blocks.shape[0]):
             blocks[device, part] = piece
@@ -681,41 +681,64 @@
     return grids
 
 
-class Operator:
-    def __init__(self, ref):
-        self.ref = ref
-
-    def __getitem__(self, part):
-        if isinstance(part, slice):
-            return [self.ref[p] for p in range(*part.indices(5))]
-        return self.ref[part]
-
-
-def prepare(counts, grids, blocks, _, *outputs):
+def kappa_of(blocks, counts, grid):
     count_x, count_y = counts
-    planes, rows, _ = grids[0].sizes
+    planes, rows, size_z2 = grid.sizes
     half_x, half_y = planes // count_x, rows // count_y
-    size_z2 = grids[0].sizes[2]
-    assert half_x * size_z2 == LANES and half_x == 2 and ROWS % half_y == 0
+    assert half_x * size_z2 == LANES and half_x == 2 and ROWS % half_y == 0 and half_y == SHORT
     share = ROWS // half_y
     kappa = [[None] * (rows // ROWS) for _ in range(planes)]
     lane = iota((ROWS, LANES), 1)
+    at = blocks.shape[1] - 1
     for tx in range(count_x):
         for group in range(rows // ROWS):
-            pieces = [blocks[tx * count_y + group * share + n] for n in range(share)]
+            pieces = [blocks[tx * count_y + group * share + n, at] for n in range(share)]
             piece = jnp.concatenate(pieces, 0)
             turned = pltpu.roll(piece, size_z2, 1)
             for p in range(half_x):
                 mine = (lane < size_z2) == (p == 0)
                 kappa[tx * half_x + p][group] = jnp.where(mine, piece, turned)
-    kappa = jnp.concatenate([jnp.concatenate(groups, 0)[None] for groups in kappa], 0)
+    return jnp.concatenate([jnp.concatenate(groups, 0)[None] for groups in kappa], 0)
+
+
+def prepare(kappa, grids):
     kappas = [kappa]
     for grid in grids[:-1]:
         kappas.append(restrict_whole(kappas[-1], grid))
-    outputs[-1][...] = ExactSolve(grids[-1], kappas[-1]).inverse
-    for number, grid in enumerate(grids[:-1]):
-        for part, value in enumerate(whole_operator(kappas[number], grid)):
-            outputs[number][part] = value
+    exact = ExactSolve(grids[-1], kappas[-1])
+    return [(grid, whole_operator(k, grid)) for grid, k in zip(grids[:-1], kappas)], exact
+
+
+def selectors(sizes, planes1, tile_x1, tile_y1, rows, _, left_one, right_one, left_zero, right_zero):
+    rows1 = tile_y1 + 2 * R1
+    whole_x1, whole_y1 = 2 * sizes[0], 2 * sizes[1]
+    start_x = lax.axis_index("tx") * tile_x1 + (whole_x1 - R1)
+    start_y = lax.axis_index("ty") * tile_y1 + (whole_y1 - R1)
+    row = iota((planes1 * rows1, 1), 0)
+    at_x = mod(div(row, rows1) + start_x, whole_x1)
+    at_y = mod(mod(row, rows1) + start_y, whole_y1)
+    target = div(at_x, 2) * sizes[1] + div(at_y, 2)
+    left_one[...] = ones_where(iota(left_one.shape, 1) == target)
+    shape = right_one.shape
+    right_one[...] = ones_where(iota(shape, 0) == div(iota(shape, 1), 2))
+    row = iota((left_zero.shape[0], 1), 0)
+    target = div(row, rows) * rows1 + div(mod(row, rows) + (2 * R1 - RY), 2)
+    left_zero[...] = ones_where(iota(left_zero.shape, 1) == target)
+    shape = right_zero.shape
+    right_zero[...] = ones_where(iota(shape, 0) == div(iota(shape, 1), 2))
+
+
+def raise_level(left, right, v):
+    def terms(x):
+        high = x.astype(BF16)
+        return high, (x - high.astype(F32)).astype(BF16)
+
+    high, low = terms(v)
+    picked = jnp.dot(left, high, preferred_element_type=F32)
+    picked_low = jnp.dot(left, low, preferred_element_type=F32)
+    return jnp.dot(picked.astype(BF16), right, preferred_element_type=F32) + jnp.dot(
+        picked_low.astype(BF16), right, preferred_element_type=F32
+    )
 
 
 def solve_whole(forcing, levels, exact):
@@ -770,9 +793,8 @@
 
 def coarse_up(
     counts, grids, blocks, window_one, one_near, one_far, row_low, row_high,
-    v_zero, forcing0, cx, cy, cz, weight, *rest,
+    v_zero, forcing0, cx, cy, cz, weight, left_one, right_one, left_zero, right_zero, *rest,
 ):
-    prepared, rest = rest[: len(grids)], rest[len(grids) :]
     (
         out, mixed_low, mixed_high, kappa_low, kappa_high, first_low, first_high,
         v_one, cx1, cy1, cz1, w1, one_a, one_b, zero_a, zero_b,
@@ -785,10 +807,7 @@
     half_x, half_y, size_z2 = tile_x1 // 2, tile_y1 // 2, size_z1 // 2
     sizes = grids[0].sizes
     forcing2 = assemble(blocks, count_x, count_y, half_x, half_y, size_z2)
-    levels = [
-        (grid, Operator(prepared[number])) for number, grid in enumerate(grids[:-1])
-    ]
-    exact = ExactSolve(grids[-1], inverse=prepared[-1][...])
+    levels, exact = prepare(kappa_of(blocks, counts, grids[0]), grids)
 
     planes1 = tile_x1 + 2 * R1
     for message, mixed, kappa_rim, low in (
@@ -834,17 +853,7 @@
     solved = solve_whole(forcing2, levels, exact)
     solved = solved.reshape(sizes[0] * sizes[1], LANES)
 
-    whole_x1, whole_y1 = 2 * sizes[0], 2 * sizes[1]
-    start_x = lax.axis_index("tx") * tile_x1 + (whole_x1 - R1)
-    start_y = lax.axis_index("ty") * tile_y1 + (whole_y1 - R1)
-    row = iota((planes1 * rows1, 1), 0)
-    at_x = mod(div(row, rows1) + start_x, whole_x1)
-    at_y = mod(mod(row, rows1) + start_y, whole_y1)
-    target = div(at_x, 2) * sizes[1] + div(at_y, 2)
-    left = ones_where(iota((planes1 * rows1, sizes[0] * sizes[1]), 1) == target)
-    shape = (LANES, size_z1)
-    right = ones_where(iota(shape, 0) == div(iota(shape, 1), 2))
-    raised = times_right(times_left(left, solved), right)
+    raised = raise_level(left_one[...], right_one[...], solved)
     for x in range(1, planes1 - 1):
         one_a[x] = v_one[x] + raised[x * rows1 : (x + 1) * rows1]
     plane_sweep(one_a, one_b, forcing1, cx1, cy1, cz1, w1, 2, planes1 - 2)
@@ -855,14 +864,7 @@
     cx, cy, cz, weight = kept(cx, RX - 2), kept(cy, RX - 1), kept(cz, RX - 1), kept(weight, RX - 1)
     first, last = R1 - 1, planes1 - R1 + 1
     stack = jnp.concatenate([one_a[x] for x in range(first, last)], 0)
-    count = last - first
-    shape = (count * rows, count * rows1)
-    out_row, in_row = iota((count * rows, 1), 0), iota(shape, 1)
-    target = div(out_row, rows) * rows1 + div(mod(out_row, rows) + (2 * R1 - RY), 2)
-    left = ones_where(in_row == target)
-    shape = (size_z1, size_z)
-    right = ones_where(iota(shape, 0) == div(iota(shape, 1), 2))
-    raised = times_right(times_left(left, stack), right)
+    raised = raise_level(left_zero[...], right_zero[...], stack)
     chunks = size_z // LANES
     top = rows - RY
     for x in range(RX - 1, planes - RX + 1):
@@ -964,10 +966,19 @@
     one_tile = (tile_x // 2, tile_y // 2, size_z // 2)
     two_tile = tuple(extent // 2 for extent in one_tile)
     grids = levels_of(counts, two_tile)
-    k_tile, kappa_blocks = call(
+
+    def bits(*shape):
+        return jax.ShapeDtypeStruct(shape, BF16)
+
+    k_tile, k_two, halves, halves_one = call(
         shrink,
         inputs[2:],
-        (one_tile, (everyone, two_tile[1], LANES)),
+        (
+            one_tile,
+            (two_tile[1], LANES),
+            bits(chunks, LANES, one_tile[2]),
+            bits(2, one_tile[2], one_tile[2]),
+        ),
         ((one_tile[0], tile_y, LANES), one_tile[1:]),
     )
     message = (plane_tiles(tile_y), ROWS, size_z)
@@ -978,18 +989,16 @@
         ((rows, size_z),),
     )
     from_low, from_high = shift_both(to_low, to_high, "tx")
-    kappa_blocks = to_everyone(kappa_blocks)
-
     wide = -(-rows // (2 * ROWS)) * ROWS
     small = (one_tile[0] + 2 * RC, wide, one_tile[2])
     pairs1 = small[0] // 2
-    short = pairs1 // 2 * (two_tile[1] + RC) // SHORT
+    short = pairs1 // 2 * (two_tile[1] + RC) // SHORT + 1
     assert pairs1 // 2 * (two_tile[1] + RC) % SHORT == 0
     message = (3 * one_tile[0] * R1 // ROWS + chunks, ROWS, LANES)
     assert one_tile[2] == LANES and tile_x <= ROWS and one_tile[1] == ROWS
     v_zero, forcing0, cx, cy, cz, weight, level_one, blocks, to_low, to_high = call(
         fine_down,
-        (window, from_low, from_high),
+        (window, k_two, halves, halves_one, from_low, from_high),
         (inner, inner, (tile_x + 3, rows, size_z), inner, inner, inner)
         + ((3,) + one_tile, (everyone, short, SHORT, LANES), message, message),
         (
@@ -1017,20 +1026,24 @@
         (),
     )
     one_near, one_far = swap_both(near, far, "tx")
-    lattice = grids[0].sizes[1], LANES
-    prepared = call(
-        functools.partial(prepare, counts, grids),
-        (kappa_blocks, window_one),
-        tuple((5, grid.sizes[0]) + lattice for grid in grids[:-1])
-        + ((-(-grids[-1].cells // ROWS) * ROWS, LANES),),
+    one = (one_tile[0] + 2 * R1, rows1, one_tile[2])
+    seen = one[0] - 2 * (R1 - 1)
+    chosen = call(
+        functools.partial(selectors, grids[0].sizes, one[0], one_tile[0], one_tile[1], rows),
+        (window_one,),
+        (
+            bits(one[0] * rows1, grids[0].sizes[0] * grids[0].sizes[1]),
+            bits(LANES, one_tile[2]),
+            bits(seen * rows, seen * rows1),
+            bits(one_tile[2], size_z),
+        ),
         (),
     )
-    one = (one_tile[0] + 2 * R1, rows1, one_tile[2])
     rim = (R1,) + one[1:]
     (updated,) = call(
         functools.partial(coarse_up, counts, grids),
         (blocks, window_one, one_near, one_far, row_low, row_high)
-        + (v_zero, forcing0, cx, cy, cz, weight, *prepared),
+        + (v_zero, forcing0, cx, cy, cz, weight, *chosen),
         (concentration.shape,),
         (rim,) * 6 + (one,) * 7 + (zero, zero),
     )

time: 45.5 us -> 43.2 us (0.949)
  starting transfers between devices: 26 us -> 20 us
  waiting for transfers between devices: 6.87 us -> 12 us
  Pallas kernels: 12.2 us -> 10.9 us
    all_to_all x2 -> x1, starting transfers between devices: 10.8 us -> 4.5 us  [to_everyone(): return lax.all_to_all(blocks, ('tx', 'ty'), 0, 0)]
    ppermute x1, waiting for transfers between devices: 0.01 us -> 2.66 us  [swap_both(): from_far = lax.ppermute(far, axis, other)]
    ppermute x3, waiting for transfers between devices: 0.95 us -> 2.68 us  [shift_both(): lax.ppermute(to_low, axis, [((i + 1) % count, i) for i in range(count)])]
    pallas_call x7, Pallas kernels: 12.2 us -> 10.9 us  [call(): pl.pallas_call(kernel, in_specs=[spec] * len(operands), out_specs=[IN_PLA...]
    ppermute x3, waiting for transfers between devices: 5.91 us -> 6.63 us  [shift_both(): lax.ppermute(to_high, axis, [(i, (i + 1) % count) for i in range(count)])]
  transfers between devices with their start and end apart: 10 -> 9, of which waited for: 3 -> 6; matrix products, arithmetic and copies ran while one was open for 0% -> 0% of each run, Pallas kernels for 16% -> 2%
where the time goes in v4:
time: 43.2 us; the launch traced here: 42.9 us
  starting transfers between devices  20 us (46%)
  waiting for transfers between devices  12 us (28%)
  Pallas kernels  10.9 us (25%)
    pallas_call x7, Pallas kernels, call(): pl.pallas_call(kernel, in_specs=[spec] * len(operands), out_specs=[IN_PLA...  10.9 us
    ppermute x3, waiting for transfers between devices, shift_both(): lax.ppermute(to_high, axis, [(i, (i + 1) % count) for i in range(count)])  6.63 us
    ppermute x3, starting transfers between devices, shift_both(): lax.ppermute(to_low, axis, [((i + 1) % count, i) for i in range(count)])  6.58 us
    all_to_all x1, starting transfers between devices, to_everyone(): return lax.all_to_all(blocks, ('tx', 'ty'), 0, 0)  4.5 us
    ppermute x1, starting transfers between devices, swap_both(): from_far = lax.ppermute(far, axis, other)  4.39 us
    ppermute x3, waiting for transfers between devices, shift_both(): lax.ppermute(to_low, axis, [((i + 1) % count, i) for i in range(count)])  2.68 us
    ppermute x1, waiting for transfers between devices, swap_both(): from_far = lax.ppermute(far, axis, other)  2.66 us
    ppermute x3, starting transfers between devices, shift_both(): lax.ppermute(to_high, axis, [(i, (i + 1) % count) for i in range(count)])  2.62 us
  transfers between devices with their start and end apart: 9, of which 6 were waited for; matrix products, arithmetic and copies ran while one was open for 0% of the time, Pallas kernels for 2%

profile of v4, /device:TPU:0, one launch (start us, length us, event | category | flops | bytes accessed | tf_op | source)
XLA Modules:
  0.0 42.9 jit_solution(2227895995139412133)
XLA Ops:
  0.0 1.2 %shard_map.37 = (f32[8,16,256]{2,1,0:T(8,128)S(1)}, f32[8,16,256]{2,1,0:T(8,128)S(1)}, s32[8,16,256]{2,1,0:T(8,128)S(1)}, f32[9,8,256]{2,1,0:T(8,128)S(1)}, f32[9,8,256]{2,1,0:T(8,128)S(1)}) custom-call(f32[8,16,256]{2,1,0:T(8,128)} %conc_in.1, f32[8,16,256]{2,1,0:T(8,128)} %source_in.1, s32[8,16,256]{2,1,0:T(8,128)} %material_in.1), custom_call_target="tpu_custom_call" | custom-call | tf_op jit(solution)/shard_map/pallas_call | solution.py:914
  1.2 0.5 %collective-permute-start = (f32[9,8,256]{2,1,0:T(8,128)S(1)}, f32[9,8,256]{2,1,0:T(8,128)S(1)}, u32[]{:S(2)}, u32[]{:S(2)}) collective-permute-start(f32[9,8,256]{2,1,0:T(8,128)S(1)} %get-tuple-element.38), channel_id=1, source_target_pairs={{0,1},{1,2},{2,3},{3,0},{4,5},{5,6},{6,7},{7,4},{8,9},{9,10},{10,1... | collective-permute-start | bytes 221192 | tf_op jit(solution)/shard_map/ppermute | solution.py:926
  1.7 2.0 %collective-permute-start.1 = (f32[9,8,256]{2,1,0:T(8,128)S(1)}, f32[9,8,256]{2,1,0:T(8,128)S(1)}, u32[]{:S(2)}, u32[]{:S(2)}) collective-permute-start(f32[9,8,256]{2,1,0:T(8,128)S(1)} %get-tuple-element.39), channel_id=1, source_target_pairs={{1,0},{2,1},{3,2},{0,3},{5,4},{6,5},{7,6},{4,7},{9,8},{10,9},{11,1... | collective-permute-start | bytes 221192 | tf_op jit(solution)/shard_map/ppermute | solution.py:927
  3.7 0.5 %shard_map.38 = (f32[4,8,128]{2,1,0:T(8,128)S(1)}, f32[4,128]{1,0:T(4,128)S(1)}, bf16[2,128,128]{2,1,0:T(8,128)(2,1)S(1)}, bf16[2,128,128]{2,1,0:T(8,128)(2,1)S(1)}) custom-call(s32[8,16,256]{2,1,0:T(8,128)S(1)} %get-tuple-element.36.material), custom_call_target="tpu_custom_call" | custom-call | tf_op jit(solution)/shard_map/pallas_call | solution.py:914
  4.2 1.5 %collective-permute-done.from_low = f32[9,8,256]{2,1,0:T(8,128)S(1)} collective-permute-done((f32[9,8,256]{2,1,0:T(8,128)S(1)}, f32[9,8,256]{2,1,0:T(8,128)S(1)}, u32[]{:S(2)}, u32[]{:S(2)}) %collective-permute-start) | collective-permute-done | bytes 73760 | tf_op jit(solution)/shard_map/ppermute | solution.py:926
  5.7 0.6 %collective-permute-done.1.from_high = f32[9,8,256]{2,1,0:T(8,128)S(1)} collective-permute-done((f32[9,8,256]{2,1,0:T(8,128)S(1)}, f32[9,8,256]{2,1,0:T(8,128)S(1)}, u32[]{:S(2)}, u32[]{:S(2)}) %collective-permute-start.1) | collective-permute-done | bytes 73760 | tf_op jit(solution)/shard_map/ppermute | solution.py:927
  6.3 0.3 shard_map.39
  6.6 1.8 %collective-permute-start.2 = (f32[15,8,256]{2,1,0:T(8,128)S(1)}, f32[15,8,256]{2,1,0:T(8,128)S(1)}, u32[]{:S(2)}, u32[]{:S(2)}) collective-permute-start(f32[15,8,256]{2,1,0:T(8,128)S(1)} %get-tuple-element.44), channel_id=1, source_target_pairs={{0,4},{4,8},{8,12},{12,16},{16,20},{20,24},{24,28},{28,0},{1,5},{5... | collective-permute-start | bytes 368648 | tf_op jit(solution)/shard_map/ppermute | solution.py:926
  8.4 3.1 %collective-permute-start.3 = (f32[15,8,256]{2,1,0:T(8,128)S(1)}, f32[15,8,256]{2,1,0:T(8,128)S(1)}, u32[]{:S(2)}, u32[]{:S(2)}) collective-permute-start(f32[15,8,256]{2,1,0:T(8,128)S(1)} %get-tuple-element.45), channel_id=1, source_target_pairs={{4,0},{8,4},{12,8},{16,12},{20,16},{24,20},{28,24},{0,28},{5,1},{9... | collective-permute-start | bytes 368648 | tf_op jit(solution)/shard_map/ppermute | solution.py:927
  11.5 3.3 %collective-permute-done.2.from_low = f32[15,8,256]{2,1,0:T(8,128)S(1)} collective-permute-done((f32[15,8,256]{2,1,0:T(8,128)S(1)}, f32[15,8,256]{2,1,0:T(8,128)S(1)}, u32[]{:S(2)}, u32[]{:S(2)}) %collective-permute-start.2) | collective-permute-done | bytes 122912 | tf_op jit(solution)/shard_map/ppermute | solution.py:926
  14.8 2.1 %collective-permute-done.3.from_high = f32[15,8,256]{2,1,0:T(8,128)S(1)} collective-permute-done((f32[15,8,256]{2,1,0:T(8,128)S(1)}, f32[15,8,256]{2,1,0:T(8,128)S(1)}, u32[]{:S(2)}, u32[]{:S(2)}) %collective-permute-start.3) | collective-permute-done | bytes 122912 | tf_op jit(solution)/shard_map/ppermute | solution.py:927
  16.9 2.4 %shard_map.40 = (f32[10,24,256]{2,1,0:T(8,128)S(1)}, f32[10,24,256]{2,1,0:T(8,128)S(1)}, f32[11,24,256]{2,1,0:T(8,128)S(1)}, f32[10,24,256]{2,1,0:T(8,128)S(1)},...) custom-call(f32[3,8,24,256]{3,2,1,0:T(8,128)S(1)} %get-tuple-element, ...), custom_call_target="tpu_custom_call" | custom-call | tf_op jit(solution)/shard_map/pallas_call | solution.py:914
  19.3 4.5 %all-to-all-start = ((f32[32,4,4,128]{3,2,1,0:T(4,128)}), f32[32,4,4,128]{3,2,1,0:T(4,128)S(1)}, u32[]{:S(2)}, u32[]{:S(2)}) async-start(f32[32,4,4,128]{3,2,1,0:T(4,128)} %get-tuple-element.46), calls=%async_computation | async-start | bytes 524288 | tf_op jit(solution)/shard_map/all_to_all | solution.py:942
  23.8 0.3 collective-permute-start.4
  24.1 1.5 %collective-permute-start.5 = (f32[8,8,128]{2,1,0:T(8,128)S(1)}, f32[8,8,128]{2,1,0:T(8,128)S(1)}, u32[]{:S(2)}, u32[]{:S(2)}) collective-permute-start(f32[8,8,128]{2,1,0:T(8,128)S(1)} %get-tuple-element.50), channel_id=1, source_target_pairs={{1,0},{2,1},{3,2},{0,3},{5,4},{6,5},{7,6},{4,7},{9,8},{10,9},{11,1... | collective-permute-start | bytes 98312 | tf_op jit(solution)/shard_map/ppermute | solution.py:927
  25.6 1.9 %collective-permute-done.4.from_low.row_low = f32[8,8,128]{2,1,0:T(8,128)S(1)} collective-permute-done((f32[8,8,128]{2,1,0:T(8,128)S(1)}, f32[8,8,128]{2,1,0:T(8,128)S(1)}, u32[]{:S(2)}, u32[]{:S(2)}) %collective-permute-start.4) | collective-permute-done | bytes 32800 | tf_op jit(solution)/shard_map/ppermute | solution.py:926
  27.4 0.0 collective-permute-done.5.from_high.row_high
  27.5 0.1 shard_map.41
  27.5 1.9 %collective-permute-start.6 = (f32[18,8,128]{2,1,0:T(8,128)S(1)}, f32[18,8,128]{2,1,0:T(8,128)S(1)}, u32[]{:S(2)}, u32[]{:S(2)}) collective-permute-start(f32[18,8,128]{2,1,0:T(8,128)S(1)} %get-tuple-element.52), channel_id=1, source_target_pairs={{0,4},{4,0},{8,12},{12,8},{16,20},{20,16},{24,28},{28,24},{1,5},{5... | collective-permute-start | bytes 221192 | tf_op jit(solution)/shard_map/ppermute | solution.py:937
  29.4 4.4 %collective-permute-start.7 = (f32[18,8,128]{2,1,0:T(8,128)S(1)}, f32[18,8,128]{2,1,0:T(8,128)S(1)}, u32[]{:S(2)}, u32[]{:S(2)}) collective-permute-start(f32[18,8,128]{2,1,0:T(8,128)S(1)} %get-tuple-element.53), channel_id=1, source_target_pairs={{0,28},{4,8},{8,4},{12,16},{16,12},{20,24},{24,20},{28,0},{1,29},{... | collective-permute-start | bytes 221192 | tf_op jit(solution)/shard_map/ppermute | solution.py:936
  33.8 0.2 shard_map.42
  34.0 0.0 collective-permute-done.6.one_near
  34.0 2.7 %collective-permute-done.7.one_far = f32[18,8,128]{2,1,0:T(8,128)S(1)} collective-permute-done((f32[18,8,128]{2,1,0:T(8,128)S(1)}, f32[18,8,128]{2,1,0:T(8,128)S(1)}, u32[]{:S(2)}, u32[]{:S(2)}) %collective-permute-start.7) | collective-permute-done | bytes 73760 | tf_op jit(solution)/shard_map/ppermute | solution.py:936
  36.6 0.0 all-to-all-done.blocks
  36.6 6.3 %shard_map.43 = f32[8,16,256]{2,1,0:T(8,128)} custom-call(f32[32,4,4,128]{3,2,1,0:T(4,128)S(1)} %all-to-all-done.blocks, f32[3,4,16,128]{3,2,1,0:T(8,128)S(1)} %get-tuple-element.51._.window_one, f32[18,8,128]{2,1,0:T(8,128)S(1)} %collective-permute-done.6.one_near, f32[18,8,128]{2,1,0:T(8,128)S(1)} %collective-permute-done.7.one_far, ...), custom_call_target="tpu_custom_call" | custom-call | tf_op jit(solution)/shard_map/pallas_call | solution.py:914
Async XLA Ops:
  1.2 4.5 %collective-permute-start = (f32[9,8,256]{2,1,0:T(8,128)S(1)}, f32[9,8,256]{2,1,0:T(8,128)S(1)}, u32[]{:S(2)}, u32[]{:S(2)}) collective-permute-start(f32[9,8,256]{2,1,0:T(8,128)S(1)} %get-tuple-element.38), channel_id=1, source_target_pairs={{0,1},{1,2},{2,3},{3,0},{4,5},{5,6},{6,7},{7,4},{8,9},{9,10},{10,1... | collective-permute-start | bytes 221192 | tf_op jit(solution)/shard_map/ppermute | solution.py:926
  1.7 4.6 %collective-permute-start.1 = (f32[9,8,256]{2,1,0:T(8,128)S(1)}, f32[9,8,256]{2,1,0:T(8,128)S(1)}, u32[]{:S(2)}, u32[]{:S(2)}) collective-permute-start(f32[9,8,256]{2,1,0:T(8,128)S(1)} %get-tuple-element.39), channel_id=1, source_target_pairs={{1,0},{2,1},{3,2},{0,3},{5,4},{6,5},{7,6},{4,7},{9,8},{10,9},{11,1... | collective-permute-start | bytes 221192 | tf_op jit(solution)/shard_map/ppermute | solution.py:927
  6.6 8.2 %collective-permute-start.2 = (f32[15,8,256]{2,1,0:T(8,128)S(1)}, f32[15,8,256]{2,1,0:T(8,128)S(1)}, u32[]{:S(2)}, u32[]{:S(2)}) collective-permute-start(f32[15,8,256]{2,1,0:T(8,128)S(1)} %get-tuple-element.44), channel_id=1, source_target_pairs={{0,4},{4,8},{8,12},{12,16},{16,20},{20,24},{24,28},{28,0},{1,5},{5... | collective-permute-start | bytes 368648 | tf_op jit(solution)/shard_map/ppermute | solution.py:926
  8.4 8.5 %collective-permute-start.3 = (f32[15,8,256]{2,1,0:T(8,128)S(1)}, f32[15,8,256]{2,1,0:T(8,128)S(1)}, u32[]{:S(2)}, u32[]{:S(2)}) collective-permute-start(f32[15,8,256]{2,1,0:T(8,128)S(1)} %get-tuple-element.45), channel_id=1, source_target_pairs={{4,0},{8,4},{12,8},{16,12},{20,16},{24,20},{28,24},{0,28},{5,1},{9... | collective-permute-start | bytes 368648 | tf_op jit(solution)/shard_map/ppermute | solution.py:927
  19.3 17.3 %all-to-all-start = ((f32[32,4,4,128]{3,2,1,0:T(4,128)}), f32[32,4,4,128]{3,2,1,0:T(4,128)S(1)}, u32[]{:S(2)}, u32[]{:S(2)}) async-start(f32[32,4,4,128]{3,2,1,0:T(4,128)} %get-tuple-element.46), calls=%async_computation | async-start | bytes 524288 | tf_op jit(solution)/shard_map/all_to_all | solution.py:942
  23.8 3.6 %collective-permute-start.4 = (f32[8,8,128]{2,1,0:T(8,128)S(1)}, f32[8,8,128]{2,1,0:T(8,128)S(1)}, u32[]{:S(2)}, u32[]{:S(2)}) collective-permute-start(f32[8,8,128]{2,1,0:T(8,128)S(1)} %get-tuple-element.49), channel_id=1, source_target_pairs={{0,1},{1,2},{2,3},{3,0},{4,5},{5,6},{6,7},{7,4},{8,9},{9,10},{10,1... | collective-permute-start | bytes 98312 | tf_op jit(solution)/shard_map/ppermute | solution.py:926
  24.1 3.4 %collective-permute-start.5 = (f32[8,8,128]{2,1,0:T(8,128)S(1)}, f32[8,8,128]{2,1,0:T(8,128)S(1)}, u32[]{:S(2)}, u32[]{:S(2)}) collective-permute-start(f32[8,8,128]{2,1,0:T(8,128)S(1)} %get-tuple-element.50), channel_id=1, source_target_pairs={{1,0},{2,1},{3,2},{0,3},{5,4},{6,5},{7,6},{4,7},{9,8},{10,9},{11,1... | collective-permute-start | bytes 98312 | tf_op jit(solution)/shard_map/ppermute | solution.py:927
  27.5 6.4 %collective-permute-start.6 = (f32[18,8,128]{2,1,0:T(8,128)S(1)}, f32[18,8,128]{2,1,0:T(8,128)S(1)}, u32[]{:S(2)}, u32[]{:S(2)}) collective-permute-start(f32[18,8,128]{2,1,0:T(8,128)S(1)} %get-tuple-element.52), channel_id=1, source_target_pairs={{0,4},{4,0},{8,12},{12,8},{16,20},{20,16},{24,28},{28,24},{1,5},{5... | collective-permute-start | bytes 221192 | tf_op jit(solution)/shard_map/ppermute | solution.py:937
  29.4 7.2 %collective-permute-start.7 = (f32[18,8,128]{2,1,0:T(8,128)S(1)}, f32[18,8,128]{2,1,0:T(8,128)S(1)}, u32[]{:S(2)}, u32[]{:S(2)}) collective-permute-start(f32[18,8,128]{2,1,0:T(8,128)S(1)} %get-tuple-element.53), channel_id=1, source_target_pairs={{0,28},{4,8},{8,4},{12,16},{16,12},{20,24},{24,20},{28,0},{1,29},{... | collective-permute-start | bytes 221192 | tf_op jit(solution)/shard_map/ppermute | solution.py:936

commit v5 on v4

--- a/solution.py
+++ b/solution.py
@@ -251,7 +251,7 @@
     return (len(BASE_PLANES) + 1) * tile_y // ROWS + -(-loose // ROWS) + 1
 
 
-def shrink(material, k_tile, k_two, halves, halves_one, paired, paired_one):
+def shrink(material, k_tile, blocks, halves, halves_one, paired, paired_one):
     tile_x, tile_y, size_z = material.shape
     tile_x1, tile_y1, size_z1 = tile_x // 2, tile_y // 2, size_z // 2
     k_one = None
@@ -283,7 +283,8 @@
         part = times_right(piece, halve_lanes(size_z1, LANES, pair * size_z1 // 2))
         block = part if block is None else block + part
     block = 0.125 * block
-    k_two[...] = block
+    for device in range(blocks.shape[0]):
+        blocks[device] = block
     for chunk in range(size_z // LANES):
         halves[chunk] = halve_lanes(LANES, size_z1, chunk * LANES // 2)
     for half in range(2):
@@ -291,7 +292,7 @@
 
 
 def fine_down(
-    window, k_two, halves, halves_one, from_low, from_high,
+    window, halves, halves_one, from_low, from_high,
     v_zero, forcing_out, cx, cy, cz, weight, level_one, blocks_out, to_low, to_high,
     conc_rim, forcing_rim, kappa_rim, once, diag, paired, blocks, left,
     k_one, f_one, u_one, v_one, cx1, cy1, cz1, w1, d1, paired_one, packed,
@@ -432,10 +433,7 @@
     used = tile_y1 // 2 + RC
     block = jnp.concatenate([result[p * ROWS : p * ROWS + used] for p in range(half_pairs)], 0)
     block = 0.125 * block
-    k_block = k_two[...]
-    for device in range(blocks.shape[0]):
-        blocks[device, blocks.shape[1] - 1] = k_block
-    for part in range(blocks.shape[1] - 1):
+    for part in range(blocks.shape[1]):
         piece = block[part * SHORT : (part + 1) * SHORT]
         for device in range(blocks.shape[0]):
             blocks[device, part] = piece
@@ -540,31 +538,44 @@
         return Grid(sizes, strides, scales, self.rows, self.lanes)
 
 
+def swapped(v):
+    return pltpu.roll(v, v.shape[-1] // 2, v.ndim - 1)
+
+
+def along_z(v, step):
+    lanes = v.shape[2]
+    half = lanes // 2
+    lane = mod(iota(v.shape, 2), half)
+    if step > 0:
+        mine = lane < half - step
+        return jnp.where(mine, pltpu.roll(v, lanes - step, 2), pltpu.roll(v, half - step, 2))
+    mine = lane >= -step
+    return jnp.where(mine, pltpu.roll(v, -step, 2), pltpu.roll(v, half - step, 2))
+
+
 def next_plane(v):
-    return v if v.shape[0] == 1 else jnp.concatenate([v[1:], v[:1]], 0)
+    return jnp.concatenate([v[1:], swapped(v[:1])], 0) if v.shape[0] > 1 else swapped(v)
 
 
 def last_plane(v):
-    return v if v.shape[0] == 1 else jnp.concatenate([v[-1:], v[:-1]], 0)
+    return jnp.concatenate([swapped(v[-1:]), v[:-1]], 0) if v.shape[0] > 1 else swapped(v)
 
 
 def restrict_whole(v, grid):
-    if grid.ratios[0] == 2:
-        v = jnp.concatenate(
-            [v[2 * x : 2 * x + 1] + v[2 * x + 1 : 2 * x + 2] for x in range(grid.sizes[0] // 2)], 0
-        )
-    for axis in (1, 2):
-        if grid.ratios[axis] == 2:
-            step = grid.strides[axis - 1]
-            even = mod(div(iota(v.shape, axis), step), 2) == 0
-            v = v + jnp.where(even, ahead(v, axis, step), back(v, axis, step))
-    return (1.0 / (grid.ratios[0] * grid.ratios[1] * grid.ratios[2])) * v
+    assert grid.ratios == (2, 2, 2) and v.shape[0] % 2 == 0
+    v = jnp.concatenate(
+        [v[2 * x : 2 * x + 1] + v[2 * x + 1 : 2 * x + 2] for x in range(v.shape[0] // 2)], 0
+    )
+    step_y, step_z = grid.strides
+    even = mod(div(iota(v.shape, 1), step_y), 2) == 0
+    v = v + jnp.where(even, ahead(v, 1, step_y), back(v, 1, step_y))
+    even = mod(div(iota(v.shape, 2), step_z), 2) == 0
+    v = v + jnp.where(even, ahead(v, 2, step_z), back(v, 2, step_z))
+    return 0.125 * v
 
 
 def prolong_whole(v, grid):
-    if grid.ratios[0] == 1:
-        return v
-    return jnp.concatenate([v[x // 2 : x // 2 + 1] for x in range(grid.sizes[0])], 0)
+    return jnp.concatenate([v[x // 2 : x // 2 + 1] for x in range(grid.sizes[0] // 2)], 0)
 
 
 def whole_operator(kappa, grid):
@@ -572,9 +583,9 @@
     step_y, step_z = grid.strides
     cx = half_x * (kappa + next_plane(kappa))
     cy = half_y * (kappa + ahead(kappa, 1, step_y))
-    cz = half_z * (kappa + ahead(kappa, 2, step_z))
+    cz = half_z * (kappa + along_z(kappa, step_z))
     diag = mass_rate + cx + last_plane(cx)
-    diag = diag + (cy + back(cy, 1, step_y)) + (cz + back(cz, 2, step_z))
+    diag = diag + (cy + back(cy, 1, step_y)) + (cz + along_z(cz, -step_z))
     return cx, cy, cz, diag, relax_weight / diag
 
 
@@ -583,11 +594,16 @@
     step_y, step_z = grid.strides
     total = cx * next_plane(v) + last_plane(cx * v)
     total = total + (cy * ahead(v, 1, step_y) + back(cy * v, 1, step_y))
-    return total + (cz * ahead(v, 2, step_z) + back(cz * v, 2, step_z))
+    return total + (cz * along_z(v, step_z) + along_z(cz * v, -step_z))
 
 
 def whole_sweep(v, forcing, operator, grid):
     return (1.0 - relax_weight) * v + operator[4] * (forcing + whole_neighbours(v, operator, grid))
+
+
+def doubled(planes):
+    first, second = planes
+    return jnp.where(iota(first.shape, first.ndim - 1) < first.shape[-1] // 2, first, second)
 
 
 class ExactSolve:
@@ -645,11 +661,14 @@
         grid = self.grid
         size_x, size_y, _ = grid.sizes
         step_y, step_z = grid.strides
+        assert size_x == 2
+        turned = swapped(v)
+        planes = [doubled((v[0], turned[0])), doubled((turned[0], v[0]))]
         sub = mod(iota((1, grid.lanes), 1), step_z)
         result = jnp.zeros((1, grid.lanes), F32)
         for x in range(size_x):
             for y in range(size_y):
-                row = v[x, y * step_y : y * step_y + 1]
+                row = planes[x][y * step_y : y * step_y + 1]
                 result = jnp.where(sub == x * size_y + y, row, result)
         return result
 
@@ -667,8 +686,8 @@
                 mine = mod(self.i, self.across) == x * size_y + y
                 row = jnp.sum(jnp.where(mine, spread, 0.0), axis=0, keepdims=True)
                 rows.append(jnp.broadcast_to(row, (step_y, grid.lanes)))
-            planes.append(jnp.concatenate(rows, 0)[None])
-        return jnp.concatenate(planes, 0)
+            planes.append(jnp.concatenate(rows, 0))
+        return doubled(planes)[None]
 
 
 def levels_of(counts, tile_sizes):
@@ -681,32 +700,44 @@
     return grids
 
 
-def kappa_of(blocks, counts, grid):
+class Operator:
+    def __init__(self, ref):
+        self.ref = ref
+
+    def __getitem__(self, part):
+        if isinstance(part, slice):
+            return [self.ref[p] for p in range(*part.indices(5))]
+        return self.ref[part]
+
+
+def prepare(counts, grids, blocks, _, *outputs):
     count_x, count_y = counts
-    planes, rows, size_z2 = grid.sizes
+    planes, rows, size_z2 = grids[0].sizes
     half_x, half_y = planes // count_x, rows // count_y
-    assert half_x * size_z2 == LANES and half_x == 2 and ROWS % half_y == 0 and half_y == SHORT
+    assert 2 * size_z2 == LANES and half_x == 2 and half_y == SHORT and planes % 2 == 0
     share = ROWS // half_y
-    kappa = [[None] * (rows // ROWS) for _ in range(planes)]
-    lane = iota((ROWS, LANES), 1)
-    at = blocks.shape[1] - 1
+    pairs = planes // 2
+    kappa = [[None] * (rows // ROWS) for _ in range(pairs)]
+    lower = iota((ROWS, LANES), 1) < size_z2
     for tx in range(count_x):
         for group in range(rows // ROWS):
-            pieces = [blocks[tx * count_y + group * share + n, at] for n in range(share)]
-            piece = jnp.concatenate(pieces, 0)
-            turned = pltpu.roll(piece, size_z2, 1)
+            piece = jnp.concatenate(
+                [blocks[tx * count_y + group * share + n] for n in range(share)], 0
+            )
+            turned = swapped(piece)
             for p in range(half_x):
-                mine = (lane < size_z2) == (p == 0)
-                kappa[tx * half_x + p][group] = jnp.where(mine, piece, turned)
-    return jnp.concatenate([jnp.concatenate(groups, 0)[None] for groups in kappa], 0)
-
-
-def prepare(kappa, grids):
-    kappas = [kappa]
+                x = tx * half_x + p
+                value = piece if x // pairs == p else turned
+                if x >= pairs:
+                    value = jnp.where(lower, kappa[x % pairs][group], value)
+                kappa[x % pairs][group] = value
+    kappas = [jnp.concatenate([jnp.concatenate(groups, 0)[None] for groups in kappa], 0)]
     for grid in grids[:-1]:
         kappas.append(restrict_whole(kappas[-1], grid))
-    exact = ExactSolve(grids[-1], kappas[-1])
-    return [(grid, whole_operator(k, grid)) for grid, k in zip(grids[:-1], kappas)], exact
+    outputs[-1][...] = ExactSolve(grids[-1], kappas[-1]).inverse
+    for number, grid in enumerate(grids[:-1]):
+        for part, value in enumerate(whole_operator(kappas[number], grid)):
+            outputs[number][part] = value
 
 
 def selectors(sizes, planes1, tile_x1, tile_y1, rows, _, left_one, right_one, left_zero, right_zero):
@@ -763,7 +794,8 @@
     sub = iota((ROWS, LANES), 0)
     lane = iota((ROWS, LANES), 1)
     nothing = jnp.zeros((ROWS, LANES), F32)
-    forcing = [[nothing] * groups for _ in range(planes)]
+    pairs = planes // 2
+    forcing = [[nothing] * groups for _ in range(pairs)]
     half_pairs = (half_x + RC) // 2
     ring = RC // 2
     for tx in range(count_x):
@@ -777,17 +809,17 @@
                 group, offset = start // ROWS, start % ROWS
                 shift = (offset - base) % ROWS
                 piece = pltpu.roll(piece, shift, 0) if shift else piece
-                turned = pltpu.roll(piece, size_z2, 1)
                 for half in range(2):
-                    moved = jnp.where((lane < size_z2) == (half == 0), piece, turned)
                     x = (tx * half_x - ring + half * half_pairs + p) % planes
+                    moved = piece if x // pairs == half else swapped(piece)
+                    here = (lane < size_z2) == (x < pairs)
                     at = group
-                    mine = (sub >= offset) & (sub < offset + used)
-                    forcing[x][at] = forcing[x][at] + jnp.where(mine, moved, 0.0)
+                    mine = here & (sub >= offset) & (sub < offset + used)
+                    forcing[x % pairs][at] = forcing[x % pairs][at] + jnp.where(mine, moved, 0.0)
                     if offset + used > ROWS:
                         at = (group + 1) % groups
-                        mine = sub < offset + used - ROWS
-                        forcing[x][at] = forcing[x][at] + jnp.where(mine, moved, 0.0)
+                        mine = here & (sub < offset + used - ROWS)
+                        forcing[x % pairs][at] = forcing[x % pairs][at] + jnp.where(mine, moved, 0.0)
     return jnp.concatenate([jnp.concatenate(groups, 0)[None] for groups in forcing], 0)
 
 
@@ -795,6 +827,7 @@
     counts, grids, blocks, window_one, one_near, one_far, row_low, row_high,
     v_zero, forcing0, cx, cy, cz, weight, left_one, right_one, left_zero, right_zero, *rest,
 ):
+    prepared, rest = rest[: len(grids)], rest[len(grids) :]
     (
         out, mixed_low, mixed_high, kappa_low, kappa_high, first_low, first_high,
         v_one, cx1, cy1, cz1, w1, one_a, one_b, zero_a, zero_b,
@@ -807,7 +840,8 @@
     half_x, half_y, size_z2 = tile_x1 // 2, tile_y1 // 2, size_z1 // 2
     sizes = grids[0].sizes
     forcing2 = assemble(blocks, count_x, count_y, half_x, half_y, size_z2)
-    levels, exact = prepare(kappa_of(blocks, counts, grids[0]), grids)
+    levels = [(grid, Operator(prepared[number])) for number, grid in enumerate(grids[:-1])]
+    exact = ExactSolve(grids[-1], inverse=prepared[-1][...])
 
     planes1 = tile_x1 + 2 * R1
     for message, mixed, kappa_rim, low in (
@@ -851,7 +885,7 @@
     plane_sweep(start1, v_one, forcing1, cx1, cy1, cz1, w1, 1, planes1 - 1)
 
     solved = solve_whole(forcing2, levels, exact)
-    solved = solved.reshape(sizes[0] * sizes[1], LANES)
+    solved = jnp.concatenate([solved, swapped(solved)], 0).reshape(sizes[0] * sizes[1], LANES)
 
     raised = raise_level(left_one[...], right_one[...], solved)
     for x in range(1, planes1 - 1):
@@ -970,12 +1004,12 @@
     def bits(*shape):
         return jax.ShapeDtypeStruct(shape, BF16)
 
-    k_tile, k_two, halves, halves_one = call(
+    k_tile, kappa_blocks, halves, halves_one = call(
         shrink,
         inputs[2:],
         (
             one_tile,
-            (two_tile[1], LANES),
+            (everyone, two_tile[1], LANES),
             bits(chunks, LANES, one_tile[2]),
             bits(2, one_tile[2], one_tile[2]),
         ),
@@ -989,16 +1023,17 @@
         ((rows, size_z),),
     )
     from_low, from_high = shift_both(to_low, to_high, "tx")
+    kappa_blocks = to_everyone(kappa_blocks)
     wide = -(-rows // (2 * ROWS)) * ROWS
     small = (one_tile[0] + 2 * RC, wide, one_tile[2])
     pairs1 = small[0] // 2
-    short = pairs1 // 2 * (two_tile[1] + RC) // SHORT + 1
+    short = pairs1 // 2 * (two_tile[1] + RC) // SHORT
     assert pairs1 // 2 * (two_tile[1] + RC) % SHORT == 0
     message = (3 * one_tile[0] * R1 // ROWS + chunks, ROWS, LANES)
     assert one_tile[2] == LANES and tile_x <= ROWS and one_tile[1] == ROWS
     v_zero, forcing0, cx, cy, cz, weight, level_one, blocks, to_low, to_high = call(
         fine_down,
-        (window, k_two, halves, halves_one, from_low, from_high),
+        (window, halves, halves_one, from_low, from_high),
         (inner, inner, (tile_x + 3, rows, size_z), inner, inner, inner)
         + ((3,) + one_tile, (everyone, short, SHORT, LANES), message, message),
         (
@@ -1039,11 +1074,19 @@
         ),
         (),
     )
+    lattice = grids[0].sizes[1], LANES
+    prepared = call(
+        functools.partial(prepare, counts, grids),
+        (kappa_blocks, window_one),
+        tuple((5, grid.sizes[0] // 2) + lattice for grid in grids[:-1])
+        + ((-(-grids[-1].cells // ROWS) * ROWS, LANES),),
+        (),
+    )
     rim = (R1,) + one[1:]
     (updated,) = call(
         functools.partial(coarse_up, counts, grids),
         (blocks, window_one, one_near, one_far, row_low, row_high)
-        + (v_zero, forcing0, cx, cy, cz, weight, *chosen),
+        + (v_zero, forcing0, cx, cy, cz, weight, *chosen, *prepared),
         (concentration.shape,),
         (rim,) * 6 + (one,) * 7 + (zero, zero),
     )

time: 43.2 us -> 45.8 us (1.060)
  starting transfers between devices: 20 us -> 26 us
  waiting for transfers between devices: 12 us -> 6.87 us
  Pallas kernels: 10.9 us -> 12.5 us
    all_to_all x1 -> x2, starting transfers between devices: 4.5 us -> 10.8 us  [to_everyone(): return lax.all_to_all(blocks, ('tx', 'ty'), 0, 0)]
    ppermute x1, waiting for transfers between devices: 2.66 us -> 0.01 us  [swap_both(): from_far = lax.ppermute(far, axis, other)]
    ppermute x3, waiting for transfers between devices: 2.68 us -> 0.95 us  [shift_both(): lax.ppermute(to_low, axis, [((i + 1) % count, i) for i in range(count)])]
    pallas_call x7 -> x8, Pallas kernels: 10.9 us -> 12.5 us  [call(): pl.pallas_call(kernel, in_specs=[spec] * len(operands), out_specs=[IN_PLA...]
    ppermute x3, waiting for transfers between devices: 6.63 us -> 5.91 us  [shift_both(): lax.ppermute(to_high, axis, [(i, (i + 1) % count) for i in range(count)])]
  transfers between devices with their start and end apart: 9 -> 10, of which waited for: 6 -> 3; matrix products, arithmetic and copies ran while one was open for 0% -> 0% of each run, Pallas kernels for 2% -> 16%
where the time goes in v5:
time: 45.8 us; the launch traced here: 45.5 us
  starting transfers between devices  26 us (57%)
  Pallas kernels  12.5 us (27%)
  waiting for transfers between devices  6.87 us (15%)
    pallas_call x8, Pallas kernels, call(): pl.pallas_call(kernel, in_specs=[spec] * len(operands), out_specs=[IN_PLA...  12.5 us
    all_to_all x2, starting transfers between devices, to_everyone(): return lax.all_to_all(blocks, ('tx', 'ty'), 0, 0)  10.8 us
    ppermute x3, starting transfers between devices, shift_both(): lax.ppermute(to_low, axis, [((i + 1) % count, i) for i in range(count)])  6.43 us
    ppermute x3, waiting for transfers between devices, shift_both(): lax.ppermute(to_high, axis, [(i, (i + 1) % count) for i in range(count)])  5.91 us
    ppermute x1, starting transfers between devices, swap_both(): from_far = lax.ppermute(far, axis, other)  4.16 us
    ppermute x3, starting transfers between devices, shift_both(): lax.ppermute(to_high, axis, [(i, (i + 1) % count) for i in range(count)])  2.67 us
    ppermute x1, starting transfers between devices, swap_both(): from_near = lax.ppermute(near, axis, partner)  2.03 us
    ppermute x3, waiting for transfers between devices, shift_both(): lax.ppermute(to_low, axis, [((i + 1) % count, i) for i in range(count)])  0.95 us
  transfers between devices with their start and end apart: 10, of which 3 were waited for; matrix products, arithmetic and copies ran while one was open for 0% of the time, Pallas kernels for 16%

profile of v5, /device:TPU:0, one launch (start us, length us, event | category | flops | bytes accessed | tf_op | source)
XLA Modules:
  0.0 45.5 jit_solution(12833242818943218506)
XLA Ops:
  0.0 1.2 %shard_map.37 = (f32[8,16,256]{2,1,0:T(8,128)S(1)}, f32[8,16,256]{2,1,0:T(8,128)S(1)}, s32[8,16,256]{2,1,0:T(8,128)S(1)}, f32[9,8,256]{2,1,0:T(8,128)S(1)}, f32[9,8,256]{2,1,0:T(8,128)S(1)}) custom-call(f32[8,16,256]{2,1,0:T(8,128)} %conc_in.1, f32[8,16,256]{2,1,0:T(8,128)} %source_in.1, s32[8,16,256]{2,1,0:T(8,128)} %material_in.1), custom_call_target="tpu_custom_call" | custom-call | tf_op jit(solution)/shard_map/pallas_call | solution.py:948
  1.2 0.5 %collective-permute-start = (f32[9,8,256]{2,1,0:T(8,128)S(1)}, f32[9,8,256]{2,1,0:T(8,128)S(1)}, u32[]{:S(2)}, u32[]{:S(2)}) collective-permute-start(f32[9,8,256]{2,1,0:T(8,128)S(1)} %get-tuple-element.42), channel_id=1, source_target_pairs={{0,1},{1,2},{2,3},{3,0},{4,5},{5,6},{6,7},{7,4},{8,9},{9,10},{10,1... | collective-permute-start | bytes 221192 | tf_op jit(solution)/shard_map/ppermute | solution.py:960
  1.7 2.0 %collective-permute-start.1 = (f32[9,8,256]{2,1,0:T(8,128)S(1)}, f32[9,8,256]{2,1,0:T(8,128)S(1)}, u32[]{:S(2)}, u32[]{:S(2)}) collective-permute-start(f32[9,8,256]{2,1,0:T(8,128)S(1)} %get-tuple-element.43), channel_id=1, source_target_pairs={{1,0},{2,1},{3,2},{0,3},{5,4},{6,5},{7,6},{4,7},{9,8},{10,9},{11,1... | collective-permute-start | bytes 221192 | tf_op jit(solution)/shard_map/ppermute | solution.py:961
  3.7 1.1 %shard_map.38 = (f32[4,8,128]{2,1,0:T(8,128)S(1)}, f32[32,4,128]{2,1,0:T(4,128)}, bf16[2,128,128]{2,1,0:T(8,128)(2,1)S(1)}, bf16[2,128,128]{2,1,0:T(8,128)(2,1)S(1)}) custom-call(s32[8,16,256]{2,1,0:T(8,128)S(1)} %get-tuple-element.40.material), custom_call_target="tpu_custom_call" | custom-call | tf_op jit(solution)/shard_map/pallas_call | solution.py:948
  4.8 6.6 %all-to-all-start.1 = ((f32[32,4,128]{2,1,0:T(4,128)}), f32[32,4,128]{2,1,0:T(4,128)S(1)}, u32[]{:S(2)}, u32[]{:S(2)}) async-start(f32[32,4,128]{2,1,0:T(4,128)} %get-tuple-element.66), calls=%async_computation.1 | async-start | bytes 131072 | tf_op jit(solution)/shard_map/all_to_all | solution.py:976
  11.5 0.0 collective-permute-done.from_low
  11.5 0.0 collective-permute-done.1.from_high
  11.5 0.3 shard_map.39
  11.8 1.8 %collective-permute-start.2 = (f32[15,8,256]{2,1,0:T(8,128)S(1)}, f32[15,8,256]{2,1,0:T(8,128)S(1)}, u32[]{:S(2)}, u32[]{:S(2)}) collective-permute-start(f32[15,8,256]{2,1,0:T(8,128)S(1)} %get-tuple-element.47), channel_id=1, source_target_pairs={{0,4},{4,8},{8,12},{12,16},{16,20},{20,24},{24,28},{28,0},{1,5},{5... | collective-permute-start | bytes 368648 | tf_op jit(solution)/shard_map/ppermute | solution.py:960
  13.6 3.0 %collective-permute-start.3 = (f32[15,8,256]{2,1,0:T(8,128)S(1)}, f32[15,8,256]{2,1,0:T(8,128)S(1)}, u32[]{:S(2)}, u32[]{:S(2)}) collective-permute-start(f32[15,8,256]{2,1,0:T(8,128)S(1)} %get-tuple-element.48), channel_id=1, source_target_pairs={{4,0},{8,4},{12,8},{16,12},{20,16},{24,20},{28,24},{0,28},{5,1},{9... | collective-permute-start | bytes 368648 | tf_op jit(solution)/shard_map/ppermute | solution.py:961
  16.6 4.2 %collective-permute-done.2.from_low = f32[15,8,256]{2,1,0:T(8,128)S(1)} collective-permute-done((f32[15,8,256]{2,1,0:T(8,128)S(1)}, f32[15,8,256]{2,1,0:T(8,128)S(1)}, u32[]{:S(2)}, u32[]{:S(2)}) %collective-permute-start.2) | collective-permute-done | bytes 122912 | tf_op jit(solution)/shard_map/ppermute | solution.py:960
  20.8 0.9 %collective-permute-done.3.from_high = f32[15,8,256]{2,1,0:T(8,128)S(1)} collective-permute-done((f32[15,8,256]{2,1,0:T(8,128)S(1)}, f32[15,8,256]{2,1,0:T(8,128)S(1)}, u32[]{:S(2)}, u32[]{:S(2)}) %collective-permute-start.3) | collective-permute-done | bytes 122912 | tf_op jit(solution)/shard_map/ppermute | solution.py:961
  21.8 2.4 %shard_map.40 = (f32[10,24,256]{2,1,0:T(8,128)S(1)}, f32[10,24,256]{2,1,0:T(8,128)S(1)}, f32[11,24,256]{2,1,0:T(8,128)S(1)}, f32[10,24,256]{2,1,0:T(8,128)S(1)},...) custom-call(f32[3,8,24,256]{3,2,1,0:T(8,128)S(1)} %get-tuple-element, ...), custom_call_target="tpu_custom_call" | custom-call | tf_op jit(solution)/shard_map/pallas_call | solution.py:948
  24.2 0.0 all-to-all-done.1.blocks
  24.2 4.2 %all-to-all-start = ((f32[32,3,4,128]{3,2,1,0:T(4,128)}), f32[32,3,4,128]{3,2,1,0:T(4,128)S(1)}, u32[]{:S(2)}, u32[]{:S(2)}) async-start(f32[32,3,4,128]{3,2,1,0:T(4,128)} %get-tuple-element.49), calls=%async_computation | async-start | bytes 393216 | tf_op jit(solution)/shard_map/all_to_all | solution.py:976
  28.3 0.3 collective-permute-start.4
  28.6 1.5 %collective-permute-start.5 = (f32[8,8,128]{2,1,0:T(8,128)S(1)}, f32[8,8,128]{2,1,0:T(8,128)S(1)}, u32[]{:S(2)}, u32[]{:S(2)}) collective-permute-start(f32[8,8,128]{2,1,0:T(8,128)S(1)} %get-tuple-element.53), channel_id=1, source_target_pairs={{1,0},{2,1},{3,2},{0,3},{5,4},{6,5},{7,6},{4,7},{9,8},{10,9},{11,1... | collective-permute-start | bytes 98312 | tf_op jit(solution)/shard_map/ppermute | solution.py:961
  30.1 1.7 %collective-permute-done.4.from_low.row_low = f32[8,8,128]{2,1,0:T(8,128)S(1)} collective-permute-done((f32[8,8,128]{2,1,0:T(8,128)S(1)}, f32[8,8,128]{2,1,0:T(8,128)S(1)}, u32[]{:S(2)}, u32[]{:S(2)}) %collective-permute-start.4) | collective-permute-done | bytes 32800 | tf_op jit(solution)/shard_map/ppermute | solution.py:960
  31.8 0.0 collective-permute-done.5.from_high.row_high
  31.8 0.1 shard_map.41
  31.9 2.0 %collective-permute-start.6 = (f32[18,8,128]{2,1,0:T(8,128)S(1)}, f32[18,8,128]{2,1,0:T(8,128)S(1)}, u32[]{:S(2)}, u32[]{:S(2)}) collective-permute-start(f32[18,8,128]{2,1,0:T(8,128)S(1)} %get-tuple-element.55), channel_id=1, source_target_pairs={{0,4},{4,0},{8,12},{12,8},{16,20},{20,16},{24,28},{28,24},{1,5},{5... | collective-permute-start | bytes 221192 | tf_op jit(solution)/shard_map/ppermute | solution.py:971
  33.9 4.2 %collective-permute-start.7 = (f32[18,8,128]{2,1,0:T(8,128)S(1)}, f32[18,8,128]{2,1,0:T(8,128)S(1)}, u32[]{:S(2)}, u32[]{:S(2)}) collective-permute-start(f32[18,8,128]{2,1,0:T(8,128)S(1)} %get-tuple-element.56), channel_id=1, source_target_pairs={{0,28},{4,8},{8,4},{12,16},{16,12},{20,24},{24,20},{28,0},{1,29},{... | collective-permute-start | bytes 221192 | tf_op jit(solution)/shard_map/ppermute | solution.py:970
  38.1 0.2 shard_map.42
  38.2 3.3 %shard_map.43 = (f32[5,8,16,128]{3,2,1,0:T(8,128)S(1)}, f32[5,4,16,128]{3,2,1,0:T(8,128)S(1)}, f32[5,2,16,128]{3,2,1,0:T(8,128)S(1)}, f32[32,128]{1,0:T(8,128)S(1)}) custom-call(f32[32,4,128]{2,1,0:T(4,128)S(1)} %all-to-all-done.1.blocks, f32[3,4,16,128]{3,2,1,0:T(8,128)S(1)} %get-tuple-element.54._.window_one), custom_call_target="tpu_custom_call" | custom-call | tf_op jit(solution)/shard_map/pallas_call | solution.py:948
  41.6 0.0 collective-permute-done.6.one_near
  41.6 0.0 collective-permute-done.7.one_far
  41.6 0.0 all-to-all-done.blocks
  41.6 3.9 %shard_map.44 = f32[8,16,256]{2,1,0:T(8,128)} custom-call(f32[32,3,4,128]{3,2,1,0:T(4,128)S(1)} %all-to-all-done.blocks, f32[3,4,16,128]{3,2,1,0:T(8,128)S(1)} %get-tuple-element.54._.window_one, f32[18,8,128]{2,1,0:T(8,128)S(1)} %collective-permute-done.6.one_near, f32[18,8,128]{2,1,0:T(8,128)S(1)} %collective-permute-done.7.one_far, ...), custom_call_target="tpu_custom_call" | custom-call | tf_op jit(solution)/shard_map/pallas_call | solution.py:948
Async XLA Ops:
  1.2 10.3 %collective-permute-start = (f32[9,8,256]{2,1,0:T(8,128)S(1)}, f32[9,8,256]{2,1,0:T(8,128)S(1)}, u32[]{:S(2)}, u32[]{:S(2)}) collective-permute-start(f32[9,8,256]{2,1,0:T(8,128)S(1)} %get-tuple-element.42), channel_id=1, source_target_pairs={{0,1},{1,2},{2,3},{3,0},{4,5},{5,6},{6,7},{7,4},{8,9},{9,10},{10,1... | collective-permute-start | bytes 221192 | tf_op jit(solution)/shard_map/ppermute | solution.py:960
  1.7 9.7 %collective-permute-start.1 = (f32[9,8,256]{2,1,0:T(8,128)S(1)}, f32[9,8,256]{2,1,0:T(8,128)S(1)}, u32[]{:S(2)}, u32[]{:S(2)}) collective-permute-start(f32[9,8,256]{2,1,0:T(8,128)S(1)} %get-tuple-element.43), channel_id=1, source_target_pairs={{1,0},{2,1},{3,2},{0,3},{5,4},{6,5},{7,6},{4,7},{9,8},{10,9},{11,1... | collective-permute-start | bytes 221192 | tf_op jit(solution)/shard_map/ppermute | solution.py:961
  4.8 19.3 %all-to-all-start.1 = ((f32[32,4,128]{2,1,0:T(4,128)}), f32[32,4,128]{2,1,0:T(4,128)S(1)}, u32[]{:S(2)}, u32[]{:S(2)}) async-start(f32[32,4,128]{2,1,0:T(4,128)} %get-tuple-element.66), calls=%async_computation.1 | async-start | bytes 131072 | tf_op jit(solution)/shard_map/all_to_all | solution.py:976
  11.8 9.0 %collective-permute-start.2 = (f32[15,8,256]{2,1,0:T(8,128)S(1)}, f32[15,8,256]{2,1,0:T(8,128)S(1)}, u32[]{:S(2)}, u32[]{:S(2)}) collective-permute-start(f32[15,8,256]{2,1,0:T(8,128)S(1)} %get-tuple-element.47), channel_id=1, source_target_pairs={{0,4},{4,8},{8,12},{12,16},{16,20},{20,24},{24,28},{28,0},{1,5},{5... | collective-permute-start | bytes 368648 | tf_op jit(solution)/shard_map/ppermute | solution.py:960
  13.6 8.1 %collective-permute-start.3 = (f32[15,8,256]{2,1,0:T(8,128)S(1)}, f32[15,8,256]{2,1,0:T(8,128)S(1)}, u32[]{:S(2)}, u32[]{:S(2)}) collective-permute-start(f32[15,8,256]{2,1,0:T(8,128)S(1)} %get-tuple-element.48), channel_id=1, source_target_pairs={{4,0},{8,4},{12,8},{16,12},{20,16},{24,20},{28,24},{0,28},{5,1},{9... | collective-permute-start | bytes 368648 | tf_op jit(solution)/shard_map/ppermute | solution.py:961
  24.2 17.4 %all-to-all-start = ((f32[32,3,4,128]{3,2,1,0:T(4,128)}), f32[32,3,4,128]{3,2,1,0:T(4,128)S(1)}, u32[]{:S(2)}, u32[]{:S(2)}) async-start(f32[32,3,4,128]{3,2,1,0:T(4,128)} %get-tuple-element.49), calls=%async_computation | async-start | bytes 393216 | tf_op jit(solution)/shard_map/all_to_all | solution.py:976
  28.3 3.5 %collective-permute-start.4 = (f32[8,8,128]{2,1,0:T(8,128)S(1)}, f32[8,8,128]{2,1,0:T(8,128)S(1)}, u32[]{:S(2)}, u32[]{:S(2)}) collective-permute-start(f32[8,8,128]{2,1,0:T(8,128)S(1)} %get-tuple-element.52), channel_id=1, source_target_pairs={{0,1},{1,2},{2,3},{3,0},{4,5},{5,6},{6,7},{7,4},{8,9},{9,10},{10,1... | collective-permute-start | bytes 98312 | tf_op jit(solution)/shard_map/ppermute | solution.py:960
  28.6 3.2 %collective-permute-start.5 = (f32[8,8,128]{2,1,0:T(8,128)S(1)}, f32[8,8,128]{2,1,0:T(8,128)S(1)}, u32[]{:S(2)}, u32[]{:S(2)}) collective-permute-start(f32[8,8,128]{2,1,0:T(8,128)S(1)} %get-tuple-element.53), channel_id=1, source_target_pairs={{1,0},{2,1},{3,2},{0,3},{5,4},{6,5},{7,6},{4,7},{9,8},{10,9},{11,1... | collective-permute-start | bytes 98312 | tf_op jit(solution)/shard_map/ppermute | solution.py:961
  31.9 9.7 %collective-permute-start.6 = (f32[18,8,128]{2,1,0:T(8,128)S(1)}, f32[18,8,128]{2,1,0:T(8,128)S(1)}, u32[]{:S(2)}, u32[]{:S(2)}) collective-permute-start(f32[18,8,128]{2,1,0:T(8,128)S(1)} %get-tuple-element.55), channel_id=1, source_target_pairs={{0,4},{4,0},{8,12},{12,8},{16,20},{20,16},{24,28},{28,24},{1,5},{5... | collective-permute-start | bytes 221192 | tf_op jit(solution)/shard_map/ppermute | solution.py:971
  33.9 7.7 %collective-permute-start.7 = (f32[18,8,128]{2,1,0:T(8,128)S(1)}, f32[18,8,128]{2,1,0:T(8,128)S(1)}, u32[]{:S(2)}, u32[]{:S(2)}) collective-permute-start(f32[18,8,128]{2,1,0:T(8,128)S(1)} %get-tuple-element.56), channel_id=1, source_target_pairs={{0,28},{4,8},{8,4},{12,16},{16,12},{20,24},{24,20},{28,0},{1,29},{... | collective-permute-start | bytes 221192 | tf_op jit(solution)/shard_map/ppermute | solution.py:970

commit v6 on v4

--- a/solution.py
+++ b/solution.py
@@ -251,7 +251,7 @@
     return (len(BASE_PLANES) + 1) * tile_y // ROWS + -(-loose // ROWS) + 1
 
 
-def shrink(material, k_tile, k_two, halves, halves_one, paired, paired_one):
+def shrink(material, k_tile, blocks, halves, halves_one, paired, paired_one):
     tile_x, tile_y, size_z = material.shape
     tile_x1, tile_y1, size_z1 = tile_x // 2, tile_y // 2, size_z // 2
     k_one = None
@@ -283,7 +283,8 @@
         part = times_right(piece, halve_lanes(size_z1, LANES, pair * size_z1 // 2))
         block = part if block is None else block + part
     block = 0.125 * block
-    k_two[...] = block
+    for device in range(blocks.shape[0]):
+        blocks[device] = block
     for chunk in range(size_z // LANES):
         halves[chunk] = halve_lanes(LANES, size_z1, chunk * LANES // 2)
     for half in range(2):
@@ -291,7 +292,7 @@
 
 
 def fine_down(
-    window, k_two, halves, halves_one, from_low, from_high,
+    window, halves, halves_one, from_low, from_high,
     v_zero, forcing_out, cx, cy, cz, weight, level_one, blocks_out, to_low, to_high,
     conc_rim, forcing_rim, kappa_rim, once, diag, paired, blocks, left,
     k_one, f_one, u_one, v_one, cx1, cy1, cz1, w1, d1, paired_one, packed,
@@ -432,10 +433,7 @@
     used = tile_y1 // 2 + RC
     block = jnp.concatenate([result[p * ROWS : p * ROWS + used] for p in range(half_pairs)], 0)
     block = 0.125 * block
-    k_block = k_two[...]
-    for device in range(blocks.shape[0]):
-        blocks[device, blocks.shape[1] - 1] = k_block
-    for part in range(blocks.shape[1] - 1):
+    for part in range(blocks.shape[1]):
         piece = block[part * SHORT : (part + 1) * SHORT]
         for device in range(blocks.shape[0]):
             blocks[device, part] = piece
@@ -681,6 +679,16 @@
     return grids
 
 
+class Operator:
+    def __init__(self, ref):
+        self.ref = ref
+
+    def __getitem__(self, part):
+        if isinstance(part, slice):
+            return [self.ref[p] for p in range(*part.indices(5))]
+        return self.ref[part]
+
+
 def kappa_of(blocks, counts, grid):
     count_x, count_y = counts
     planes, rows, size_z2 = grid.sizes
@@ -689,10 +697,9 @@
     share = ROWS // half_y
     kappa = [[None] * (rows // ROWS) for _ in range(planes)]
     lane = iota((ROWS, LANES), 1)
-    at = blocks.shape[1] - 1
     for tx in range(count_x):
         for group in range(rows // ROWS):
-            pieces = [blocks[tx * count_y + group * share + n, at] for n in range(share)]
+            pieces = [blocks[tx * count_y + group * share + n] for n in range(share)]
             piece = jnp.concatenate(pieces, 0)
             turned = pltpu.roll(piece, size_z2, 1)
             for p in range(half_x):
@@ -701,12 +708,14 @@
     return jnp.concatenate([jnp.concatenate(groups, 0)[None] for groups in kappa], 0)
 
 
-def prepare(kappa, grids):
-    kappas = [kappa]
+def prepare(counts, grids, blocks, _, *outputs):
+    kappas = [kappa_of(blocks, counts, grids[0])]
     for grid in grids[:-1]:
         kappas.append(restrict_whole(kappas[-1], grid))
-    exact = ExactSolve(grids[-1], kappas[-1])
-    return [(grid, whole_operator(k, grid)) for grid, k in zip(grids[:-1], kappas)], exact
+    outputs[-1][...] = ExactSolve(grids[-1], kappas[-1]).inverse
+    for number, grid in enumerate(grids[:-1]):
+        for part, value in enumerate(whole_operator(kappas[number], grid)):
+            outputs[number][part] = value
 
 
 def selectors(sizes, planes1, tile_x1, tile_y1, rows, _, left_one, right_one, left_zero, right_zero):
@@ -795,6 +804,7 @@
     counts, grids, blocks, window_one, one_near, one_far, row_low, row_high,
     v_zero, forcing0, cx, cy, cz, weight, left_one, right_one, left_zero, right_zero, *rest,
 ):
+    prepared, rest = rest[: len(grids)], rest[len(grids) :]
     (
         out, mixed_low, mixed_high, kappa_low, kappa_high, first_low, first_high,
         v_one, cx1, cy1, cz1, w1, one_a, one_b, zero_a, zero_b,
@@ -807,7 +817,8 @@
     half_x, half_y, size_z2 = tile_x1 // 2, tile_y1 // 2, size_z1 // 2
     sizes = grids[0].sizes
     forcing2 = assemble(blocks, count_x, count_y, half_x, half_y, size_z2)
-    levels, exact = prepare(kappa_of(blocks, counts, grids[0]), grids)
+    levels = [(grid, Operator(prepared[number])) for number, grid in enumerate(grids[:-1])]
+    exact = ExactSolve(grids[-1], inverse=prepared[-1][...])
 
     planes1 = tile_x1 + 2 * R1
     for message, mixed, kappa_rim, low in (
@@ -970,12 +981,12 @@
     def bits(*shape):
         return jax.ShapeDtypeStruct(shape, BF16)
 
-    k_tile, k_two, halves, halves_one = call(
+    k_tile, kappa_blocks, halves, halves_one = call(
         shrink,
         inputs[2:],
         (
             one_tile,
-            (two_tile[1], LANES),
+            (everyone, two_tile[1], LANES),
             bits(chunks, LANES, one_tile[2]),
             bits(2, one_tile[2], one_tile[2]),
         ),
@@ -989,16 +1000,17 @@
         ((rows, size_z),),
     )
     from_low, from_high = shift_both(to_low, to_high, "tx")
+    kappa_blocks = to_everyone(kappa_blocks)
     wide = -(-rows // (2 * ROWS)) * ROWS
     small = (one_tile[0] + 2 * RC, wide, one_tile[2])
     pairs1 = small[0] // 2
-    short = pairs1 // 2 * (two_tile[1] + RC) // SHORT + 1
+    short = pairs1 // 2 * (two_tile[1] + RC) // SHORT
     assert pairs1 // 2 * (two_tile[1] + RC) % SHORT == 0
     message = (3 * one_tile[0] * R1 // ROWS + chunks, ROWS, LANES)
     assert one_tile[2] == LANES and tile_x <= ROWS and one_tile[1] == ROWS
     v_zero, forcing0, cx, cy, cz, weight, level_one, blocks, to_low, to_high = call(
         fine_down,
-        (window, k_two, halves, halves_one, from_low, from_high),
+        (window, halves, halves_one, from_low, from_high),
         (inner, inner, (tile_x + 3, rows, size_z), inner, inner, inner)
         + ((3,) + one_tile, (everyone, short, SHORT, LANES), message, message),
         (
@@ -1039,11 +1051,19 @@
         ),
         (),
     )
+    lattice = grids[0].sizes[1], LANES
+    prepared = call(
+        functools.partial(prepare, counts, grids),
+        (kappa_blocks, window_one),
+        tuple((5, grid.sizes[0]) + lattice for grid in grids[:-1])
+        + ((-(-grids[-1].cells // ROWS) * ROWS, LANES),),
+        (),
+    )
     rim = (R1,) + one[1:]
     (updated,) = call(
         functools.partial(coarse_up, counts, grids),
         (blocks, window_one, one_near, one_far, row_low, row_high)
-        + (v_zero, forcing0, cx, cy, cz, weight, *chosen),
+        + (v_zero, forcing0, cx, cy, cz, weight, *chosen, *prepared),
         (concentration.shape,),
         (rim,) * 6 + (one,) * 7 + (zero, zero),
     )

time: 43.2 us -> 45.5 us (1.053)
  starting transfers between devices: 20 us -> 26 us
  waiting for transfers between devices: 12 us -> 6.87 us
  Pallas kernels: 10.9 us -> 12.2 us
    all_to_all x1 -> x2, starting transfers between devices: 4.5 us -> 10.8 us  [to_everyone(): return lax.all_to_all(blocks, ('tx', 'ty'), 0, 0)]
    ppermute x1, waiting for transfers between devices: 2.66 us -> 0.01 us  [swap_both(): from_far = lax.ppermute(far, axis, other)]
    ppermute x3, waiting for transfers between devices: 2.68 us -> 0.95 us  [shift_both(): lax.ppermute(to_low, axis, [((i + 1) % count, i) for i in range(count)])]
    pallas_call x7 -> x8, Pallas kernels: 10.9 us -> 12.2 us  [call(): pl.pallas_call(kernel, in_specs=[spec] * len(operands), out_specs=[IN_PLA...]
    ppermute x3, waiting for transfers between devices: 6.63 us -> 5.91 us  [shift_both(): lax.ppermute(to_high, axis, [(i, (i + 1) % count) for i in range(count)])]
  transfers between devices with their start and end apart: 9 -> 10, of which waited for: 6 -> 3; matrix products, arithmetic and copies ran while one was open for 0% -> 0% of each run, Pallas kernels for 2% -> 16%
where the time goes in v6:
time: 45.5 us; the launch traced here: 45.2 us
  starting transfers between devices  26 us (57%)
  Pallas kernels  12.2 us (27%)
  waiting for transfers between devices  6.87 us (15%)
    pallas_call x8, Pallas kernels, call(): pl.pallas_call(kernel, in_specs=[spec] * len(operands), out_specs=[IN_PLA...  12.2 us
    all_to_all x2, starting transfers between devices, to_everyone(): return lax.all_to_all(blocks, ('tx', 'ty'), 0, 0)  10.8 us
    ppermute x3, starting transfers between devices, shift_both(): lax.ppermute(to_low, axis, [((i + 1) % count, i) for i in range(count)])  6.43 us
    ppermute x3, waiting for transfers between devices, shift_both(): lax.ppermute(to_high, axis, [(i, (i + 1) % count) for i in range(count)])  5.91 us
    ppermute x1, starting transfers between devices, swap_both(): from_far = lax.ppermute(far, axis, other)  4.16 us
    ppermute x3, starting transfers between devices, shift_both(): lax.ppermute(to_high, axis, [(i, (i + 1) % count) for i in range(count)])  2.67 us
    ppermute x1, starting transfers between devices, swap_both(): from_near = lax.ppermute(near, axis, partner)  2.03 us
    ppermute x3, waiting for transfers between devices, shift_both(): lax.ppermute(to_low, axis, [((i + 1) % count, i) for i in range(count)])  0.95 us
  transfers between devices with their start and end apart: 10, of which 3 were waited for; matrix products, arithmetic and copies ran while one was open for 0% of the time, Pallas kernels for 16%

profile of v6, /device:TPU:0, one launch (start us, length us, event | category | flops | bytes accessed | tf_op | source)
XLA Modules:
  0.0 45.2 jit_solution(9298207921355132364)
XLA Ops:
  0.0 1.2 %shard_map.37 = (f32[8,16,256]{2,1,0:T(8,128)S(1)}, f32[8,16,256]{2,1,0:T(8,128)S(1)}, s32[8,16,256]{2,1,0:T(8,128)S(1)}, f32[9,8,256]{2,1,0:T(8,128)S(1)}, f32[9,8,256]{2,1,0:T(8,128)S(1)}) custom-call(f32[8,16,256]{2,1,0:T(8,128)} %conc_in.1, f32[8,16,256]{2,1,0:T(8,128)} %source_in.1, s32[8,16,256]{2,1,0:T(8,128)} %material_in.1), custom_call_target="tpu_custom_call" | custom-call | tf_op jit(solution)/shard_map/pallas_call | solution.py:925
  1.2 0.5 %collective-permute-start = (f32[9,8,256]{2,1,0:T(8,128)S(1)}, f32[9,8,256]{2,1,0:T(8,128)S(1)}, u32[]{:S(2)}, u32[]{:S(2)}) collective-permute-start(f32[9,8,256]{2,1,0:T(8,128)S(1)} %get-tuple-element.42), channel_id=1, source_target_pairs={{0,1},{1,2},{2,3},{3,0},{4,5},{5,6},{6,7},{7,4},{8,9},{9,10},{10,1... | collective-permute-start | bytes 221192 | tf_op jit(solution)/shard_map/ppermute | solution.py:937
  1.7 2.0 %collective-permute-start.1 = (f32[9,8,256]{2,1,0:T(8,128)S(1)}, f32[9,8,256]{2,1,0:T(8,128)S(1)}, u32[]{:S(2)}, u32[]{:S(2)}) collective-permute-start(f32[9,8,256]{2,1,0:T(8,128)S(1)} %get-tuple-element.43), channel_id=1, source_target_pairs={{1,0},{2,1},{3,2},{0,3},{5,4},{6,5},{7,6},{4,7},{9,8},{10,9},{11,1... | collective-permute-start | bytes 221192 | tf_op jit(solution)/shard_map/ppermute | solution.py:938
  3.7 1.1 %shard_map.38 = (f32[4,8,128]{2,1,0:T(8,128)S(1)}, f32[32,4,128]{2,1,0:T(4,128)}, bf16[2,128,128]{2,1,0:T(8,128)(2,1)S(1)}, bf16[2,128,128]{2,1,0:T(8,128)(2,1)S(1)}) custom-call(s32[8,16,256]{2,1,0:T(8,128)S(1)} %get-tuple-element.40.material), custom_call_target="tpu_custom_call" | custom-call | tf_op jit(solution)/shard_map/pallas_call | solution.py:925
  4.8 6.6 %all-to-all-start.1 = ((f32[32,4,128]{2,1,0:T(4,128)}), f32[32,4,128]{2,1,0:T(4,128)S(1)}, u32[]{:S(2)}, u32[]{:S(2)}) async-start(f32[32,4,128]{2,1,0:T(4,128)} %get-tuple-element.66), calls=%async_computation.1 | async-start | bytes 131072 | tf_op jit(solution)/shard_map/all_to_all | solution.py:953
  11.5 0.0 collective-permute-done.from_low
  11.5 0.0 collective-permute-done.1.from_high
  11.5 0.3 shard_map.39
  11.8 1.8 %collective-permute-start.2 = (f32[15,8,256]{2,1,0:T(8,128)S(1)}, f32[15,8,256]{2,1,0:T(8,128)S(1)}, u32[]{:S(2)}, u32[]{:S(2)}) collective-permute-start(f32[15,8,256]{2,1,0:T(8,128)S(1)} %get-tuple-element.47), channel_id=1, source_target_pairs={{0,4},{4,8},{8,12},{12,16},{16,20},{20,24},{24,28},{28,0},{1,5},{5... | collective-permute-start | bytes 368648 | tf_op jit(solution)/shard_map/ppermute | solution.py:937
  13.6 3.0 %collective-permute-start.3 = (f32[15,8,256]{2,1,0:T(8,128)S(1)}, f32[15,8,256]{2,1,0:T(8,128)S(1)}, u32[]{:S(2)}, u32[]{:S(2)}) collective-permute-start(f32[15,8,256]{2,1,0:T(8,128)S(1)} %get-tuple-element.48), channel_id=1, source_target_pairs={{4,0},{8,4},{12,8},{16,12},{20,16},{24,20},{28,24},{0,28},{5,1},{9... | collective-permute-start | bytes 368648 | tf_op jit(solution)/shard_map/ppermute | solution.py:938
  16.6 4.2 %collective-permute-done.2.from_low = f32[15,8,256]{2,1,0:T(8,128)S(1)} collective-permute-done((f32[15,8,256]{2,1,0:T(8,128)S(1)}, f32[15,8,256]{2,1,0:T(8,128)S(1)}, u32[]{:S(2)}, u32[]{:S(2)}) %collective-permute-start.2) | collective-permute-done | bytes 122912 | tf_op jit(solution)/shard_map/ppermute | solution.py:937
  20.8 0.9 %collective-permute-done.3.from_high = f32[15,8,256]{2,1,0:T(8,128)S(1)} collective-permute-done((f32[15,8,256]{2,1,0:T(8,128)S(1)}, f32[15,8,256]{2,1,0:T(8,128)S(1)}, u32[]{:S(2)}, u32[]{:S(2)}) %collective-permute-start.3) | collective-permute-done | bytes 122912 | tf_op jit(solution)/shard_map/ppermute | solution.py:938
  21.8 2.4 %shard_map.40 = (f32[10,24,256]{2,1,0:T(8,128)S(1)}, f32[10,24,256]{2,1,0:T(8,128)S(1)}, f32[11,24,256]{2,1,0:T(8,128)S(1)}, f32[10,24,256]{2,1,0:T(8,128)S(1)},...) custom-call(f32[3,8,24,256]{3,2,1,0:T(8,128)S(1)} %get-tuple-element, ...), custom_call_target="tpu_custom_call" | custom-call | tf_op jit(solution)/shard_map/pallas_call | solution.py:925
  24.2 0.0 all-to-all-done.1.blocks
  24.2 4.2 %all-to-all-start = ((f32[32,3,4,128]{3,2,1,0:T(4,128)}), f32[32,3,4,128]{3,2,1,0:T(4,128)S(1)}, u32[]{:S(2)}, u32[]{:S(2)}) async-start(f32[32,3,4,128]{3,2,1,0:T(4,128)} %get-tuple-element.49), calls=%async_computation | async-start | bytes 393216 | tf_op jit(solution)/shard_map/all_to_all | solution.py:953
  28.3 0.3 collective-permute-start.4
  28.6 1.5 %collective-permute-start.5 = (f32[8,8,128]{2,1,0:T(8,128)S(1)}, f32[8,8,128]{2,1,0:T(8,128)S(1)}, u32[]{:S(2)}, u32[]{:S(2)}) collective-permute-start(f32[8,8,128]{2,1,0:T(8,128)S(1)} %get-tuple-element.53), channel_id=1, source_target_pairs={{1,0},{2,1},{3,2},{0,3},{5,4},{6,5},{7,6},{4,7},{9,8},{10,9},{11,1... | collective-permute-start | bytes 98312 | tf_op jit(solution)/shard_map/ppermute | solution.py:938
  30.1 1.7 %collective-permute-done.4.from_low.row_low = f32[8,8,128]{2,1,0:T(8,128)S(1)} collective-permute-done((f32[8,8,128]{2,1,0:T(8,128)S(1)}, f32[8,8,128]{2,1,0:T(8,128)S(1)}, u32[]{:S(2)}, u32[]{:S(2)}) %collective-permute-start.4) | collective-permute-done | bytes 32800 | tf_op jit(solution)/shard_map/ppermute | solution.py:937
  31.8 0.0 collective-permute-done.5.from_high.row_high
  31.8 0.1 shard_map.41
  31.9 2.0 %collective-permute-start.6 = (f32[18,8,128]{2,1,0:T(8,128)S(1)}, f32[18,8,128]{2,1,0:T(8,128)S(1)}, u32[]{:S(2)}, u32[]{:S(2)}) collective-permute-start(f32[18,8,128]{2,1,0:T(8,128)S(1)} %get-tuple-element.55), channel_id=1, source_target_pairs={{0,4},{4,0},{8,12},{12,8},{16,20},{20,16},{24,28},{28,24},{1,5},{5... | collective-permute-start | bytes 221192 | tf_op jit(solution)/shard_map/ppermute | solution.py:948
  33.9 4.2 %collective-permute-start.7 = (f32[18,8,128]{2,1,0:T(8,128)S(1)}, f32[18,8,128]{2,1,0:T(8,128)S(1)}, u32[]{:S(2)}, u32[]{:S(2)}) collective-permute-start(f32[18,8,128]{2,1,0:T(8,128)S(1)} %get-tuple-element.56), channel_id=1, source_target_pairs={{0,28},{4,8},{8,4},{12,16},{16,12},{20,24},{24,20},{28,0},{1,29},{... | collective-permute-start | bytes 221192 | tf_op jit(solution)/shard_map/ppermute | solution.py:947
  38.1 0.2 shard_map.42
  38.2 3.2 %shard_map.43 = (f32[5,16,16,128]{3,2,1,0:T(8,128)S(1)}, f32[5,8,16,128]{3,2,1,0:T(8,128)S(1)}, f32[5,4,16,128]{3,2,1,0:T(8,128)S(1)}, f32[32,128]{1,0:T(8,128)S(1)}) custom-call(f32[32,4,128]{2,1,0:T(4,128)S(1)} %all-to-all-done.1.blocks, f32[3,4,16,128]{3,2,1,0:T(8,128)S(1)} %get-tuple-element.54._.window_one), custom_call_target="tpu_custom_call" | custom-call | tf_op jit(solution)/shard_map/pallas_call | solution.py:925
  41.5 0.0 collective-permute-done.6.one_near
  41.5 0.0 collective-permute-done.7.one_far
  41.5 0.0 all-to-all-done.blocks
  41.5 3.7 %shard_map.44 = f32[8,16,256]{2,1,0:T(8,128)} custom-call(f32[32,3,4,128]{3,2,1,0:T(4,128)S(1)} %all-to-all-done.blocks, f32[3,4,16,128]{3,2,1,0:T(8,128)S(1)} %get-tuple-element.54._.window_one, f32[18,8,128]{2,1,0:T(8,128)S(1)} %collective-permute-done.6.one_near, f32[18,8,128]{2,1,0:T(8,128)S(1)} %collective-permute-done.7.one_far, ...), custom_call_target="tpu_custom_call" | custom-call | tf_op jit(solution)/shard_map/pallas_call | solution.py:925
Async XLA Ops:
  1.2 10.3 %collective-permute-start = (f32[9,8,256]{2,1,0:T(8,128)S(1)}, f32[9,8,256]{2,1,0:T(8,128)S(1)}, u32[]{:S(2)}, u32[]{:S(2)}) collective-permute-start(f32[9,8,256]{2,1,0:T(8,128)S(1)} %get-tuple-element.42), channel_id=1, source_target_pairs={{0,1},{1,2},{2,3},{3,0},{4,5},{5,6},{6,7},{7,4},{8,9},{9,10},{10,1... | collective-permute-start | bytes 221192 | tf_op jit(solution)/shard_map/ppermute | solution.py:937
  1.7 9.7 %collective-permute-start.1 = (f32[9,8,256]{2,1,0:T(8,128)S(1)}, f32[9,8,256]{2,1,0:T(8,128)S(1)}, u32[]{:S(2)}, u32[]{:S(2)}) collective-permute-start(f32[9,8,256]{2,1,0:T(8,128)S(1)} %get-tuple-element.43), channel_id=1, source_target_pairs={{1,0},{2,1},{3,2},{0,3},{5,4},{6,5},{7,6},{4,7},{9,8},{10,9},{11,1... | collective-permute-start | bytes 221192 | tf_op jit(solution)/shard_map/ppermute | solution.py:938
  4.8 19.3 %all-to-all-start.1 = ((f32[32,4,128]{2,1,0:T(4,128)}), f32[32,4,128]{2,1,0:T(4,128)S(1)}, u32[]{:S(2)}, u32[]{:S(2)}) async-start(f32[32,4,128]{2,1,0:T(4,128)} %get-tuple-element.66), calls=%async_computation.1 | async-start | bytes 131072 | tf_op jit(solution)/shard_map/all_to_all | solution.py:953
  11.8 9.0 %collective-permute-start.2 = (f32[15,8,256]{2,1,0:T(8,128)S(1)}, f32[15,8,256]{2,1,0:T(8,128)S(1)}, u32[]{:S(2)}, u32[]{:S(2)}) collective-permute-start(f32[15,8,256]{2,1,0:T(8,128)S(1)} %get-tuple-element.47), channel_id=1, source_target_pairs={{0,4},{4,8},{8,12},{12,16},{16,20},{20,24},{24,28},{28,0},{1,5},{5... | collective-permute-start | bytes 368648 | tf_op jit(solution)/shard_map/ppermute | solution.py:937
  13.6 8.1 %collective-permute-start.3 = (f32[15,8,256]{2,1,0:T(8,128)S(1)}, f32[15,8,256]{2,1,0:T(8,128)S(1)}, u32[]{:S(2)}, u32[]{:S(2)}) collective-permute-start(f32[15,8,256]{2,1,0:T(8,128)S(1)} %get-tuple-element.48), channel_id=1, source_target_pairs={{4,0},{8,4},{12,8},{16,12},{20,16},{24,20},{28,24},{0,28},{5,1},{9... | collective-permute-start | bytes 368648 | tf_op jit(solution)/shard_map/ppermute | solution.py:938
  24.2 17.3 %all-to-all-start = ((f32[32,3,4,128]{3,2,1,0:T(4,128)}), f32[32,3,4,128]{3,2,1,0:T(4,128)S(1)}, u32[]{:S(2)}, u32[]{:S(2)}) async-start(f32[32,3,4,128]{3,2,1,0:T(4,128)} %get-tuple-element.49), calls=%async_computation | async-start | bytes 393216 | tf_op jit(solution)/shard_map/all_to_all | solution.py:953
  28.3 3.5 %collective-permute-start.4 = (f32[8,8,128]{2,1,0:T(8,128)S(1)}, f32[8,8,128]{2,1,0:T(8,128)S(1)}, u32[]{:S(2)}, u32[]{:S(2)}) collective-permute-start(f32[8,8,128]{2,1,0:T(8,128)S(1)} %get-tuple-element.52), channel_id=1, source_target_pairs={{0,1},{1,2},{2,3},{3,0},{4,5},{5,6},{6,7},{7,4},{8,9},{9,10},{10,1... | collective-permute-start | bytes 98312 | tf_op jit(solution)/shard_map/ppermute | solution.py:937
  28.6 3.2 %collective-permute-start.5 = (f32[8,8,128]{2,1,0:T(8,128)S(1)}, f32[8,8,128]{2,1,0:T(8,128)S(1)}, u32[]{:S(2)}, u32[]{:S(2)}) collective-permute-start(f32[8,8,128]{2,1,0:T(8,128)S(1)} %get-tuple-element.53), channel_id=1, source_target_pairs={{1,0},{2,1},{3,2},{0,3},{5,4},{6,5},{7,6},{4,7},{9,8},{10,9},{11,1... | collective-permute-start | bytes 98312 | tf_op jit(solution)/shard_map/ppermute | solution.py:938
  31.9 9.6 %collective-permute-start.6 = (f32[18,8,128]{2,1,0:T(8,128)S(1)}, f32[18,8,128]{2,1,0:T(8,128)S(1)}, u32[]{:S(2)}, u32[]{:S(2)}) collective-permute-start(f32[18,8,128]{2,1,0:T(8,128)S(1)} %get-tuple-element.55), channel_id=1, source_target_pairs={{0,4},{4,0},{8,12},{12,8},{16,20},{20,16},{24,28},{28,24},{1,5},{5... | collective-permute-start | bytes 221192 | tf_op jit(solution)/shard_map/ppermute | solution.py:948
  33.9 7.6 %collective-permute-start.7 = (f32[18,8,128]{2,1,0:T(8,128)S(1)}, f32[18,8,128]{2,1,0:T(8,128)S(1)}, u32[]{:S(2)}, u32[]{:S(2)}) collective-permute-start(f32[18,8,128]{2,1,0:T(8,128)S(1)} %get-tuple-element.56), channel_id=1, source_target_pairs={{0,28},{4,8},{8,4},{12,16},{16,12},{20,24},{24,20},{28,0},{1,29},{... | collective-permute-start | bytes 221192 | tf_op jit(solution)/shard_map/ppermute | solution.py:947

commit v7 on v6

--- a/solution.py
+++ b/solution.py
@@ -47,20 +47,6 @@
     return Planes(first, [(ref, x) for x in range(ref.shape[0])])
 
 
-def is_even(axis):
-    return lax.rem(lax.axis_index(axis), 2) == 0
-
-
-def on_sides(axis, near, far, body):
-    @pl.when(is_even(axis))
-    def _():
-        body(far, near)
-
-    @pl.when(jnp.logical_not(is_even(axis)))
-    def _():
-        body(near, far)
-
-
 class Picked:
     def __init__(self, flag, when_true, when_false):
         self.flag = flag
@@ -71,11 +57,6 @@
         first, second = self.when_true[index], self.when_false[index]
         flag = jnp.where(self.flag, jnp.int32(1), jnp.int32(0))
         return jnp.where(jnp.full(first.shape, flag) == 1, first, second)
-
-
-def by_side(axis, near, far):
-    even = is_even(axis)
-    return Picked(even, far, near), Picked(even, near, far)
 
 
 def iota(shape, dim):
@@ -251,7 +232,7 @@
     return (len(BASE_PLANES) + 1) * tile_y // ROWS + -(-loose // ROWS) + 1
 
 
-def shrink(material, k_tile, blocks, halves, halves_one, paired, paired_one):
+def shrink(material, k_tile, blocks, halves, halves_one, twice_one, twice_zero, paired, paired_one):
     tile_x, tile_y, size_z = material.shape
     tile_x1, tile_y1, size_z1 = tile_x // 2, tile_y // 2, size_z // 2
     k_one = None
@@ -289,6 +270,8 @@
         halves[chunk] = halve_lanes(LANES, size_z1, chunk * LANES // 2)
     for half in range(2):
         halves_one[half] = halve_lanes(size_z1, size_z1, half * size_z1 // 2)
+    for twice in (twice_one, twice_zero):
+        twice[...] = ones_where(iota(twice.shape, 0) == div(iota(twice.shape, 1), 2))
 
 
 def fine_down(
@@ -464,7 +447,7 @@
     return R1 + 1 - layer
 
 
-def middle(level_one, v_zero, from_low, from_high, window, near, far):
+def middle(level_one, v_zero, from_low, from_high, window, to_low, to_high):
     _, tile_x1, tile_y1, _ = level_one.shape
     planes, rows, size_z = v_zero.shape
     top1 = R1 + tile_y1
@@ -478,41 +461,38 @@
     chunks = size_z // LANES
     top = rows - RY
 
-    def pack(to_low, to_high):
-        for to, low in ((to_low, True), (to_high, False)):
-            at = 0
-            for which in (0, 2):
-                for layer in range(1, R1 + 1):
-                    x = layer - 1 if low else tile_x1 - layer
-                    outer = 1 if which == 0 and layer == R1 else which
-                    to[at] = window[outer, x, R1:top1]
-                    at += 1
-            loose = at * ROWS
-            for which in (0, 2):
-                for layer in range(1, R1 + 1):
-                    x = layer - 1 if low else tile_x1 - layer
-                    outer = 1 if which == 0 else which
-                    for distance in range(1, reach_of(layer) + 1):
-                        source = outer if distance == reach_of(layer) else which
-                        for row in (R1 - distance, top1 + distance - 1):
-                            to[loose // ROWS, loose % ROWS : loose % ROWS + 1] = window[
-                                source, x, row : row + 1
-                            ]
-                            loose += 1
-            second, first = (2, 1) if low else (planes - 3, planes - 2)
-            for row in (RY - 1, top):
-                for chunk in range(chunks):
-                    lanes = slice(chunk * LANES, (chunk + 1) * LANES)
-                    to[loose // ROWS, loose % ROWS : loose % ROWS + 1] = v_zero[first, row : row + 1, lanes]
-                    loose += 1
-            at = -(-loose // ROWS)
+    for to, low in ((to_low, True), (to_high, False)):
+        at = 0
+        for which in (0, 2):
+            for layer in range(1, R1 + 1):
+                x = layer - 1 if low else tile_x1 - layer
+                outer = 1 if which == 0 and layer == R1 else which
+                to[at] = window[outer, x, R1:top1]
+                at += 1
+        loose = at * ROWS
+        for which in (0, 2):
+            for layer in range(1, R1 + 1):
+                x = layer - 1 if low else tile_x1 - layer
+                outer = 1 if which == 0 else which
+                for distance in range(1, reach_of(layer) + 1):
+                    source = outer if distance == reach_of(layer) else which
+                    for row in (R1 - distance, top1 + distance - 1):
+                        to[loose // ROWS, loose % ROWS : loose % ROWS + 1] = window[
+                            source, x, row : row + 1
+                        ]
+                        loose += 1
+        second, first = (2, 1) if low else (planes - 3, planes - 2)
+        for row in (RY - 1, top):
             for chunk in range(chunks):
                 lanes = slice(chunk * LANES, (chunk + 1) * LANES)
-                for half in range((top - RY) // ROWS):
-                    to[at] = v_zero[second, RY + half * ROWS : RY + (half + 1) * ROWS, lanes]
-                    at += 1
-
-    on_sides("tx", near, far, pack)
+                to[loose // ROWS, loose % ROWS : loose % ROWS + 1] = v_zero[first, row : row + 1, lanes]
+                loose += 1
+        at = -(-loose // ROWS)
+        for chunk in range(chunks):
+            lanes = slice(chunk * LANES, (chunk + 1) * LANES)
+            for half in range((top - RY) // ROWS):
+                to[at] = v_zero[second, RY + half * ROWS : RY + (half + 1) * ROWS, lanes]
+                at += 1
 
 
 def middle_tiles(tile_y, chunks):
@@ -718,35 +698,11 @@
             outputs[number][part] = value
 
 
-def selectors(sizes, planes1, tile_x1, tile_y1, rows, _, left_one, right_one, left_zero, right_zero):
-    rows1 = tile_y1 + 2 * R1
-    whole_x1, whole_y1 = 2 * sizes[0], 2 * sizes[1]
-    start_x = lax.axis_index("tx") * tile_x1 + (whole_x1 - R1)
-    start_y = lax.axis_index("ty") * tile_y1 + (whole_y1 - R1)
-    row = iota((planes1 * rows1, 1), 0)
-    at_x = mod(div(row, rows1) + start_x, whole_x1)
-    at_y = mod(mod(row, rows1) + start_y, whole_y1)
-    target = div(at_x, 2) * sizes[1] + div(at_y, 2)
-    left_one[...] = ones_where(iota(left_one.shape, 1) == target)
-    shape = right_one.shape
-    right_one[...] = ones_where(iota(shape, 0) == div(iota(shape, 1), 2))
-    row = iota((left_zero.shape[0], 1), 0)
-    target = div(row, rows) * rows1 + div(mod(row, rows) + (2 * R1 - RY), 2)
-    left_zero[...] = ones_where(iota(left_zero.shape, 1) == target)
-    shape = right_zero.shape
-    right_zero[...] = ones_where(iota(shape, 0) == div(iota(shape, 1), 2))
-
-
-def raise_level(left, right, v):
-    def terms(x):
-        high = x.astype(BF16)
-        return high, (x - high.astype(F32)).astype(BF16)
-
-    high, low = terms(v)
-    picked = jnp.dot(left, high, preferred_element_type=F32)
-    picked_low = jnp.dot(left, low, preferred_element_type=F32)
-    return jnp.dot(picked.astype(BF16), right, preferred_element_type=F32) + jnp.dot(
-        picked_low.astype(BF16), right, preferred_element_type=F32
+def spread_lanes(v, twice):
+    high = v.astype(BF16)
+    low = (v - high.astype(F32)).astype(BF16)
+    return jnp.dot(high, twice, preferred_element_type=F32) + jnp.dot(
+        low, twice, preferred_element_type=F32
     )
 
 
@@ -801,16 +757,15 @@
 
 
 def coarse_up(
-    counts, grids, blocks, window_one, one_near, one_far, row_low, row_high,
-    v_zero, forcing0, cx, cy, cz, weight, left_one, right_one, left_zero, right_zero, *rest,
+    counts, grids, blocks, window_one, one_low, one_high, row_low, row_high,
+    v_zero, forcing0, cx, cy, cz, weight, twice_one, twice_zero, *rest,
 ):
     prepared, rest = rest[: len(grids)], rest[len(grids) :]
     (
         out, mixed_low, mixed_high, kappa_low, kappa_high, first_low, first_high,
-        v_one, cx1, cy1, cz1, w1, one_a, one_b, zero_a, zero_b,
+        v_one, cx1, cy1, cz1, w1, one_a, one_b, zero_a, zero_b, lattice, raised_one, raised_zero,
     ) = rest
     count_x, count_y = counts
-    one_low, one_high = by_side("tx", one_near, one_far)
     _, tile_x1, rows1, size_z1 = window_one.shape
     tile_y1 = rows1 - 2 * R1
     top1 = R1 + tile_y1
@@ -862,11 +817,20 @@
     plane_sweep(start1, v_one, forcing1, cx1, cy1, cz1, w1, 1, planes1 - 1)
 
     solved = solve_whole(forcing2, levels, exact)
-    solved = solved.reshape(sizes[0] * sizes[1], LANES)
-
-    raised = raise_level(left_one[...], right_one[...], solved)
+    lattice[:, 0 : sizes[1]] = solved
+    wrap = rows1 // 2
+    lattice[:, sizes[1] :] = solved[:, 0:wrap]
+    start_x = lax.axis_index("tx") * half_x + (sizes[0] - R1 // 2)
+    start_y = lax.rem(lax.axis_index("ty") * half_y + (sizes[1] - R1 // 2), sizes[1])
+    pieces = [
+        lattice[lax.rem(start_x + x, sizes[0]), pl.ds(start_y, wrap)] for x in range(planes1 // 2)
+    ]
+    wide = spread_lanes(jnp.concatenate(pieces, 0), twice_one[...])
+    for x in range(planes1 // 2):
+        for parity in range(2):
+            raised_one[x, pl.ds(parity, wrap, stride=2)] = wide[x * wrap : (x + 1) * wrap]
     for x in range(1, planes1 - 1):
-        one_a[x] = v_one[x] + raised[x * rows1 : (x + 1) * rows1]
+        one_a[x] = v_one[x] + raised_one[x // 2]
     plane_sweep(one_a, one_b, forcing1, cx1, cy1, cz1, w1, 2, planes1 - 2)
     plane_sweep(one_b, one_a, forcing1, cx1, cy1, cz1, w1, 3, planes1 - 3)
 
@@ -875,8 +839,13 @@
     cx, cy, cz, weight = kept(cx, RX - 2), kept(cy, RX - 1), kept(cz, RX - 1), kept(weight, RX - 1)
     first, last = R1 - 1, planes1 - R1 + 1
     stack = jnp.concatenate([one_a[x] for x in range(first, last)], 0)
-    raised = raise_level(left_zero[...], right_zero[...], stack)
+    wide = spread_lanes(stack, twice_zero[...])
     chunks = size_z // LANES
+    for x in range(last - first):
+        for chunk in range(chunks):
+            piece = wide[x * rows1 : (x + 1) * rows1, chunk * LANES : (chunk + 1) * LANES]
+            for parity in range(2):
+                raised_zero[chunk, x, pl.ds(parity, rows1, stride=2)] = piece
     top = rows - RY
     for x in range(RX - 1, planes - RX + 1):
         zero_b[x] = v_zero[x]
@@ -907,7 +876,10 @@
                 at += 1
     for x in range(RX - 2, planes - RX + 2):
         at = (x - RX + 2 * R1) // 2 - first
-        zero_a[x] = zero_b[x] + raised[at * rows : (at + 1) * rows]
+        for chunk in range(chunks):
+            lanes = slice(chunk * LANES, (chunk + 1) * LANES)
+            raised = raised_zero[chunk, at, 2 * R1 - RY : 2 * R1 - RY + rows]
+            zero_a[x, :, lanes] = zero_b[x, :, lanes] + raised
     plane_sweep(zero_a, zero_b, forcing0, cx, cy, cz, weight, RX - 1, planes - RX + 1)
     plane_sweep(zero_b, zero_a, forcing0, cx, cy, cz, weight, RX, planes - RX)
     for x in range(planes - 2 * RX):
@@ -937,16 +909,6 @@
     from_low = lax.ppermute(to_high, axis, [(i, (i + 1) % count) for i in range(count)])
     from_high = lax.ppermute(to_low, axis, [((i + 1) % count, i) for i in range(count)])
     return from_low, from_high
-
-
-def swap_both(near, far, axis):
-    count = lax.axis_size(axis)
-    assert count % 2 == 0
-    partner = [(i, i ^ 1) for i in range(count)]
-    other = [(i, (i - 1 if i % 2 == 0 else i + 1) % count) for i in range(count)]
-    from_far = lax.ppermute(far, axis, other)
-    from_near = lax.ppermute(near, axis, partner)
-    return from_near, from_far
 
 
 def to_everyone(blocks):
@@ -981,7 +943,7 @@
     def bits(*shape):
         return jax.ShapeDtypeStruct(shape, BF16)
 
-    k_tile, kappa_blocks, halves, halves_one = call(
+    k_tile, kappa_blocks, halves, halves_one, *twice = call(
         shrink,
         inputs[2:],
         (
@@ -989,6 +951,8 @@
             (everyone, two_tile[1], LANES),
             bits(chunks, LANES, one_tile[2]),
             bits(2, one_tile[2], one_tile[2]),
+            bits(LANES, one_tile[2]),
+            bits(one_tile[2], size_z),
         ),
         ((one_tile[0], tile_y, LANES), one_tile[1:]),
     )
@@ -1031,26 +995,14 @@
     blocks = to_everyone(blocks)
     rows1 = one_tile[1] + 2 * R1
     message = (middle_tiles(tile_y, chunks), ROWS, LANES)
-    window_one, near, far = call(
+    window_one, to_low, to_high = call(
         middle,
         (level_one, v_zero, row_low, row_high),
         ((3, one_tile[0], rows1, one_tile[2]), message, message),
         (),
     )
-    one_near, one_far = swap_both(near, far, "tx")
+    one_low, one_high = shift_both(to_low, to_high, "tx")
     one = (one_tile[0] + 2 * R1, rows1, one_tile[2])
-    seen = one[0] - 2 * (R1 - 1)
-    chosen = call(
-        functools.partial(selectors, grids[0].sizes, one[0], one_tile[0], one_tile[1], rows),
-        (window_one,),
-        (
-            bits(one[0] * rows1, grids[0].sizes[0] * grids[0].sizes[1]),
-            bits(LANES, one_tile[2]),
-            bits(seen * rows, seen * rows1),
-            bits(one_tile[2], size_z),
-        ),
-        (),
-    )
     lattice = grids[0].sizes[1], LANES
     prepared = call(
         functools.partial(prepare, counts, grids),
@@ -1062,10 +1014,17 @@
     rim = (R1,) + one[1:]
     (updated,) = call(
         functools.partial(coarse_up, counts, grids),
-        (blocks, window_one, one_near, one_far, row_low, row_high)
-        + (v_zero, forcing0, cx, cy, cz, weight, *chosen, *prepared),
+        (blocks, window_one, one_low, one_high, row_low, row_high)
+        + (v_zero, forcing0, cx, cy, cz, weight, *twice, *prepared),
         (concentration.shape,),
-        (rim,) * 6 + (one,) * 7 + (zero, zero),
+        (rim,) * 6
+        + (one,) * 7
+        + (zero, zero)
+        + (
+            (grids[0].sizes[0], grids[0].sizes[1] + rows1 // 2, LANES),
+            (one[0] // 2, rows1, one[2]),
+            (chunks, (one[0] - 2 * (R1 - 1)), 2 * rows1, LANES),
+        ),
     )
     return updated
 

time: 45.5 us -> 44.6 us (0.980)
  Pallas kernels: 12.2 us -> 11.7 us
  starting transfers between devices: 26 us -> 25.5 us
    ppermute x2 -> x0, starting transfers between devices: 6.18 us -> none  [the longest x1 4.16 us: swap_both(): from_far = lax.ppermute(far, axis, other)]
    ppermute x3 -> x4, starting transfers between devices: 6.43 us -> 10.1 us  [shift_both(): lax.ppermute(to_low, axis, [((i + 1) % count, i) for i in range(count)])]
    ppermute x3 -> x4, starting transfers between devices: 2.67 us -> 4.68 us  [shift_both(): lax.ppermute(to_high, axis, [(i, (i + 1) % count) for i in range(count)])]
    pallas_call x8 -> x7, Pallas kernels: 12.2 us -> 11.7 us  [call(): pl.pallas_call(kernel, in_specs=[spec] * len(operands), out_specs=[IN_PLA...]
    ppermute x3 -> x4, waiting for transfers between devices: 0.95 us -> 0.96 us  [shift_both(): lax.ppermute(to_low, axis, [((i + 1) % count, i) for i in range(count)])]
    ppermute x3 -> x4, waiting for transfers between devices: 5.91 us -> 5.91 us  [shift_both(): lax.ppermute(to_high, axis, [(i, (i + 1) % count) for i in range(count)])]
where the time goes in v7:
time: 44.6 us; the launch traced here: 44.2 us
  starting transfers between devices  25.5 us (57%)
  Pallas kernels  11.7 us (26%)
  waiting for transfers between devices  6.87 us (15%)
    pallas_call x7, Pallas kernels, call(): pl.pallas_call(kernel, in_specs=[spec] * len(operands), out_specs=[IN_PLA...  11.7 us
    all_to_all x2, starting transfers between devices, to_everyone(): return lax.all_to_all(blocks, ('tx', 'ty'), 0, 0)  10.8 us
    ppermute x4, starting transfers between devices, shift_both(): lax.ppermute(to_low, axis, [((i + 1) % count, i) for i in range(count)])  10.1 us
    ppermute x4, waiting for transfers between devices, shift_both(): lax.ppermute(to_high, axis, [(i, (i + 1) % count) for i in range(count)])  5.91 us
    ppermute x4, starting transfers between devices, shift_both(): lax.ppermute(to_high, axis, [(i, (i + 1) % count) for i in range(count)])  4.68 us
    ppermute x4, waiting for transfers between devices, shift_both(): lax.ppermute(to_low, axis, [((i + 1) % count, i) for i in range(count)])  0.96 us
  transfers between devices with their start and end apart: 10, of which 3 were waited for; matrix products, arithmetic and copies ran while one was open for 0% of the time, Pallas kernels for 16%

profile of v7, /device:TPU:0, one launch (start us, length us, event | category | flops | bytes accessed | tf_op | source)
XLA Modules:
  0.0 44.2 jit_solution(10389403174640364278)
XLA Ops:
  0.0 1.2 %shard_map.37 = (f32[8,16,256]{2,1,0:T(8,128)S(1)}, f32[8,16,256]{2,1,0:T(8,128)S(1)}, s32[8,16,256]{2,1,0:T(8,128)S(1)}, f32[9,8,256]{2,1,0:T(8,128)S(1)}, f32[9,8,256]{2,1,0:T(8,128)S(1)}) custom-call(f32[8,16,256]{2,1,0:T(8,128)} %conc_in.1, f32[8,16,256]{2,1,0:T(8,128)} %source_in.1, s32[8,16,256]{2,1,0:T(8,128)} %material_in.1), custom_call_target="tpu_custom_call" | custom-call | tf_op jit(solution)/shard_map/pallas_call | solution.py:897
  1.2 0.5 %collective-permute-start = (f32[9,8,256]{2,1,0:T(8,128)S(1)}, f32[9,8,256]{2,1,0:T(8,128)S(1)}, u32[]{:S(2)}, u32[]{:S(2)}) collective-permute-start(f32[9,8,256]{2,1,0:T(8,128)S(1)} %get-tuple-element.40), channel_id=1, source_target_pairs={{0,1},{1,2},{2,3},{3,0},{4,5},{5,6},{6,7},{7,4},{8,9},{9,10},{10,1... | collective-permute-start | bytes 221192 | tf_op jit(solution)/shard_map/ppermute | solution.py:909
  1.7 2.0 %collective-permute-start.1 = (f32[9,8,256]{2,1,0:T(8,128)S(1)}, f32[9,8,256]{2,1,0:T(8,128)S(1)}, u32[]{:S(2)}, u32[]{:S(2)}) collective-permute-start(f32[9,8,256]{2,1,0:T(8,128)S(1)} %get-tuple-element.41), channel_id=1, source_target_pairs={{1,0},{2,1},{3,2},{0,3},{5,4},{6,5},{7,6},{4,7},{9,8},{10,9},{11,1... | collective-permute-start | bytes 221192 | tf_op jit(solution)/shard_map/ppermute | solution.py:910
  3.7 1.1 %shard_map.38 = (f32[4,8,128]{2,1,0:T(8,128)S(1)}, f32[32,4,128]{2,1,0:T(4,128)}, bf16[2,128,128]{2,1,0:T(8,128)(2,1)S(1)}, bf16[2,128,128]{2,1,0:T(8,128)(2,1)S...) custom-call(s32[8,16,256]{2,1,0:T(8,128)S(1)} %get-tuple-element.38.material), custom_call_target="tpu_custom_call" | custom-call | tf_op jit(solution)/shard_map/pallas_call | solution.py:897
  4.9 6.6 %all-to-all-start.1 = ((f32[32,4,128]{2,1,0:T(4,128)}), f32[32,4,128]{2,1,0:T(4,128)S(1)}, u32[]{:S(2)}, u32[]{:S(2)}) async-start(f32[32,4,128]{2,1,0:T(4,128)} %get-tuple-element.62), calls=%async_computation.1 | async-start | bytes 131072 | tf_op jit(solution)/shard_map/all_to_all | solution.py:915
  11.5 0.0 collective-permute-done.from_low
  11.5 0.0 collective-permute-done.1.from_high
  11.5 0.3 shard_map.39
  11.8 1.8 %collective-permute-start.2 = (f32[15,8,256]{2,1,0:T(8,128)S(1)}, f32[15,8,256]{2,1,0:T(8,128)S(1)}, u32[]{:S(2)}, u32[]{:S(2)}) collective-permute-start(f32[15,8,256]{2,1,0:T(8,128)S(1)} %get-tuple-element.45), channel_id=1, source_target_pairs={{0,4},{4,8},{8,12},{12,16},{16,20},{20,24},{24,28},{28,0},{1,5},{5... | collective-permute-start | bytes 368648 | tf_op jit(solution)/shard_map/ppermute | solution.py:909
  13.6 3.0 %collective-permute-start.3 = (f32[15,8,256]{2,1,0:T(8,128)S(1)}, f32[15,8,256]{2,1,0:T(8,128)S(1)}, u32[]{:S(2)}, u32[]{:S(2)}) collective-permute-start(f32[15,8,256]{2,1,0:T(8,128)S(1)} %get-tuple-element.46), channel_id=1, source_target_pairs={{4,0},{8,4},{12,8},{16,12},{20,16},{24,20},{28,24},{0,28},{5,1},{9... | collective-permute-start | bytes 368648 | tf_op jit(solution)/shard_map/ppermute | solution.py:910
  16.6 4.2 %collective-permute-done.2.from_low = f32[15,8,256]{2,1,0:T(8,128)S(1)} collective-permute-done((f32[15,8,256]{2,1,0:T(8,128)S(1)}, f32[15,8,256]{2,1,0:T(8,128)S(1)}, u32[]{:S(2)}, u32[]{:S(2)}) %collective-permute-start.2) | collective-permute-done | bytes 122912 | tf_op jit(solution)/shard_map/ppermute | solution.py:909
  20.8 0.9 %collective-permute-done.3.from_high = f32[15,8,256]{2,1,0:T(8,128)S(1)} collective-permute-done((f32[15,8,256]{2,1,0:T(8,128)S(1)}, f32[15,8,256]{2,1,0:T(8,128)S(1)}, u32[]{:S(2)}, u32[]{:S(2)}) %collective-permute-start.3) | collective-permute-done | bytes 122912 | tf_op jit(solution)/shard_map/ppermute | solution.py:910
  21.8 2.4 %shard_map.40 = (f32[10,24,256]{2,1,0:T(8,128)S(1)}, f32[10,24,256]{2,1,0:T(8,128)S(1)}, f32[11,24,256]{2,1,0:T(8,128)S(1)}, f32[10,24,256]{2,1,0:T(8,128)S(1)},...) custom-call(f32[3,8,24,256]{3,2,1,0:T(8,128)S(1)} %get-tuple-element, ...), custom_call_target="tpu_custom_call" | custom-call | tf_op jit(solution)/shard_map/pallas_call | solution.py:897
  24.2 0.0 all-to-all-done.1.blocks
  24.2 4.2 %all-to-all-start = ((f32[32,3,4,128]{3,2,1,0:T(4,128)}), f32[32,3,4,128]{3,2,1,0:T(4,128)S(1)}, u32[]{:S(2)}, u32[]{:S(2)}) async-start(f32[32,3,4,128]{3,2,1,0:T(4,128)} %get-tuple-element.47), calls=%async_computation | async-start | bytes 393216 | tf_op jit(solution)/shard_map/all_to_all | solution.py:915
  28.3 0.3 collective-permute-start.4
  28.6 1.5 %collective-permute-start.5 = (f32[8,8,128]{2,1,0:T(8,128)S(1)}, f32[8,8,128]{2,1,0:T(8,128)S(1)}, u32[]{:S(2)}, u32[]{:S(2)}) collective-permute-start(f32[8,8,128]{2,1,0:T(8,128)S(1)} %get-tuple-element.51), channel_id=1, source_target_pairs={{1,0},{2,1},{3,2},{0,3},{5,4},{6,5},{7,6},{4,7},{9,8},{10,9},{11,1... | collective-permute-start | bytes 98312 | tf_op jit(solution)/shard_map/ppermute | solution.py:910
  30.1 1.7 %collective-permute-done.4.from_low.row_low = f32[8,8,128]{2,1,0:T(8,128)S(1)} collective-permute-done((f32[8,8,128]{2,1,0:T(8,128)S(1)}, f32[8,8,128]{2,1,0:T(8,128)S(1)}, u32[]{:S(2)}, u32[]{:S(2)}) %collective-permute-start.4) | collective-permute-done | bytes 32800 | tf_op jit(solution)/shard_map/ppermute | solution.py:909
  31.8 0.0 collective-permute-done.5.from_high.row_high
  31.9 2.0 %collective-permute-start.6 = (f32[18,8,128]{2,1,0:T(8,128)S(1)}, f32[18,8,128]{2,1,0:T(8,128)S(1)}, u32[]{:S(2)}, u32[]{:S(2)}) collective-permute-start(f32[18,8,128]{2,1,0:T(8,128)S(1)} %get-tuple-element.53), channel_id=1, source_target_pairs={{0,4},{4,8},{8,12},{12,16},{16,20},{20,24},{24,28},{28,0},{1,5},{5... | collective-permute-start | bytes 221192 | tf_op jit(solution)/shard_map/ppermute | solution.py:909
  33.9 3.7 %collective-permute-start.7 = (f32[18,8,128]{2,1,0:T(8,128)S(1)}, f32[18,8,128]{2,1,0:T(8,128)S(1)}, u32[]{:S(2)}, u32[]{:S(2)}) collective-permute-start(f32[18,8,128]{2,1,0:T(8,128)S(1)} %get-tuple-element.54), channel_id=1, source_target_pairs={{4,0},{8,4},{12,8},{16,12},{20,16},{24,20},{28,24},{0,28},{5,1},{9... | collective-permute-start | bytes 221192 | tf_op jit(solution)/shard_map/ppermute | solution.py:910
  37.5 3.2 %shard_map.42 = (f32[5,16,16,128]{3,2,1,0:T(8,128)S(1)}, f32[5,8,16,128]{3,2,1,0:T(8,128)S(1)}, f32[5,4,16,128]{3,2,1,0:T(8,128)S(1)}, f32[32,128]{1,0:T(8,128)S(1)}) custom-call(f32[32,4,128]{2,1,0:T(4,128)S(1)} %all-to-all-done.1.blocks, f32[3,4,16,128]{3,2,1,0:T(8,128)S(1)} %get-tuple-element.52._.window_one), custom_call_target="tpu_custom_call" | custom-call | tf_op jit(solution)/shard_map/pallas_call | solution.py:897
  40.8 0.0 collective-permute-done.6.one_low
  40.8 0.0 collective-permute-done.7.one_high
  40.8 0.0 all-to-all-done.blocks
  40.8 3.4 %shard_map.43 = f32[8,16,256]{2,1,0:T(8,128)} custom-call(f32[32,3,4,128]{3,2,1,0:T(4,128)S(1)} %all-to-all-done.blocks, f32[3,4,16,128]{3,2,1,0:T(8,128)S(1)} %get-tuple-element.52._.window_one, f32[18,8,128]{2,1,0:T(8,128)S(1)} %collective-permute-done.6.one_low, f32[18,8,128]{2,1,0:T(8,128)S(1)} %collective-permute-done.7.one_high, ...), custom_call_target="tpu_custom_call" | custom-call | tf_op jit(solution)/shard_map/pallas_call | solution.py:897
  (1 shorter events, 0.0 us)
Async XLA Ops:
  1.2 10.3 %collective-permute-start = (f32[9,8,256]{2,1,0:T(8,128)S(1)}, f32[9,8,256]{2,1,0:T(8,128)S(1)}, u32[]{:S(2)}, u32[]{:S(2)}) collective-permute-start(f32[9,8,256]{2,1,0:T(8,128)S(1)} %get-tuple-element.40), channel_id=1, source_target_pairs={{0,1},{1,2},{2,3},{3,0},{4,5},{5,6},{6,7},{7,4},{8,9},{9,10},{10,1... | collective-permute-start | bytes 221192 | tf_op jit(solution)/shard_map/ppermute | solution.py:909
  1.7 9.8 %collective-permute-start.1 = (f32[9,8,256]{2,1,0:T(8,128)S(1)}, f32[9,8,256]{2,1,0:T(8,128)S(1)}, u32[]{:S(2)}, u32[]{:S(2)}) collective-permute-start(f32[9,8,256]{2,1,0:T(8,128)S(1)} %get-tuple-element.41), channel_id=1, source_target_pairs={{1,0},{2,1},{3,2},{0,3},{5,4},{6,5},{7,6},{4,7},{9,8},{10,9},{11,1... | collective-permute-start | bytes 221192 | tf_op jit(solution)/shard_map/ppermute | solution.py:910
  4.9 19.3 %all-to-all-start.1 = ((f32[32,4,128]{2,1,0:T(4,128)}), f32[32,4,128]{2,1,0:T(4,128)S(1)}, u32[]{:S(2)}, u32[]{:S(2)}) async-start(f32[32,4,128]{2,1,0:T(4,128)} %get-tuple-element.62), calls=%async_computation.1 | async-start | bytes 131072 | tf_op jit(solution)/shard_map/all_to_all | solution.py:915
  11.8 9.0 %collective-permute-start.2 = (f32[15,8,256]{2,1,0:T(8,128)S(1)}, f32[15,8,256]{2,1,0:T(8,128)S(1)}, u32[]{:S(2)}, u32[]{:S(2)}) collective-permute-start(f32[15,8,256]{2,1,0:T(8,128)S(1)} %get-tuple-element.45), channel_id=1, source_target_pairs={{0,4},{4,8},{8,12},{12,16},{16,20},{20,24},{24,28},{28,0},{1,5},{5... | collective-permute-start | bytes 368648 | tf_op jit(solution)/shard_map/ppermute | solution.py:909
  13.6 8.1 %collective-permute-start.3 = (f32[15,8,256]{2,1,0:T(8,128)S(1)}, f32[15,8,256]{2,1,0:T(8,128)S(1)}, u32[]{:S(2)}, u32[]{:S(2)}) collective-permute-start(f32[15,8,256]{2,1,0:T(8,128)S(1)} %get-tuple-element.46), channel_id=1, source_target_pairs={{4,0},{8,4},{12,8},{16,12},{20,16},{24,20},{28,24},{0,28},{5,1},{9... | collective-permute-start | bytes 368648 | tf_op jit(solution)/shard_map/ppermute | solution.py:910
  24.2 16.6 %all-to-all-start = ((f32[32,3,4,128]{3,2,1,0:T(4,128)}), f32[32,3,4,128]{3,2,1,0:T(4,128)S(1)}, u32[]{:S(2)}, u32[]{:S(2)}) async-start(f32[32,3,4,128]{3,2,1,0:T(4,128)} %get-tuple-element.47), calls=%async_computation | async-start | bytes 393216 | tf_op jit(solution)/shard_map/all_to_all | solution.py:915
  28.3 3.5 %collective-permute-start.4 = (f32[8,8,128]{2,1,0:T(8,128)S(1)}, f32[8,8,128]{2,1,0:T(8,128)S(1)}, u32[]{:S(2)}, u32[]{:S(2)}) collective-permute-start(f32[8,8,128]{2,1,0:T(8,128)S(1)} %get-tuple-element.50), channel_id=1, source_target_pairs={{0,1},{1,2},{2,3},{3,0},{4,5},{5,6},{6,7},{7,4},{8,9},{9,10},{10,1... | collective-permute-start | bytes 98312 | tf_op jit(solution)/shard_map/ppermute | solution.py:909
  28.6 3.2 %collective-permute-start.5 = (f32[8,8,128]{2,1,0:T(8,128)S(1)}, f32[8,8,128]{2,1,0:T(8,128)S(1)}, u32[]{:S(2)}, u32[]{:S(2)}) collective-permute-start(f32[8,8,128]{2,1,0:T(8,128)S(1)} %get-tuple-element.51), channel_id=1, source_target_pairs={{1,0},{2,1},{3,2},{0,3},{5,4},{6,5},{7,6},{4,7},{9,8},{10,9},{11,1... | collective-permute-start | bytes 98312 | tf_op jit(solution)/shard_map/ppermute | solution.py:910
  31.9 8.9 %collective-permute-start.6 = (f32[18,8,128]{2,1,0:T(8,128)S(1)}, f32[18,8,128]{2,1,0:T(8,128)S(1)}, u32[]{:S(2)}, u32[]{:S(2)}) collective-permute-start(f32[18,8,128]{2,1,0:T(8,128)S(1)} %get-tuple-element.53), channel_id=1, source_target_pairs={{0,4},{4,8},{8,12},{12,16},{16,20},{20,24},{24,28},{28,0},{1,5},{5... | collective-permute-start | bytes 221192 | tf_op jit(solution)/shard_map/ppermute | solution.py:909
  33.9 6.9 %collective-permute-start.7 = (f32[18,8,128]{2,1,0:T(8,128)S(1)}, f32[18,8,128]{2,1,0:T(8,128)S(1)}, u32[]{:S(2)}, u32[]{:S(2)}) collective-permute-start(f32[18,8,128]{2,1,0:T(8,128)S(1)} %get-tuple-element.54), channel_id=1, source_target_pairs={{4,0},{8,4},{12,8},{16,12},{20,16},{24,20},{28,24},{0,28},{5,1},{9... | collective-permute-start | bytes 221192 | tf_op jit(solution)/shard_map/ppermute | solution.py:910

commit v8 on v7

--- a/solution.py
+++ b/solution.py
@@ -14,6 +14,7 @@
 LANES = 128
 ROWS = 8
 SHORT = 4
+PIECES = 1
 RX = 2
 RY = 4
 R1 = 4
@@ -133,13 +134,25 @@
         out[x] = (1.0 - relax_weight) * v[x] + weight[x] * (forcing[x] + neighbours(v, cx, cy, cz, x))
 
 
+def pieces_of(pairs, parts, semaphores):
+    copies = []
+    for n, (whence, whither) in enumerate(pairs):
+        size = whence.shape[0] // parts
+        assert size * parts == whence.shape[0]
+        for part in range(parts):
+            piece = pl.ds(part * size, size)
+            copies.append(
+                pltpu.make_async_copy(
+                    whence.at[piece], whither.at[piece], semaphores.at[n * parts + part]
+                )
+            )
+    return copies
+
+
 def edges(conc_in, source_in, material_in, conc, source, material, to_low, to_high, arrived):
-    copies = [
-        pltpu.make_async_copy(whence, whither, arrived.at[n])
-        for n, (whence, whither) in enumerate(
-            ((conc_in, conc), (source_in, source), (material_in, material))
-        )
-    ]
+    copies = pieces_of(
+        ((conc_in, conc), (source_in, source), (material_in, material)), conc.shape[0] // 2, arrived
+    )
     for copy in copies:
         copy.start()
     for copy in copies:
@@ -420,8 +433,9 @@
         piece = block[part * SHORT : (part + 1) * SHORT]
         for device in range(blocks.shape[0]):
             blocks[device, part] = piece
-    copy = pltpu.make_async_copy(blocks, blocks_out, left)
-    copy.start()
+    copies = pieces_of(((blocks, blocks_out),), left.shape[0], left)
+    for copy in copies:
+        copy.start()
     for x in range(RX - 1, planes - RX + 1):
         forcing_out[x - RX + 1] = forcing[x]
 
@@ -440,7 +454,8 @@
             row = v_zero[x + 1, row0 : row0 + 1]
             for chunk in range(chunks):
                 to[start + chunk, x : x + 1] = row[:, chunk * LANES : (chunk + 1) * LANES]
-    copy.wait()
+    for copy in copies:
+        copy.wait()
 
 
 def reach_of(layer):
@@ -764,6 +779,7 @@
     (
         out, mixed_low, mixed_high, kappa_low, kappa_high, first_low, first_high,
         v_one, cx1, cy1, cz1, w1, one_a, one_b, zero_a, zero_b, lattice, raised_one, raised_zero,
+        finished, left,
     ) = rest
     count_x, count_y = counts
     _, tile_x1, rows1, size_z1 = window_one.shape
@@ -881,9 +897,13 @@
             raised = raised_zero[chunk, at, 2 * R1 - RY : 2 * R1 - RY + rows]
             zero_a[x, :, lanes] = zero_b[x, :, lanes] + raised
     plane_sweep(zero_a, zero_b, forcing0, cx, cy, cz, weight, RX - 1, planes - RX + 1)
-    plane_sweep(zero_b, zero_a, forcing0, cx, cy, cz, weight, RX, planes - RX)
+    copies = pieces_of(((finished, out),), finished.shape[0], left)
     for x in range(planes - 2 * RX):
-        out[x] = zero_a[x + RX, RY:top]
+        plane_sweep(zero_b, zero_a, forcing0, cx, cy, cz, weight, x + RX, x + RX + 1)
+        finished[x] = zero_a[x + RX, RY:top]
+        copies[x].start()
+    for copy in copies:
+        copy.wait()
 
 
 VM = pl.BlockSpec(memory_space=pltpu.VMEM)
@@ -930,7 +950,7 @@
         ),
         tuple(jax.ShapeDtypeStruct(v.shape, v.dtype) for v in (concentration, source, material))
         + (message, message),
-        (pltpu.SemaphoreType.DMA((3,)),),
+        (pltpu.SemaphoreType.DMA((3 * (tile_x // 2),)),),
         IN_PLACE,
     )
     from_low, from_high = shift_both(to_low, to_high, "ty")
@@ -985,7 +1005,7 @@
             zero,
             (chunks, max(small[0], tile_x), 2 * wide, LANES),
             (everyone, short, SHORT, LANES),
-            pltpu.SemaphoreType.DMA,
+            pltpu.SemaphoreType.DMA((PIECES,)),
         )
         + (small,) * 9
         + ((pairs1, wide, one_tile[2]), (pairs1, ROWS, one_tile[2])),
@@ -1024,7 +1044,10 @@
             (grids[0].sizes[0], grids[0].sizes[1] + rows1 // 2, LANES),
             (one[0] // 2, rows1, one[2]),
             (chunks, (one[0] - 2 * (R1 - 1)), 2 * rows1, LANES),
+            concentration.shape,
+            pltpu.SemaphoreType.DMA((tile_x,)),
         ),
+        in_hbm=(0,),
     )
     return updated
 

time: 44.6 us -> 44.6 us (level)
  no operation moved by 1% of the time
where the time goes in v8:
time: 44.6 us; the launch traced here: 44.2 us
  starting transfers between devices  25.5 us (57%)
  Pallas kernels  11.7 us (26%)
  waiting for transfers between devices  6.87 us (15%)
    pallas_call x7, Pallas kernels, call(): pl.pallas_call(kernel, in_specs=[spec] * len(operands), out_specs=[IN_PLA...  11.7 us
    all_to_all x2, starting transfers between devices, to_everyone(): return lax.all_to_all(blocks, ('tx', 'ty'), 0, 0)  10.8 us
    ppermute x4, starting transfers between devices, shift_both(): lax.ppermute(to_low, axis, [((i + 1) % count, i) for i in range(count)])  10.1 us
    ppermute x4, waiting for transfers between devices, shift_both(): lax.ppermute(to_high, axis, [(i, (i + 1) % count) for i in range(count)])  5.91 us
    ppermute x4, starting transfers between devices, shift_both(): lax.ppermute(to_high, axis, [(i, (i + 1) % count) for i in range(count)])  4.68 us
    ppermute x4, waiting for transfers between devices, shift_both(): lax.ppermute(to_low, axis, [((i + 1) % count, i) for i in range(count)])  0.96 us
  transfers between devices with their start and end apart: 10, of which 3 were waited for; matrix products, arithmetic and copies ran while one was open for 0% of the time, Pallas kernels for 16%

profile of v8, /device:TPU:0, one launch (start us, length us, event | category | flops | bytes accessed | tf_op | source)
XLA Modules:
  0.0 44.2 jit_solution(10719574231987569103)
XLA Ops:
  0.0 1.2 %shard_map.37 = (f32[8,16,256]{2,1,0:T(8,128)S(1)}, f32[8,16,256]{2,1,0:T(8,128)S(1)}, s32[8,16,256]{2,1,0:T(8,128)S(1)}, f32[9,8,256]{2,1,0:T(8,128)S(1)}, f32[9,8,256]{2,1,0:T(8,128)S(1)}) custom-call(f32[8,16,256]{2,1,0:T(8,128)} %conc_in.1, f32[8,16,256]{2,1,0:T(8,128)} %source_in.1, s32[8,16,256]{2,1,0:T(8,128)} %material_in.1), custom_call_target="tpu_custom_call" | custom-call | tf_op jit(solution)/shard_map/pallas_call | solution.py:917
  1.2 0.5 %collective-permute-start = (f32[9,8,256]{2,1,0:T(8,128)S(1)}, f32[9,8,256]{2,1,0:T(8,128)S(1)}, u32[]{:S(2)}, u32[]{:S(2)}) collective-permute-start(f32[9,8,256]{2,1,0:T(8,128)S(1)} %get-tuple-element.40), channel_id=1, source_target_pairs={{0,1},{1,2},{2,3},{3,0},{4,5},{5,6},{6,7},{7,4},{8,9},{9,10},{10,1... | collective-permute-start | bytes 221192 | tf_op jit(solution)/shard_map/ppermute | solution.py:929
  1.7 2.0 %collective-permute-start.1 = (f32[9,8,256]{2,1,0:T(8,128)S(1)}, f32[9,8,256]{2,1,0:T(8,128)S(1)}, u32[]{:S(2)}, u32[]{:S(2)}) collective-permute-start(f32[9,8,256]{2,1,0:T(8,128)S(1)} %get-tuple-element.41), channel_id=1, source_target_pairs={{1,0},{2,1},{3,2},{0,3},{5,4},{6,5},{7,6},{4,7},{9,8},{10,9},{11,1... | collective-permute-start | bytes 221192 | tf_op jit(solution)/shard_map/ppermute | solution.py:930
  3.7 1.1 %shard_map.38 = (f32[4,8,128]{2,1,0:T(8,128)S(1)}, f32[32,4,128]{2,1,0:T(4,128)}, bf16[2,128,128]{2,1,0:T(8,128)(2,1)S(1)}, bf16[2,128,128]{2,1,0:T(8,128)(2,1)S...) custom-call(s32[8,16,256]{2,1,0:T(8,128)S(1)} %get-tuple-element.38.material), custom_call_target="tpu_custom_call" | custom-call | tf_op jit(solution)/shard_map/pallas_call | solution.py:917
  4.8 6.6 %all-to-all-start.1 = ((f32[32,4,128]{2,1,0:T(4,128)}), f32[32,4,128]{2,1,0:T(4,128)S(1)}, u32[]{:S(2)}, u32[]{:S(2)}) async-start(f32[32,4,128]{2,1,0:T(4,128)} %get-tuple-element.62), calls=%async_computation.1 | async-start | bytes 131072 | tf_op jit(solution)/shard_map/all_to_all | solution.py:935
  11.4 0.0 collective-permute-done.from_low
  11.5 0.0 collective-permute-done.1.from_high
  11.5 0.3 shard_map.39
  11.8 1.8 %collective-permute-start.2 = (f32[15,8,256]{2,1,0:T(8,128)S(1)}, f32[15,8,256]{2,1,0:T(8,128)S(1)}, u32[]{:S(2)}, u32[]{:S(2)}) collective-permute-start(f32[15,8,256]{2,1,0:T(8,128)S(1)} %get-tuple-element.45), channel_id=1, source_target_pairs={{0,4},{4,8},{8,12},{12,16},{16,20},{20,24},{24,28},{28,0},{1,5},{5... | collective-permute-start | bytes 368648 | tf_op jit(solution)/shard_map/ppermute | solution.py:929
  13.6 3.0 %collective-permute-start.3 = (f32[15,8,256]{2,1,0:T(8,128)S(1)}, f32[15,8,256]{2,1,0:T(8,128)S(1)}, u32[]{:S(2)}, u32[]{:S(2)}) collective-permute-start(f32[15,8,256]{2,1,0:T(8,128)S(1)} %get-tuple-element.46), channel_id=1, source_target_pairs={{4,0},{8,4},{12,8},{16,12},{20,16},{24,20},{28,24},{0,28},{5,1},{9... | collective-permute-start | bytes 368648 | tf_op jit(solution)/shard_map/ppermute | solution.py:930
  16.6 4.2 %collective-permute-done.2.from_low = f32[15,8,256]{2,1,0:T(8,128)S(1)} collective-permute-done((f32[15,8,256]{2,1,0:T(8,128)S(1)}, f32[15,8,256]{2,1,0:T(8,128)S(1)}, u32[]{:S(2)}, u32[]{:S(2)}) %collective-permute-start.2) | collective-permute-done | bytes 122912 | tf_op jit(solution)/shard_map/ppermute | solution.py:929
  20.8 0.9 %collective-permute-done.3.from_high = f32[15,8,256]{2,1,0:T(8,128)S(1)} collective-permute-done((f32[15,8,256]{2,1,0:T(8,128)S(1)}, f32[15,8,256]{2,1,0:T(8,128)S(1)}, u32[]{:S(2)}, u32[]{:S(2)}) %collective-permute-start.3) | collective-permute-done | bytes 122912 | tf_op jit(solution)/shard_map/ppermute | solution.py:930
  21.7 2.4 %shard_map.40 = (f32[10,24,256]{2,1,0:T(8,128)S(1)}, f32[10,24,256]{2,1,0:T(8,128)S(1)}, f32[11,24,256]{2,1,0:T(8,128)S(1)}, f32[10,24,256]{2,1,0:T(8,128)S(1)},...) custom-call(f32[3,8,24,256]{3,2,1,0:T(8,128)S(1)} %get-tuple-element, ...), custom_call_target="tpu_custom_call" | custom-call | tf_op jit(solution)/shard_map/pallas_call | solution.py:917
  24.1 0.0 all-to-all-done.1.blocks
  24.1 4.2 %all-to-all-start = ((f32[32,3,4,128]{3,2,1,0:T(4,128)}), f32[32,3,4,128]{3,2,1,0:T(4,128)S(1)}, u32[]{:S(2)}, u32[]{:S(2)}) async-start(f32[32,3,4,128]{3,2,1,0:T(4,128)} %get-tuple-element.47), calls=%async_computation | async-start | bytes 393216 | tf_op jit(solution)/shard_map/all_to_all | solution.py:935
  28.3 0.3 collective-permute-start.4
  28.6 1.5 %collective-permute-start.5 = (f32[8,8,128]{2,1,0:T(8,128)S(1)}, f32[8,8,128]{2,1,0:T(8,128)S(1)}, u32[]{:S(2)}, u32[]{:S(2)}) collective-permute-start(f32[8,8,128]{2,1,0:T(8,128)S(1)} %get-tuple-element.51), channel_id=1, source_target_pairs={{1,0},{2,1},{3,2},{0,3},{5,4},{6,5},{7,6},{4,7},{9,8},{10,9},{11,1... | collective-permute-start | bytes 98312 | tf_op jit(solution)/shard_map/ppermute | solution.py:930
  30.1 1.7 %collective-permute-done.4.from_low.row_low = f32[8,8,128]{2,1,0:T(8,128)S(1)} collective-permute-done((f32[8,8,128]{2,1,0:T(8,128)S(1)}, f32[8,8,128]{2,1,0:T(8,128)S(1)}, u32[]{:S(2)}, u32[]{:S(2)}) %collective-permute-start.4) | collective-permute-done | bytes 32800 | tf_op jit(solution)/shard_map/ppermute | solution.py:929
  31.8 0.0 collective-permute-done.5.from_high.row_high
  31.8 2.0 %collective-permute-start.6 = (f32[18,8,128]{2,1,0:T(8,128)S(1)}, f32[18,8,128]{2,1,0:T(8,128)S(1)}, u32[]{:S(2)}, u32[]{:S(2)}) collective-permute-start(f32[18,8,128]{2,1,0:T(8,128)S(1)} %get-tuple-element.53), channel_id=1, source_target_pairs={{0,4},{4,8},{8,12},{12,16},{16,20},{20,24},{24,28},{28,0},{1,5},{5... | collective-permute-start | bytes 221192 | tf_op jit(solution)/shard_map/ppermute | solution.py:929
  33.9 3.7 %collective-permute-start.7 = (f32[18,8,128]{2,1,0:T(8,128)S(1)}, f32[18,8,128]{2,1,0:T(8,128)S(1)}, u32[]{:S(2)}, u32[]{:S(2)}) collective-permute-start(f32[18,8,128]{2,1,0:T(8,128)S(1)} %get-tuple-element.54), channel_id=1, source_target_pairs={{4,0},{8,4},{12,8},{16,12},{20,16},{24,20},{28,24},{0,28},{5,1},{9... | collective-permute-start | bytes 221192 | tf_op jit(solution)/shard_map/ppermute | solution.py:930
  37.5 3.2 %shard_map.42 = (f32[5,16,16,128]{3,2,1,0:T(8,128)S(1)}, f32[5,8,16,128]{3,2,1,0:T(8,128)S(1)}, f32[5,4,16,128]{3,2,1,0:T(8,128)S(1)}, f32[32,128]{1,0:T(8,128)S(1)}) custom-call(f32[32,4,128]{2,1,0:T(4,128)S(1)} %all-to-all-done.1.blocks, f32[3,4,16,128]{3,2,1,0:T(8,128)S(1)} %get-tuple-element.52._.window_one), custom_call_target="tpu_custom_call" | custom-call | tf_op jit(solution)/shard_map/pallas_call | solution.py:917
  40.8 0.0 collective-permute-done.6.one_low
  40.8 0.0 collective-permute-done.7.one_high
  40.8 0.0 all-to-all-done.blocks
  40.8 3.4 %shard_map.43 = f32[8,16,256]{2,1,0:T(8,128)} custom-call(f32[32,3,4,128]{3,2,1,0:T(4,128)S(1)} %all-to-all-done.blocks, f32[3,4,16,128]{3,2,1,0:T(8,128)S(1)} %get-tuple-element.52._.window_one, f32[18,8,128]{2,1,0:T(8,128)S(1)} %collective-permute-done.6.one_low, f32[18,8,128]{2,1,0:T(8,128)S(1)} %collective-permute-done.7.one_high, ...), custom_call_target="tpu_custom_call" | custom-call | tf_op jit(solution)/shard_map/pallas_call | solution.py:917
  (1 shorter events, 0.0 us)
Async XLA Ops:
  1.2 10.3 %collective-permute-start = (f32[9,8,256]{2,1,0:T(8,128)S(1)}, f32[9,8,256]{2,1,0:T(8,128)S(1)}, u32[]{:S(2)}, u32[]{:S(2)}) collective-permute-start(f32[9,8,256]{2,1,0:T(8,128)S(1)} %get-tuple-element.40), channel_id=1, source_target_pairs={{0,1},{1,2},{2,3},{3,0},{4,5},{5,6},{6,7},{7,4},{8,9},{9,10},{10,1... | collective-permute-start | bytes 221192 | tf_op jit(solution)/shard_map/ppermute | solution.py:929
  1.7 9.8 %collective-permute-start.1 = (f32[9,8,256]{2,1,0:T(8,128)S(1)}, f32[9,8,256]{2,1,0:T(8,128)S(1)}, u32[]{:S(2)}, u32[]{:S(2)}) collective-permute-start(f32[9,8,256]{2,1,0:T(8,128)S(1)} %get-tuple-element.41), channel_id=1, source_target_pairs={{1,0},{2,1},{3,2},{0,3},{5,4},{6,5},{7,6},{4,7},{9,8},{10,9},{11,1... | collective-permute-start | bytes 221192 | tf_op jit(solution)/shard_map/ppermute | solution.py:930
  4.8 19.3 %all-to-all-start.1 = ((f32[32,4,128]{2,1,0:T(4,128)}), f32[32,4,128]{2,1,0:T(4,128)S(1)}, u32[]{:S(2)}, u32[]{:S(2)}) async-start(f32[32,4,128]{2,1,0:T(4,128)} %get-tuple-element.62), calls=%async_computation.1 | async-start | bytes 131072 | tf_op jit(solution)/shard_map/all_to_all | solution.py:935
  11.8 9.0 %collective-permute-start.2 = (f32[15,8,256]{2,1,0:T(8,128)S(1)}, f32[15,8,256]{2,1,0:T(8,128)S(1)}, u32[]{:S(2)}, u32[]{:S(2)}) collective-permute-start(f32[15,8,256]{2,1,0:T(8,128)S(1)} %get-tuple-element.45), channel_id=1, source_target_pairs={{0,4},{4,8},{8,12},{12,16},{16,20},{20,24},{24,28},{28,0},{1,5},{5... | collective-permute-start | bytes 368648 | tf_op jit(solution)/shard_map/ppermute | solution.py:929
  13.6 8.1 %collective-permute-start.3 = (f32[15,8,256]{2,1,0:T(8,128)S(1)}, f32[15,8,256]{2,1,0:T(8,128)S(1)}, u32[]{:S(2)}, u32[]{:S(2)}) collective-permute-start(f32[15,8,256]{2,1,0:T(8,128)S(1)} %get-tuple-element.46), channel_id=1, source_target_pairs={{4,0},{8,4},{12,8},{16,12},{20,16},{24,20},{28,24},{0,28},{5,1},{9... | collective-permute-start | bytes 368648 | tf_op jit(solution)/shard_map/ppermute | solution.py:930
  24.1 16.6 %all-to-all-start = ((f32[32,3,4,128]{3,2,1,0:T(4,128)}), f32[32,3,4,128]{3,2,1,0:T(4,128)S(1)}, u32[]{:S(2)}, u32[]{:S(2)}) async-start(f32[32,3,4,128]{3,2,1,0:T(4,128)} %get-tuple-element.47), calls=%async_computation | async-start | bytes 393216 | tf_op jit(solution)/shard_map/all_to_all | solution.py:935
  28.3 3.5 %collective-permute-start.4 = (f32[8,8,128]{2,1,0:T(8,128)S(1)}, f32[8,8,128]{2,1,0:T(8,128)S(1)}, u32[]{:S(2)}, u32[]{:S(2)}) collective-permute-start(f32[8,8,128]{2,1,0:T(8,128)S(1)} %get-tuple-element.50), channel_id=1, source_target_pairs={{0,1},{1,2},{2,3},{3,0},{4,5},{5,6},{6,7},{7,4},{8,9},{9,10},{10,1... | collective-permute-start | bytes 98312 | tf_op jit(solution)/shard_map/ppermute | solution.py:929
  28.6 3.2 %collective-permute-start.5 = (f32[8,8,128]{2,1,0:T(8,128)S(1)}, f32[8,8,128]{2,1,0:T(8,128)S(1)}, u32[]{:S(2)}, u32[]{:S(2)}) collective-permute-start(f32[8,8,128]{2,1,0:T(8,128)S(1)} %get-tuple-element.51), channel_id=1, source_target_pairs={{1,0},{2,1},{3,2},{0,3},{5,4},{6,5},{7,6},{4,7},{9,8},{10,9},{11,1... | collective-permute-start | bytes 98312 | tf_op jit(solution)/shard_map/ppermute | solution.py:930
  31.8 8.9 %collective-permute-start.6 = (f32[18,8,128]{2,1,0:T(8,128)S(1)}, f32[18,8,128]{2,1,0:T(8,128)S(1)}, u32[]{:S(2)}, u32[]{:S(2)}) collective-permute-start(f32[18,8,128]{2,1,0:T(8,128)S(1)} %get-tuple-element.53), channel_id=1, source_target_pairs={{0,4},{4,8},{8,12},{12,16},{16,20},{20,24},{24,28},{28,0},{1,5},{5... | collective-permute-start | bytes 221192 | tf_op jit(solution)/shard_map/ppermute | solution.py:929
  33.9 6.9 %collective-permute-start.7 = (f32[18,8,128]{2,1,0:T(8,128)S(1)}, f32[18,8,128]{2,1,0:T(8,128)S(1)}, u32[]{:S(2)}, u32[]{:S(2)}) collective-permute-start(f32[18,8,128]{2,1,0:T(8,128)S(1)} %get-tuple-element.54), channel_id=1, source_target_pairs={{4,0},{8,4},{12,8},{16,12},{20,16},{24,20},{28,24},{0,28},{5,1},{9... | collective-permute-start | bytes 221192 | tf_op jit(solution)/shard_map/ppermute | solution.py:930

commit v9 on v8

--- a/solution.py
+++ b/solution.py
@@ -899,8 +899,10 @@
     plane_sweep(zero_a, zero_b, forcing0, cx, cy, cz, weight, RX - 1, planes - RX + 1)
     copies = pieces_of(((finished, out),), finished.shape[0], left)
     for x in range(planes - 2 * RX):
-        plane_sweep(zero_b, zero_a, forcing0, cx, cy, cz, weight, x + RX, x + RX + 1)
-        finished[x] = zero_a[x + RX, RY:top]
+        at = x + RX
+        total = forcing0[at] + neighbours(zero_b, cx, cy, cz, at)
+        swept = (1.0 - relax_weight) * zero_b[at] + weight[at] * total
+        finished[x] = swept[RY:top]
         copies[x].start()
     for copy in copies:
         copy.wait()

time: 44.6 us -> 44.6 us (level)
  no operation moved by 1% of the time
where the time goes in v9:
time: 44.6 us; the launch traced here: 44.2 us
  starting transfers between devices  25.5 us (57%)
  Pallas kernels  11.7 us (26%)
  waiting for transfers between devices  6.87 us (15%)
    pallas_call x7, Pallas kernels, call(): pl.pallas_call(kernel, in_specs=[spec] * len(operands), out_specs=[IN_PLA...  11.7 us
    all_to_all x2, starting transfers between devices, to_everyone(): return lax.all_to_all(blocks, ('tx', 'ty'), 0, 0)  10.8 us
    ppermute x4, starting transfers between devices, shift_both(): lax.ppermute(to_low, axis, [((i + 1) % count, i) for i in range(count)])  10.1 us
    ppermute x4, waiting for transfers between devices, shift_both(): lax.ppermute(to_high, axis, [(i, (i + 1) % count) for i in range(count)])  5.91 us
    ppermute x4, starting transfers between devices, shift_both(): lax.ppermute(to_high, axis, [(i, (i + 1) % count) for i in range(count)])  4.68 us
    ppermute x4, waiting for transfers between devices, shift_both(): lax.ppermute(to_low, axis, [((i + 1) % count, i) for i in range(count)])  0.96 us
  transfers between devices with their start and end apart: 10, of which 3 were waited for; matrix products, arithmetic and copies ran while one was open for 0% of the time, Pallas kernels for 16%

profile of v9, /device:TPU:0, one launch (start us, length us, event | category | flops | bytes accessed | tf_op | source)
XLA Modules:
  0.0 44.2 jit_solution(7143101970937288351)
XLA Ops:
  0.0 1.2 %shard_map.37 = (f32[8,16,256]{2,1,0:T(8,128)S(1)}, f32[8,16,256]{2,1,0:T(8,128)S(1)}, s32[8,16,256]{2,1,0:T(8,128)S(1)}, f32[9,8,256]{2,1,0:T(8,128)S(1)}, f32[9,8,256]{2,1,0:T(8,128)S(1)}) custom-call(f32[8,16,256]{2,1,0:T(8,128)} %conc_in.1, f32[8,16,256]{2,1,0:T(8,128)} %source_in.1, s32[8,16,256]{2,1,0:T(8,128)} %material_in.1), custom_call_target="tpu_custom_call" | custom-call | tf_op jit(solution)/shard_map/pallas_call | solution.py:919
  1.2 0.5 %collective-permute-start = (f32[9,8,256]{2,1,0:T(8,128)S(1)}, f32[9,8,256]{2,1,0:T(8,128)S(1)}, u32[]{:S(2)}, u32[]{:S(2)}) collective-permute-start(f32[9,8,256]{2,1,0:T(8,128)S(1)} %get-tuple-element.40), channel_id=1, source_target_pairs={{0,1},{1,2},{2,3},{3,0},{4,5},{5,6},{6,7},{7,4},{8,9},{9,10},{10,1... | collective-permute-start | bytes 221192 | tf_op jit(solution)/shard_map/ppermute | solution.py:931
  1.7 2.0 %collective-permute-start.1 = (f32[9,8,256]{2,1,0:T(8,128)S(1)}, f32[9,8,256]{2,1,0:T(8,128)S(1)}, u32[]{:S(2)}, u32[]{:S(2)}) collective-permute-start(f32[9,8,256]{2,1,0:T(8,128)S(1)} %get-tuple-element.41), channel_id=1, source_target_pairs={{1,0},{2,1},{3,2},{0,3},{5,4},{6,5},{7,6},{4,7},{9,8},{10,9},{11,1... | collective-permute-start | bytes 221192 | tf_op jit(solution)/shard_map/ppermute | solution.py:932
  3.7 1.1 %shard_map.38 = (f32[4,8,128]{2,1,0:T(8,128)S(1)}, f32[32,4,128]{2,1,0:T(4,128)}, bf16[2,128,128]{2,1,0:T(8,128)(2,1)S(1)}, bf16[2,128,128]{2,1,0:T(8,128)(2,1)S...) custom-call(s32[8,16,256]{2,1,0:T(8,128)S(1)} %get-tuple-element.38.material), custom_call_target="tpu_custom_call" | custom-call | tf_op jit(solution)/shard_map/pallas_call | solution.py:919
  4.8 6.6 %all-to-all-start.1 = ((f32[32,4,128]{2,1,0:T(4,128)}), f32[32,4,128]{2,1,0:T(4,128)S(1)}, u32[]{:S(2)}, u32[]{:S(2)}) async-start(f32[32,4,128]{2,1,0:T(4,128)} %get-tuple-element.62), calls=%async_computation.1 | async-start | bytes 131072 | tf_op jit(solution)/shard_map/all_to_all | solution.py:937
  11.4 0.0 collective-permute-done.from_low
  11.5 0.0 collective-permute-done.1.from_high
  11.5 0.3 shard_map.39
  11.8 1.8 %collective-permute-start.2 = (f32[15,8,256]{2,1,0:T(8,128)S(1)}, f32[15,8,256]{2,1,0:T(8,128)S(1)}, u32[]{:S(2)}, u32[]{:S(2)}) collective-permute-start(f32[15,8,256]{2,1,0:T(8,128)S(1)} %get-tuple-element.45), channel_id=1, source_target_pairs={{0,4},{4,8},{8,12},{12,16},{16,20},{20,24},{24,28},{28,0},{1,5},{5... | collective-permute-start | bytes 368648 | tf_op jit(solution)/shard_map/ppermute | solution.py:931
  13.6 3.0 %collective-permute-start.3 = (f32[15,8,256]{2,1,0:T(8,128)S(1)}, f32[15,8,256]{2,1,0:T(8,128)S(1)}, u32[]{:S(2)}, u32[]{:S(2)}) collective-permute-start(f32[15,8,256]{2,1,0:T(8,128)S(1)} %get-tuple-element.46), channel_id=1, source_target_pairs={{4,0},{8,4},{12,8},{16,12},{20,16},{24,20},{28,24},{0,28},{5,1},{9... | collective-permute-start | bytes 368648 | tf_op jit(solution)/shard_map/ppermute | solution.py:932
  16.6 4.2 %collective-permute-done.2.from_low = f32[15,8,256]{2,1,0:T(8,128)S(1)} collective-permute-done((f32[15,8,256]{2,1,0:T(8,128)S(1)}, f32[15,8,256]{2,1,0:T(8,128)S(1)}, u32[]{:S(2)}, u32[]{:S(2)}) %collective-permute-start.2) | collective-permute-done | bytes 122912 | tf_op jit(solution)/shard_map/ppermute | solution.py:931
  20.8 0.9 %collective-permute-done.3.from_high = f32[15,8,256]{2,1,0:T(8,128)S(1)} collective-permute-done((f32[15,8,256]{2,1,0:T(8,128)S(1)}, f32[15,8,256]{2,1,0:T(8,128)S(1)}, u32[]{:S(2)}, u32[]{:S(2)}) %collective-permute-start.3) | collective-permute-done | bytes 122912 | tf_op jit(solution)/shard_map/ppermute | solution.py:932
  21.7 2.4 %shard_map.40 = (f32[10,24,256]{2,1,0:T(8,128)S(1)}, f32[10,24,256]{2,1,0:T(8,128)S(1)}, f32[11,24,256]{2,1,0:T(8,128)S(1)}, f32[10,24,256]{2,1,0:T(8,128)S(1)},...) custom-call(f32[3,8,24,256]{3,2,1,0:T(8,128)S(1)} %get-tuple-element, ...), custom_call_target="tpu_custom_call" | custom-call | tf_op jit(solution)/shard_map/pallas_call | solution.py:919
  24.1 0.0 all-to-all-done.1.blocks
  24.1 4.2 %all-to-all-start = ((f32[32,3,4,128]{3,2,1,0:T(4,128)}), f32[32,3,4,128]{3,2,1,0:T(4,128)S(1)}, u32[]{:S(2)}, u32[]{:S(2)}) async-start(f32[32,3,4,128]{3,2,1,0:T(4,128)} %get-tuple-element.47), calls=%async_computation | async-start | bytes 393216 | tf_op jit(solution)/shard_map/all_to_all | solution.py:937
  28.3 0.3 collective-permute-start.4
  28.6 1.5 %collective-permute-start.5 = (f32[8,8,128]{2,1,0:T(8,128)S(1)}, f32[8,8,128]{2,1,0:T(8,128)S(1)}, u32[]{:S(2)}, u32[]{:S(2)}) collective-permute-start(f32[8,8,128]{2,1,0:T(8,128)S(1)} %get-tuple-element.51), channel_id=1, source_target_pairs={{1,0},{2,1},{3,2},{0,3},{5,4},{6,5},{7,6},{4,7},{9,8},{10,9},{11,1... | collective-permute-start | bytes 98312 | tf_op jit(solution)/shard_map/ppermute | solution.py:932
  30.1 1.7 %collective-permute-done.4.from_low.row_low = f32[8,8,128]{2,1,0:T(8,128)S(1)} collective-permute-done((f32[8,8,128]{2,1,0:T(8,128)S(1)}, f32[8,8,128]{2,1,0:T(8,128)S(1)}, u32[]{:S(2)}, u32[]{:S(2)}) %collective-permute-start.4) | collective-permute-done | bytes 32800 | tf_op jit(solution)/shard_map/ppermute | solution.py:931
  31.8 0.0 collective-permute-done.5.from_high.row_high
  31.8 2.0 %collective-permute-start.6 = (f32[18,8,128]{2,1,0:T(8,128)S(1)}, f32[18,8,128]{2,1,0:T(8,128)S(1)}, u32[]{:S(2)}, u32[]{:S(2)}) collective-permute-start(f32[18,8,128]{2,1,0:T(8,128)S(1)} %get-tuple-element.53), channel_id=1, source_target_pairs={{0,4},{4,8},{8,12},{12,16},{16,20},{20,24},{24,28},{28,0},{1,5},{5... | collective-permute-start | bytes 221192 | tf_op jit(solution)/shard_map/ppermute | solution.py:931
  33.9 3.7 %collective-permute-start.7 = (f32[18,8,128]{2,1,0:T(8,128)S(1)}, f32[18,8,128]{2,1,0:T(8,128)S(1)}, u32[]{:S(2)}, u32[]{:S(2)}) collective-permute-start(f32[18,8,128]{2,1,0:T(8,128)S(1)} %get-tuple-element.54), channel_id=1, source_target_pairs={{4,0},{8,4},{12,8},{16,12},{20,16},{24,20},{28,24},{0,28},{5,1},{9... | collective-permute-start | bytes 221192 | tf_op jit(solution)/shard_map/ppermute | solution.py:932
  37.5 3.2 %shard_map.42 = (f32[5,16,16,128]{3,2,1,0:T(8,128)S(1)}, f32[5,8,16,128]{3,2,1,0:T(8,128)S(1)}, f32[5,4,16,128]{3,2,1,0:T(8,128)S(1)}, f32[32,128]{1,0:T(8,128)S(1)}) custom-call(f32[32,4,128]{2,1,0:T(4,128)S(1)} %all-to-all-done.1.blocks, f32[3,4,16,128]{3,2,1,0:T(8,128)S(1)} %get-tuple-element.52._.window_one), custom_call_target="tpu_custom_call" | custom-call | tf_op jit(solution)/shard_map/pallas_call | solution.py:919
  40.8 0.0 collective-permute-done.6.one_low
  40.8 0.0 collective-permute-done.7.one_high
  40.8 0.0 all-to-all-done.blocks
  40.8 3.4 %shard_map.43 = f32[8,16,256]{2,1,0:T(8,128)} custom-call(f32[32,3,4,128]{3,2,1,0:T(4,128)S(1)} %all-to-all-done.blocks, f32[3,4,16,128]{3,2,1,0:T(8,128)S(1)} %get-tuple-element.52._.window_one, f32[18,8,128]{2,1,0:T(8,128)S(1)} %collective-permute-done.6.one_low, f32[18,8,128]{2,1,0:T(8,128)S(1)} %collective-permute-done.7.one_high, ...), custom_call_target="tpu_custom_call" | custom-call | tf_op jit(solution)/shard_map/pallas_call | solution.py:919
  (1 shorter events, 0.0 us)
Async XLA Ops:
  1.2 10.3 %collective-permute-start = (f32[9,8,256]{2,1,0:T(8,128)S(1)}, f32[9,8,256]{2,1,0:T(8,128)S(1)}, u32[]{:S(2)}, u32[]{:S(2)}) collective-permute-start(f32[9,8,256]{2,1,0:T(8,128)S(1)} %get-tuple-element.40), channel_id=1, source_target_pairs={{0,1},{1,2},{2,3},{3,0},{4,5},{5,6},{6,7},{7,4},{8,9},{9,10},{10,1... | collective-permute-start | bytes 221192 | tf_op jit(solution)/shard_map/ppermute | solution.py:931
  1.7 9.8 %collective-permute-start.1 = (f32[9,8,256]{2,1,0:T(8,128)S(1)}, f32[9,8,256]{2,1,0:T(8,128)S(1)}, u32[]{:S(2)}, u32[]{:S(2)}) collective-permute-start(f32[9,8,256]{2,1,0:T(8,128)S(1)} %get-tuple-element.41), channel_id=1, source_target_pairs={{1,0},{2,1},{3,2},{0,3},{5,4},{6,5},{7,6},{4,7},{9,8},{10,9},{11,1... | collective-permute-start | bytes 221192 | tf_op jit(solution)/shard_map/ppermute | solution.py:932
  4.8 19.3 %all-to-all-start.1 = ((f32[32,4,128]{2,1,0:T(4,128)}), f32[32,4,128]{2,1,0:T(4,128)S(1)}, u32[]{:S(2)}, u32[]{:S(2)}) async-start(f32[32,4,128]{2,1,0:T(4,128)} %get-tuple-element.62), calls=%async_computation.1 | async-start | bytes 131072 | tf_op jit(solution)/shard_map/all_to_all | solution.py:937
  11.8 9.0 %collective-permute-start.2 = (f32[15,8,256]{2,1,0:T(8,128)S(1)}, f32[15,8,256]{2,1,0:T(8,128)S(1)}, u32[]{:S(2)}, u32[]{:S(2)}) collective-permute-start(f32[15,8,256]{2,1,0:T(8,128)S(1)} %get-tuple-element.45), channel_id=1, source_target_pairs={{0,4},{4,8},{8,12},{12,16},{16,20},{20,24},{24,28},{28,0},{1,5},{5... | collective-permute-start | bytes 368648 | tf_op jit(solution)/shard_map/ppermute | solution.py:931
  13.6 8.1 %collective-permute-start.3 = (f32[15,8,256]{2,1,0:T(8,128)S(1)}, f32[15,8,256]{2,1,0:T(8,128)S(1)}, u32[]{:S(2)}, u32[]{:S(2)}) collective-permute-start(f32[15,8,256]{2,1,0:T(8,128)S(1)} %get-tuple-element.46), channel_id=1, source_target_pairs={{4,0},{8,4},{12,8},{16,12},{20,16},{24,20},{28,24},{0,28},{5,1},{9... | collective-permute-start | bytes 368648 | tf_op jit(solution)/shard_map/ppermute | solution.py:932
  24.1 16.6 %all-to-all-start = ((f32[32,3,4,128]{3,2,1,0:T(4,128)}), f32[32,3,4,128]{3,2,1,0:T(4,128)S(1)}, u32[]{:S(2)}, u32[]{:S(2)}) async-start(f32[32,3,4,128]{3,2,1,0:T(4,128)} %get-tuple-element.47), calls=%async_computation | async-start | bytes 393216 | tf_op jit(solution)/shard_map/all_to_all | solution.py:937
  28.3 3.5 %collective-permute-start.4 = (f32[8,8,128]{2,1,0:T(8,128)S(1)}, f32[8,8,128]{2,1,0:T(8,128)S(1)}, u32[]{:S(2)}, u32[]{:S(2)}) collective-permute-start(f32[8,8,128]{2,1,0:T(8,128)S(1)} %get-tuple-element.50), channel_id=1, source_target_pairs={{0,1},{1,2},{2,3},{3,0},{4,5},{5,6},{6,7},{7,4},{8,9},{9,10},{10,1... | collective-permute-start | bytes 98312 | tf_op jit(solution)/shard_map/ppermute | solution.py:931
  28.6 3.2 %collective-permute-start.5 = (f32[8,8,128]{2,1,0:T(8,128)S(1)}, f32[8,8,128]{2,1,0:T(8,128)S(1)}, u32[]{:S(2)}, u32[]{:S(2)}) collective-permute-start(f32[8,8,128]{2,1,0:T(8,128)S(1)} %get-tuple-element.51), channel_id=1, source_target_pairs={{1,0},{2,1},{3,2},{0,3},{5,4},{6,5},{7,6},{4,7},{9,8},{10,9},{11,1... | collective-permute-start | bytes 98312 | tf_op jit(solution)/shard_map/ppermute | solution.py:932
  31.8 8.9 %collective-permute-start.6 = (f32[18,8,128]{2,1,0:T(8,128)S(1)}, f32[18,8,128]{2,1,0:T(8,128)S(1)}, u32[]{:S(2)}, u32[]{:S(2)}) collective-permute-start(f32[18,8,128]{2,1,0:T(8,128)S(1)} %get-tuple-element.53), channel_id=1, source_target_pairs={{0,4},{4,8},{8,12},{12,16},{16,20},{20,24},{24,28},{28,0},{1,5},{5... | collective-permute-start | bytes 221192 | tf_op jit(solution)/shard_map/ppermute | solution.py:931
  33.9 6.9 %collective-permute-start.7 = (f32[18,8,128]{2,1,0:T(8,128)S(1)}, f32[18,8,128]{2,1,0:T(8,128)S(1)}, u32[]{:S(2)}, u32[]{:S(2)}) collective-permute-start(f32[18,8,128]{2,1,0:T(8,128)S(1)} %get-tuple-element.54), channel_id=1, source_target_pairs={{4,0},{8,4},{12,8},{16,12},{20,16},{24,20},{28,24},{0,28},{5,1},{9... | collective-permute-start | bytes 221192 | tf_op jit(solution)/shard_map/ppermute | solution.py:932
